TPU v7x, 128 devices: a whole 4x4x4 slice. The times are simulated.
128 devices in a mesh: ctx: 16 (over x, y_hi, core), head: 8 (over z, y_lo).
Axes of the slice: x: 4, y: 4 (y_hi: 2, y_lo: 2; y = y_hi * 2 + y_lo), z: 4, core: 2. Of those that a mesh axis runs over, the one named last changes fastest.
Arguments:
- queries: bfloat16 [2, 8192, 5120], P(None, ('ctx', 'head')), may hold values from -6 to 6
- keys: bfloat16 [2, 8192, 5120], P(None, ('ctx', 'head')), may hold values from -6 to 6
- values: bfloat16 [2, 8192, 5120], P(None, ('ctx', 'head')), may hold values from -6 to 6
- rates: bfloat16 [2, 8192, 8], P(None, ('ctx', 'head')), may hold values from 0.00013065338 to 0.0013046265
- gate_fast: float32 [8, 640, 640], P('head'), may hold values from -0.25 to 0.25
- up_fast: float32 [8, 640, 640], P('head'), may hold values from -0.25 to 0.25
- down_fast: float32 [8, 640, 640], P('head'), may hold values from -0.25 to 0.25
- out_gain: float32 [5120], P('head'), may hold values from 0.5 to 1.5
- out_proj: bfloat16 [5120, 5120], P('head'), may hold values from -0.078125 to 0.078125
Outputs:
- mixed: bfloat16 [2, 8192, 5120], P(None, ('ctx', 'head'))
All inputs are finite; a program needn't handle non-finite values.
Results may differ from a plain program's by a relative error of at most 0.014.
Values may be sent and summed in bfloat16 or wider, within the bound.
No kernel may reach another device: no remote copies, remote signals or barrier semaphores. Data moves between devices by JAX's collectives and lax.ppermute only.
A program may use at most 128 MiB of HBM per device.

v0:
```python
import jax
import jax.numpy as jnp
from jax import lax
from jax.experimental import pallas as pl
from jax.experimental.pallas import tpu as pltpu
from jax.sharding import Mesh, PartitionSpec as P

F32 = jnp.float32
BF16 = jnp.bfloat16
AXES = ("x", "yh", "core", "z", "yl")
SIZES = (4, 2, 2, 4, 2)
HD = 640
WIDE = 5120
TOK = 64
HALF = 320
PART = 80
PIECE = 240
COLS = 2560
SLAB = 1280
TILE = 640


VMEM = pl.BlockSpec(memory_space=pltpu.VMEM)
SMEM = pl.BlockSpec(memory_space=pltpu.SMEM)


def cost(flops, moved):
    return pl.CostEstimate(flops=flops, bytes_accessed=moved, transcendentals=0)


def room(mib):
    return pltpu.CompilerParams(vmem_limit_bytes=mib << 20)


def nt(left, right):
    return lax.dot_general(left, right, (((1,), (1,)), ((), ())), preferred_element_type=F32)


def nn(left, right):
    return lax.dot_general(left, right, (((1,), (0,)), ((), ())), preferred_element_type=F32)


def shift(array, axis, by, size):
    return lax.ppermute(array, axis, [(i, (i + by) % size) for i in range(size)])


def to_heads(array):
    return lax.all_to_all(array, ("z", "yl"), 0, 0, tiled=True)


def add(*terms):
    total = terms[0].astype(F32)
    for term in terms[1:]:
        total = total + term.astype(F32)
    return total


def split(matrix):
    high = matrix.astype(BF16)
    return high, (matrix - high.astype(F32)).astype(BF16)


def pack_keys(key_block, value_block, rate_block, out_ref):
    rates = rate_block[0].astype(F32)
    row = lax.broadcasted_iota(jnp.int32, (TOK, TOK), 0)
    lane = lax.broadcasted_iota(jnp.int32, (TOK, TOK), 1)
    for head in range(8):
        cols = slice(head * HD, (head + 1) * HD)
        out_ref[head, :TOK, :] = key_block[0, :, cols]
        spread = jnp.broadcast_to(rates[head : head + 1, :], (TOK, TOK))
        rate = jnp.sum(jnp.where(row == lane, spread, 0.0), axis=1, keepdims=True)
        target = value_block[0, :, cols].astype(F32) * rate
        out_ref[head, TOK : 2 * TOK, :] = target.astype(BF16)


def pack_first_kernel(key_ref, value_ref, rate_ref, out_ref):
    pack_keys(key_ref, value_ref, rate_ref, out_ref)


def pack_second_kernel(key_ref, value_ref, rate_ref, query_ref, out_ref):
    pack_keys(key_ref, value_ref, rate_ref, out_ref)
    for head in range(8):
        for block in range(2):
            start = (2 + block) * TOK
            cols = slice(head * HD, (head + 1) * HD)
            out_ref[head, start : start + TOK, :] = query_ref[block, :, cols]


def block_of(block, width):
    return pl.BlockSpec((1, TOK, width), lambda i: (block, 0, 0))


def rates_of(block):
    return pl.BlockSpec((1, 8, TOK), lambda i: (block, 0, 0))


def pack_first(keys, values, rates):
    return pl.pallas_call(
        pack_first_kernel,
        grid=(1,),
        in_specs=[block_of(0, WIDE), block_of(0, WIDE), rates_of(0)],
        out_specs=pl.BlockSpec((8, 2 * TOK, HD), lambda i: (0, 0, 0)),
        out_shape=jax.ShapeDtypeStruct((8, 2 * TOK, HD), BF16),
        cost_estimate=cost(1 << 20, 4 * TOK * WIDE * 2),
        name="pack_first",
    )(keys, values, rates)


def pack_second(keys, values, rates, queries):
    return pl.pallas_call(
        pack_second_kernel,
        grid=(1,),
        in_specs=[
            block_of(1, WIDE),
            block_of(1, WIDE),
            rates_of(1),
            pl.BlockSpec((2, TOK, WIDE), lambda i: (0, 0, 0)),
        ],
        out_specs=pl.BlockSpec((8, 4 * TOK, HD), lambda i: (0, 0, 0)),
        out_shape=jax.ShapeDtypeStruct((8, 4 * TOK, HD), BF16),
        cost_estimate=cost(1 << 20, 8 * TOK * WIDE * 2),
        name="pack_second",
    )(keys, values, rates, queries)


def start_half_kernel(place_ref, gate_ref, up_ref, down_ref, high_ref, low_ref, turned):
    half = pl.ds(pl.multiple_of(place_ref[0] * HALF, HALF), HALF)
    for slot, ref in ((0, gate_ref), (1, up_ref)):
        turned[...] = ref[0].T
        high_ref[slot], low_ref[slot] = split(turned[half, :])
    high_ref[2], low_ref[2] = split(down_ref[0, half, :])


def start_half(place, gate, up, down):
    return pl.pallas_call(
        start_half_kernel,
        in_specs=[SMEM] + [VMEM] * 3,
        out_specs=[VMEM] * 2,
        out_shape=[pltpu.VMEM((3, HALF, HD), BF16)] * 2,
        scratch_shapes=[pltpu.VMEM((HD, HD), F32)],
        compiler_params=room(16),
        cost_estimate=cost(1 << 24, 3 * HD * HD * 6),
        name="start_half",
    )(place, gate, up, down)


def start_full_kernel(gate_ref, up_ref, down_ref, master_ref, row_norm_ref, col_norm_ref):
    for slot, ref in ((0, gate_ref), (1, up_ref)):
        matrix = ref[0].T
        master_ref[slot] = matrix
        row_norm_ref[slot] = jnp.sqrt(jnp.sum(matrix * matrix, axis=1, keepdims=True))
    matrix = down_ref[0]
    master_ref[2] = matrix
    col_norm_ref[...] = jnp.sqrt(jnp.sum(matrix * matrix, axis=0, keepdims=True))


def start_full(gate, up, down):
    return pl.pallas_call(
        start_full_kernel,
        in_specs=[VMEM] * 3,
        out_specs=[VMEM] * 3,
        out_shape=[
            pltpu.VMEM((3, HD, HD), F32),
            pltpu.VMEM((2, HD, 1), F32),
            pltpu.VMEM((1, HD), F32),
        ],
        compiler_params=room(16),
        cost_estimate=cost(1 << 24, 3 * HD * HD * 8),
        name="start_full",
    )(gate, up, down)


def renorm_kernel(count, place_ref, *refs):
    old_refs, (row_norm_ref, col_norm_ref) = refs[:count], refs[count : count + 2]
    pieces, (high_ref, low_ref, down_ref) = refs[count + 2 : count + 10], refs[count + 10 :]
    core, x = place_ref[0], place_ref[1]
    squares = jnp.zeros((8, HD), F32)

    def moved_rows(slot, rows, step):
        total = step.astype(F32)
        for old_ref in old_refs:
            total = total + old_ref[slot, rows, :].astype(F32)
        return total

    for index, piece in enumerate(pieces):
        side, d = index // 4, index % 4
        owner = core if side == 0 else 1 - core
        start = pl.multiple_of(owner * HALF + lax.rem(x + 4 - d, 4) * PART, 16)
        rows = pl.ds(start, PART)
        for slot in range(2):
            moved = moved_rows(slot, rows, piece[slot * PART : (slot + 1) * PART, :])
            scale = row_norm_ref[slot, rows, :] * lax.rsqrt(
                jnp.sum(moved * moved, axis=1, keepdims=True) + 1e-6
            )
            high_ref[slot, rows, :], low_ref[slot, rows, :] = split(moved * scale)
        moved = moved_rows(2, rows, piece[2 * PART :, :])
        down_ref[rows, :] = moved
        squares = squares + jnp.sum((moved * moved).reshape(PART // 8, 8, HD), axis=0)
    scale = col_norm_ref[...] * lax.rsqrt(jnp.sum(squares, axis=0, keepdims=True) + 1e-6)
    high_ref[2], low_ref[2] = split(down_ref[...] * scale)


def renorm(place, weights, row_norm, col_norm, pieces):
    return pl.pallas_call(
        lambda *refs: renorm_kernel(len(weights), *refs),
        in_specs=[SMEM] + [VMEM] * (10 + len(weights)),
        out_specs=[VMEM] * 2,
        out_shape=[pltpu.VMEM((3, HD, HD), BF16)] * 2,
        scratch_shapes=[pltpu.VMEM((HD, HD), F32)],
        compiler_params=room(16),
        cost_estimate=cost(1 << 24, 3 * HD * HD * 10),
        name="renorm",
    )(place, *weights, row_norm, col_norm, *pieces)


def grads_kernel(place_ref, high_ref, low_ref, near_ref, far_ref, *refs):
    outs, (tokens, inner, total) = refs[:4], refs[4:]
    core, x = place_ref[0], place_ref[1]
    for side, ref in enumerate((near_ref, far_ref)):
        for index in range(8):
            rows = pl.ds((side * 8 + index) * TOK, TOK)
            tokens[0, rows, :] = ref[index, :TOK, :]
            tokens[1, rows, :] = ref[index, TOK : 2 * TOK, :]
    height = high_ref.shape[1]
    half = pl.ds(pl.multiple_of(core * (height - HALF), HALF), HALF)

    def product(slot, rows):
        return nt(high_ref[slot, half, :], rows) + nt(low_ref[slot, half, :], rows)

    def chunk(step, carry):
        rows = pl.ds(pl.multiple_of(step * 256, 256), 256)
        key = tokens[0, rows, :]
        gate = product(0, key)
        up = product(1, key)
        back = product(2, tokens[1, rows, :])
        sigma = jax.nn.sigmoid(gate)
        silu = gate * sigma
        inner[0, :, rows] = (back * up * sigma * (1.0 + gate * (1.0 - sigma))).astype(BF16)
        inner[1, :, rows] = (back * silu).astype(BF16)
        inner[2, :, rows] = (silu * up).astype(BF16)
        return carry

    lax.fori_loop(0, 4, chunk, 0)

    def finish(slot, carry):
        total[slot] = nn(inner[slot], tokens[slot // 2])
        return carry

    lax.fori_loop(0, 3, finish, 0)
    for d in range(4):
        rows = pl.ds(pl.multiple_of(lax.rem(x + d, 4) * PART, 16), PART)
        for slot in range(3):
            outs[d][slot * PART : (slot + 1) * PART, :] = total[slot, rows, :].astype(outs[d].dtype)


def grads(place, weights, near, far):
    part = pl.BlockSpec((8, 2 * TOK, HD), lambda i: (0, 0, 0))
    held = pl.BlockSpec(weights[0].shape, lambda i: (0, 0, 0))
    return pl.pallas_call(
        grads_kernel,
        grid=(1,),
        in_specs=[SMEM] + [held] * 2 + [part] * 2,
        out_specs=[pl.BlockSpec((PIECE, HD), lambda i: (0, 0))] * 4,
        out_shape=[pltpu.VMEM((PIECE, HD), F32 if d == 0 else BF16) for d in range(4)],
        scratch_shapes=[
            pltpu.VMEM((2, 16 * TOK, HD), BF16),
            pltpu.VMEM((3, HALF, 16 * TOK), BF16),
            pltpu.VMEM((3, HALF, HD), F32),
        ],
        cost_estimate=cost(12 * 16 * TOK * HALF * HD, 8 << 20),
        compiler_params=room(16),
        name="grads",
    )(place, *weights, near, far)


def sum_over_ctx(parts):
    received = {d: shift(parts[d], "x", d, 4) for d in (1, 3, 2)}
    mine = lax.optimization_barrier(add(parts[0], received[1], received[3], received[2]))
    other = shift(mine.astype(BF16), "yh", 1, 2)
    mine = add(mine, other).astype(BF16)
    near = {d: shift(mine, "x", d, 4) for d in (1, 3, 2)}
    pieces = [mine, near[1], near[2], near[3]]
    far = {d: shift(pieces[d], "core", 1, 2) for d in (0, 1, 3, 2)}
    return pieces + [far[d] for d in range(4)]


def apply_kernel(place_ref, high_ref, low_ref, gain_ref, query_ref, *refs):
    outs, (rows_in, rows_out) = refs[:4], refs[4:]
    z, yl = place_ref[2], place_ref[3]
    for d in range(4):
        for dy in range(2):
            source = lax.rem(z + 4 - d, 4) * 2 + lax.rem(yl + dy, 2)
            rows_in[pl.ds((d * 2 + dy) * TOK, TOK), :] = query_ref[source]
    gain = gain_ref[...]

    def chunk(step, carry):
        rows = pl.ds(pl.multiple_of(step * 4 * TOK, 4 * TOK), 4 * TOK)
        query = rows_in[rows, :]
        gate = nt(query, high_ref[0]) + nt(query, low_ref[0])
        up = nt(query, high_ref[1]) + nt(query, low_ref[1])
        hidden = (gate * jax.nn.sigmoid(gate) * up).astype(BF16)
        out = nn(hidden, high_ref[2])
        mean = jnp.sum(out * out, axis=1, keepdims=True) * (1.0 / HD)
        rows_out[rows, :] = (out * lax.rsqrt(mean + 1e-5) * gain).astype(BF16)
        return carry

    lax.fori_loop(0, 2, chunk, 0)
    for d in range(4):
        outs[d][...] = rows_out[d * 2 * TOK : (d + 1) * 2 * TOK, :]


def apply_weights(block, place, weights, gain, queries):
    return pl.pallas_call(
        apply_kernel,
        grid=(1,),
        in_specs=[
            SMEM,
            pl.BlockSpec((3, HD, HD), lambda i: (0, 0, 0)),
            pl.BlockSpec((2, HD, HD), lambda i: (0, 0, 0)),
            pl.BlockSpec((1, HD), lambda i: (0, 0)),
            pl.BlockSpec((8, TOK, HD), lambda i: (0, 2 + block, 0)),
        ],
        out_specs=[pl.BlockSpec((2 * TOK, HD), lambda i: (0, 0))] * 4,
        out_shape=[jax.ShapeDtypeStruct((2 * TOK, HD), BF16)] * 4,
        scratch_shapes=[pltpu.VMEM((8 * TOK, HD), BF16)] * 2,
        compiler_params=room(16),
        cost_estimate=cost(10 * 8 * TOK * HD * HD, 5 << 20),
        name="apply_weights",
    )(place, *weights, gain, queries)


def project_body(side, part_of_side, place_ref, *refs):
    rows, own, parts = refs[:8], refs[8], refs[9:15]
    keep_ref, send_ref, both, slots, total, sems = refs[15:]
    step = pl.program_id(0)
    tiles = SLAB // TILE
    base = part_of_side * SLAB
    half = place_ref[0] if side == 0 else 1 - place_ref[0]

    def copies(t):
        slot = lax.rem(t, 2)
        cols = pl.ds(pl.multiple_of(base + t * TILE, TILE), TILE)
        own_cols = pl.ds(pl.multiple_of(half * COLS + base + t * TILE, TILE), TILE)
        pairs = [(own.at[:, own_cols], slots.at[slot, pl.ds(0, HD)])]
        for index, part in enumerate(parts):
            start = HD + index * HALF
            pairs.append((part.at[:, cols], slots.at[slot, pl.ds(start, HALF)]))
        return [
            pltpu.make_async_copy(source, target, sems.at[slot, index])
            for index, (source, target) in enumerate(pairs)
        ]

    @pl.when(step == 0)
    def _():
        for copy in copies(step):
            copy.start()
        for block in range(2):
            for d in range(4):
                piece = rows[block * 4 + d]
                cols = slice(d * HD, (d + 1) * HD)
                both[block * TOK : (block + 1) * TOK, cols] = piece[:TOK, :]
                both[(2 + block) * TOK : (3 + block) * TOK, cols] = piece[TOK:, :]

    @pl.when(step + 1 < tiles)
    def _():
        for copy in copies(step + 1):
            copy.start()

    for copy in copies(step):
        copy.wait()
    slot = lax.rem(step, 2)

    def depth(k, carry):
        cols = pl.ds(pl.multiple_of(k * 512, 512), 512)
        total[...] += nn(both[:, cols], slots[slot, cols, :])
        return carry

    total[...] = jnp.zeros_like(total)
    lax.fori_loop(0, 5, depth, 0)
    keep_ref[...] = total[: 2 * TOK, :].astype(BF16)
    send_ref[...] = total[2 * TOK :, :].astype(BF16)


def project(side, part_of_side, place, rows, own, parts):
    tiles = SLAB // TILE
    out = pl.BlockSpec((2 * TOK, TILE), lambda t, place_ref: (0, t))
    return pl.pallas_call(
        lambda *refs: project_body(side, part_of_side, *refs),
        grid_spec=pltpu.PrefetchScalarGridSpec(
            num_scalar_prefetch=1,
            grid=(tiles,),
            in_specs=[pl.BlockSpec((2 * TOK, HD), lambda t, place_ref: (0, 0))] * 8
            + [pl.BlockSpec(memory_space=pl.ANY)] * 7,
            out_specs=[out, out],
            scratch_shapes=[
                pltpu.VMEM((4 * TOK, 4 * HD), BF16),
                pltpu.VMEM((2, 4 * HD, TILE), BF16),
                pltpu.VMEM((4 * TOK, TILE), F32),
                pltpu.SemaphoreType.DMA((2, 7)),
            ],
        ),
        out_shape=[jax.ShapeDtypeStruct((2 * TOK, SLAB), BF16)] * 2,
        compiler_params=room(16),
        cost_estimate=cost(2 * 256 * 2560 * SLAB, 2560 * SLAB * 2),
    )(place, *rows, own, *parts)


def finish_kernel(place_ref, *refs):
    out_ref = refs[-1]
    for index in range(WIDE // SLAB):
        keep, got = refs[index * 2 : index * 2 + 2]
        side, part_of_side = divmod(index, COLS // SLAB)
        half = place_ref[0] if side == 0 else 1 - place_ref[0]
        cols = pl.ds(pl.multiple_of(half * COLS + part_of_side * SLAB, 128), SLAB)
        for block in range(2):
            rows = pl.ds(block * TOK, TOK)
            total = keep[rows, :].astype(F32) + got[rows, :].astype(F32)
            out_ref[block, :, cols] = total.astype(BF16)


def finish(place, parts):
    return pl.pallas_call(
        finish_kernel,
        in_specs=[SMEM] + [VMEM] * 8,
        out_specs=VMEM,
        out_shape=jax.ShapeDtypeStruct((2, TOK, WIDE), BF16),
        compiler_params=room(16),
        cost_estimate=cost(1 << 20, 6 << 20),
        name="finish",
    )(place, *parts)


def per_device(queries, keys, values, rates, gate_fast, up_fast, down_fast, out_gain, out_proj):
    core = lax.axis_index("core")
    place = jnp.stack([core] + [lax.axis_index(name) for name in ("x", "z", "yl")])
    place = place.astype(jnp.int32)
    gain = out_gain.reshape(1, HD)
    rates = rates.transpose(0, 2, 1)

    first = to_heads(pack_first(keys, values, rates))
    first_far = shift(first, "core", 1, 2)
    second = to_heads(pack_second(keys, values, rates, queries))
    second_far = shift(second, "core", 1, 2)

    low = lax.dynamic_slice(out_proj, (0, core * COLS), (HALF, COLS))
    high = lax.dynamic_slice(out_proj, (HALF, core * COLS), (HALF, COLS))
    before_low = shift(low, "z", 1, 4)
    after_high = shift(high, "z", 3, 4)
    before_high = shift(high, "z", 1, 4)
    after_low = shift(low, "z", 3, 4)
    far_low = shift(before_low, "z", 1, 4)
    far_high = shift(after_high, "z", 3, 4)
    own_side = (before_low, before_high, far_low, far_high, after_low, after_high)
    other_near = [shift(own_side[i], "core", 1, 2) for i in (0, 1, 4, 5)]
    other_far = [shift(part, "core", 1, 2) for part in (far_low, far_high)]
    other_side = (*other_near[:2], *other_far, *other_near[2:])

    halves = start_half(place, gate_fast, up_fast, down_fast)
    master, row_norm, col_norm = start_full(gate_fast, up_fast, down_fast)

    def spread(block, weights):
        rows = apply_weights(block, place, weights, gain, second)
        back = {d: shift(rows[d], "z", 4 - d, 4) for d in (2, 1, 3)}
        return [rows[0], back[3], back[2], back[1]]

    total = sum_over_ctx(grads(place, halves, first, first_far))
    weights = renorm(place, [master], row_norm, col_norm, total)
    parts = grads(place, weights, second, second_far)
    total = sum_over_ctx(parts)
    rows = spread(0, weights)
    weights = renorm(place, weights, row_norm, col_norm, total)
    rows += spread(1, weights)
    mixed = []
    for side, gathered in enumerate((own_side, other_side)):
        for part_of_side in range(COLS // SLAB):
            keep, send = project(side, part_of_side, place, rows, out_proj, gathered)
            mixed += [keep, shift(send, "yl", 1, 2)]
    return finish(place, mixed)


def solution(mesh):
    fine = Mesh(mesh.devices.reshape(SIZES), AXES)
    tokens = P(None, AXES, None)
    head = ("z", "yl")
    placed = (
        tokens,
        tokens,
        tokens,
        tokens,
        P(head, None, None),
        P(head, None, None),
        P(head, None, None),
        P(head),
        P(head, None),
    )
    return jax.shard_map(per_device, mesh=fine, in_specs=placed, out_specs=tokens, check_vma=False)
```

profile of v0, /device:TPU:1, one launch (start us, length us, event | category | flops | bytes accessed | tf_op | source)
XLA Modules:
  0.0 318.8 jit_solution(7677967763865487154)
XLA Ops:
  0.0 2.5 pack_first.1
  2.5 6.9 %all-to-all-start = ((bf16[8,128,640]{2,1,0:T(8,128)(2,1)}), bf16[8,128,640]{2,1,0:T(8,128)(2,1)S(1)}, u32[]{:S(2)}, u32[]{:S(2)}) async-start(bf16[8,128,640]{2,1,0:T(8,128)(2,1)} %pack_first.1), calls=%async_computation | async-start | bytes 2621440 | tf_op jit(solution)/shard_map/all_to_all | solution.py:48
  9.4 3.5 %pack_second.1 = bf16[8,256,640]{2,1,0:T(8,128)(2,1)} custom-call(bf16[2,64,5120]{2,1,0:T(8,128)(2,1)} %key_ref.3, bf16[2,64,5120]{2,1,0:T(8,128)(2,1)} %value_ref.3, bf16[2,8,64]{2,1,0:T(8,128)(2,1)} %bitcast.8, bf16[2,64,5120]{2,1,0:T(8,128)(2,1)} %query_ref.1), custom_call_target="tpu_custom_call" | custom-call | flops 1048576 | bytes 5242880 | tf_op jit(solution)/shard_map/pack_second/pallas_call | solution.py:110
  12.9 14.2 %all-to-all-done.near_ref = bf16[8,128,640]{2,1,0:T(8,128)(2,1)S(1)} async-done(((bf16[8,128,640]{2,1,0:T(8,128)(2,1)}), bf16[8,128,640]{2,1,0:T(8,128)(2,1)S(1)}, u32[]{:S(2)}, u32[]{:S(2)}) %all-to-all-start) | async-done | bytes 1310752 | tf_op jit(solution)/shard_map/all_to_all | solution.py:48
  28.2 3.7 %all-to-all-start.1 = ((bf16[8,256,640]{2,1,0:T(8,128)(2,1)}), bf16[8,256,640]{2,1,0:T(8,128)(2,1)S(1)}, u32[]{:S(2)}, u32[]{:S(2)}) async-start(bf16[8,256,640]{2,1,0:T(8,128)(2,1)} %pack_second.1), calls=%async_computation.1 | async-start | bytes 5242880 | tf_op jit(solution)/shard_map/all_to_all | solution.py:48
  31.9 1.8 collective-permute-start
  33.7 29.2 %all-to-all-done.1.query_ref.near_ref = bf16[8,256,640]{2,1,0:T(8,128)(2,1)S(1)} async-done(((bf16[8,256,640]{2,1,0:T(8,128)(2,1)}), bf16[8,256,640]{2,1,0:T(8,128)(2,1)S(1)}, u32[]{:S(2)}, u32[]{:S(2)}) %all-to-all-start.1) | async-done | bytes 2621472 | tf_op jit(solution)/shard_map/all_to_all | solution.py:48
  62.9 2.5 collective-permute-start.15
  65.5 1.4 copy-done
  67.0 1.4 copy-done.2
  68.4 1.4 copy-done.4
  69.8 2.0 start_half.1
  71.9 7.6 %grads.2 = (f32[240,640]{1,0:T(8,128)S(1)}, bf16[240,640]{1,0:T(8,128)(2,1)S(1)}, bf16[240,640]{1,0:T(8,128)(2,1)S(1)}, bf16[240,640]{1,0:T(8,128)(2,1)S(1)}) custom-call(s32[4]{0:T(128)S(1)} %pad_add_fusion.place_ref.refs_0_, bf16[3,320,640]{2,1,0:T(8,128)(2,1)S(1)} %get-tuple-element.41.high_ref, bf16[3,320,640]{2,1,0:T(8,128)(2,1)S(1)} %get-tuple-element.42.low_ref, ...), custom_call_target="tpu_custom_call" | custom-call | flops 2516582400 | bytes 8388608 | tf_op jit(solution)/shard_map/grads/pallas_call | solution.py:259
  79.5 2.8 collective-permute-start.3
  83.8 6.2 %collective-permute-done.3 = bf16[240,640]{1,0:T(8,128)(2,1)S(1)} collective-permute-done((bf16[240,640]{1,0:T(8,128)(2,1)S(1)}, bf16[240,640]{1,0:T(8,128)(2,1)S(1)}, u32[]{:S(2)}, u32[]{:S(2)}) %collective-permute-start.3) | collective-permute-done | bytes 307232 | tf_op jit(solution)/shard_map/ppermute | solution.py:44
  90.0 6.7 %collective-permute-done.2 = bf16[240,640]{1,0:T(8,128)(2,1)S(1)} collective-permute-done((bf16[240,640]{1,0:T(8,128)(2,1)S(1)}, bf16[240,640]{1,0:T(8,128)(2,1)S(1)}, u32[]{:S(2)}, u32[]{:S(2)}) %collective-permute-start.2) | collective-permute-done | bytes 307232 | tf_op jit(solution)/shard_map/ppermute | solution.py:44
  97.1 2.7 collective-permute-start.4
  99.8 7.1 %collective-permute-done.4 = bf16[240,640]{1,0:T(8,128)(2,1)S(1)} collective-permute-done((bf16[240,640]{1,0:T(8,128)(2,1)S(1)}, bf16[240,640]{1,0:T(8,128)(2,1)S(1)}, u32[]{:S(2)}, u32[]{:S(2)}) %collective-permute-start.4) | collective-permute-done | bytes 307232 | tf_op jit(solution)/shard_map/ppermute | solution.py:44
  106.9 1.4 collective-permute-start.5
  108.3 2.5 collective-permute-start.6
  112.0 1.4 copy-done.1
  113.4 1.4 copy-done.3
  114.8 1.4 copy-done.5
  116.2 1.3 start_full.1
  117.6 2.3 collective-permute-start.8
  120.0 3.5 %collective-permute-done.6.refs_6_ = bf16[240,640]{1,0:T(8,128)(2,1)S(1)} collective-permute-done((bf16[240,640]{1,0:T(8,128)(2,1)S(1)}, bf16[240,640]{1,0:T(8,128)(2,1)S(1)}, u32[]{:S(2)}, u32[]{:S(2)}) %collective-permute-start.6) | collective-permute-done | bytes 307232 | tf_op jit(solution)/shard_map/ppermute | solution.py:44
  123.5 2.2 collective-permute-start.10
  125.7 2.1 constant_dynamic-slice_fusion
  127.9 2.7 collective-permute-start.33
  130.6 2.9 renorm.2
  133.5 7.7 %grads.3 = (f32[240,640]{1,0:T(8,128)S(1)}, bf16[240,640]{1,0:T(8,128)(2,1)S(1)}, bf16[240,640]{1,0:T(8,128)(2,1)S(1)}, bf16[240,640]{1,0:T(8,128)(2,1)S(1)}) custom-call(s32[4]{0:T(128)S(1)} %pad_add_fusion.place_ref.refs_0_, bf16[3,640,640]{2,1,0:T(8,128)(2,1)S(1)} %get-tuple-element.47.high_ref.refs_1_, ...), custom_call_target="tpu_custom_call" | custom-call | flops 2516582400 | bytes 8388608 | tf_op jit(solution)/shard_map/grads/pallas_call | solution.py:259
  141.2 2.5 collective-permute-start.18
  145.2 5.4 %collective-permute-done.18 = bf16[240,640]{1,0:T(8,128)(2,1)S(1)} collective-permute-done((bf16[240,640]{1,0:T(8,128)(2,1)S(1)}, bf16[240,640]{1,0:T(8,128)(2,1)S(1)}, u32[]{:S(2)}, u32[]{:S(2)}) %collective-permute-start.18) | collective-permute-done | bytes 307232 | tf_op jit(solution)/shard_map/ppermute | solution.py:44
  150.6 6.6 %collective-permute-done.17 = bf16[240,640]{1,0:T(8,128)(2,1)S(1)} collective-permute-done((bf16[240,640]{1,0:T(8,128)(2,1)S(1)}, bf16[240,640]{1,0:T(8,128)(2,1)S(1)}, u32[]{:S(2)}, u32[]{:S(2)}) %collective-permute-start.17) | collective-permute-done | bytes 307232 | tf_op jit(solution)/shard_map/ppermute | solution.py:44
  158.8 2.7 collective-permute-start.19
  161.5 7.2 %collective-permute-done.19 = bf16[240,640]{1,0:T(8,128)(2,1)S(1)} collective-permute-done((bf16[240,640]{1,0:T(8,128)(2,1)S(1)}, bf16[240,640]{1,0:T(8,128)(2,1)S(1)}, u32[]{:S(2)}, u32[]{:S(2)}) %collective-permute-start.19) | collective-permute-done | bytes 307232 | tf_op jit(solution)/shard_map/ppermute | solution.py:44
  169.9 2.1 collective-permute-start.21
  172.0 1.3 collective-permute-start.22
  173.3 2.2 collective-permute-start.23
  175.5 2.0 collective-permute-done.20.refs_6_
  177.5 3.5 %collective-permute-start.24 = (bf16[240,640]{1,0:T(8,128)(2,1)S(1)}, bf16[240,640]{1,0:T(8,128)(2,1)S(1)}, u32[]{:S(2)}, u32[]{:S(2)}) collective-permute-start(bf16[240,640]{1,0:T(8,128)(2,1)S(1)} %collective-permute-done.20.refs_6_), channel_id=1, source_target_pairs={{0,8},{8,0},{1,9},{9,1},{2,10},{10,2},{3,11},{11,3},{4,12},{12,4},... | collective-permute-start | bytes 921608 | tf_op jit(solution)/shard_map/ppermute | solution.py:44
  181.1 3.5 %collective-permute-done.21.refs_7_ = bf16[240,640]{1,0:T(8,128)(2,1)S(1)} collective-permute-done((bf16[240,640]{1,0:T(8,128)(2,1)S(1)}, bf16[240,640]{1,0:T(8,128)(2,1)S(1)}, u32[]{:S(2)}, u32[]{:S(2)}) %collective-permute-start.21) | collective-permute-done | bytes 307232 | tf_op jit(solution)/shard_map/ppermute | solution.py:44
  184.6 2.2 collective-permute-start.25
  187.0 2.7 collective-permute-start.35
  189.6 2.7 collective-permute-start.34
  192.3 1.5 collective-permute-start.38
  193.8 4.4 %apply_weights.2 = (bf16[128,640]{1,0:T(8,128)(2,1)S(1)}, bf16[128,640]{1,0:T(8,128)(2,1)S(1)}, bf16[128,640]{1,0:T(8,128)(2,1)S(1)}, bf16[128,640]{1,0:T(8,128)(2,1)S(1)}) custom-call(s32[4]{0:T(128)S(1)} %pad_add_fusion.place_ref.refs_0_, bf16[3,640,640]{2,1,0:T(8,128)(2,1)S(1)} %get-tuple-element.47.high_ref.refs_1_, ...), custom_call_target="tpu_custom_call" | custom-call | flops 2097152000 | bytes 5242880 | tf_op jit(solution)/shard_map/apply_weights/pallas_call | solution.py:313
  198.2 2.9 renorm.3
  201.1 24.0 %collective-permute-done.31.refs_11_ = bf16[320,2560]{1,0:T(8,128)(2,1)S(1)} collective-permute-done((bf16[320,2560]{1,0:T(8,128)(2,1)S(1)}, bf16[320,2560]{1,0:T(8,128)(2,1)S(1)}, u32[]{:S(2)}, u32[]{:S(2)}) %collective-permute-start.31) | collective-permute-done | bytes 1638432 | tf_op jit(solution)/shard_map/ppermute | solution.py:44
  225.1 4.4 %apply_weights.3 = (bf16[128,640]{1,0:T(8,128)(2,1)S(1)}, bf16[128,640]{1,0:T(8,128)(2,1)S(1)}, bf16[128,640]{1,0:T(8,128)(2,1)S(1)}, bf16[128,640]{1,0:T(8,128)(2,1)S(1)}) custom-call(s32[4]{0:T(128)S(1)} %pad_add_fusion.place_ref.refs_0_, bf16[3,640,640]{2,1,0:T(8,128)(2,1)S(1)} %get-tuple-element.57.high_ref, ...), custom_call_target="tpu_custom_call" | custom-call | flops 2097152000 | bytes 5242880 | tf_op jit(solution)/shard_map/apply_weights/pallas_call | solution.py:313
  230.1 30.2 %collective-permute-done.32.refs_12_ = bf16[320,2560]{1,0:T(8,128)(2,1)S(1)} collective-permute-done((bf16[320,2560]{1,0:T(8,128)(2,1)S(1)}, bf16[320,2560]{1,0:T(8,128)(2,1)S(1)}, u32[]{:S(2)}, u32[]{:S(2)}) %collective-permute-start.32) | collective-permute-done | bytes 1638432 | tf_op jit(solution)/shard_map/ppermute | solution.py:44
  260.3 1.5 collective-permute-start.27
  261.7 5.3 %collective-permute-start.28 = (bf16[128,640]{1,0:T(8,128)(2,1)S(1)}, bf16[128,640]{1,0:T(8,128)(2,1)S(1)}, u32[]{:S(2)}, u32[]{:S(2)}) collective-permute-start(bf16[128,640]{1,0:T(8,128)(2,1)S(1)} %get-tuple-element.61), channel_id=1, source_target_pairs={{0,4},{2,6},{4,0},{6,2},{1,5},{3,7},{5,1},{7,3},{8,12},{10,14},{12... | collective-permute-start | bytes 491528 | tf_op jit(solution)/shard_map/ppermute | solution.py:44
  267.3 3.3 %collective-permute-start.39 = (bf16[320,2560]{1,0:T(8,128)(2,1)S(1)}, bf16[320,2560]{1,0:T(8,128)(2,1)S(1)}, u32[]{:S(2)}, u32[]{:S(2)}) collective-permute-start(bf16[320,2560]{1,0:T(8,128)(2,1)S(1)} %collective-permute-done.31.refs_11_), channel_id=1, source_target_pairs={{0,8},{8,0},{1,9},{9,1},{2,10},{10,2},{3,11},{11,3},{4,12},{12,4},... | collective-permute-start | bytes 4915208 | tf_op jit(solution)/shard_map/ppermute | solution.py:44
  270.7 3.2 %collective-permute-start.43 = (bf16[320,2560]{1,0:T(8,128)(2,1)S(1)}, bf16[320,2560]{1,0:T(8,128)(2,1)S(1)}, u32[]{:S(2)}, u32[]{:S(2)}) collective-permute-start(bf16[320,2560]{1,0:T(8,128)(2,1)S(1)} %collective-permute-done.33.refs_15_), channel_id=1, source_target_pairs={{0,8},{8,0},{1,9},{9,1},{2,10},{10,2},{3,11},{11,3},{4,12},{12,4},... | collective-permute-start | bytes 4915208 | tf_op jit(solution)/shard_map/ppermute | solution.py:44
  274.0 1.8 collective-permute-start.40
  275.9 5.5 %shard_map.91 = (bf16[128,1280]{1,0:T(8,128)(2,1)S(1)}, bf16[128,1280]{1,0:T(8,128)(2,1)S(1)}) custom-call(s32[4]{0:T(128)S(1)} %pad_add_fusion.place_ref.refs_0_, bf16[128,640]{1,0:T(8,128)(2,1)S(1)} %get-tuple-element.49.refs_1_, bf16[128,640]{1,0:T(8,128)(2,1)S(1)} %collective-permute-done.12.refs_2_, ...), custom_call_target="tpu_custom_call" | custom-call | flops 1677721600 | bytes 6553600 | tf_op jit(solution)/shard_map/pallas_call | solution.py:387
  281.3 5.5 %shard_map.92 = (bf16[128,1280]{1,0:T(8,128)(2,1)S(1)}, bf16[128,1280]{1,0:T(8,128)(2,1)S(1)}) custom-call(s32[4]{0:T(128)S(1)} %pad_add_fusion.place_ref.refs_0_, bf16[128,640]{1,0:T(8,128)(2,1)S(1)} %get-tuple-element.49.refs_1_, bf16[128,640]{1,0:T(8,128)(2,1)S(1)} %collective-permute-done.12.refs_2_, ...), custom_call_target="tpu_custom_call" | custom-call | flops 1677721600 | bytes 6553600 | tf_op jit(solution)/shard_map/pallas_call | solution.py:387
  288.4 5.5 %shard_map.93 = (bf16[128,1280]{1,0:T(8,128)(2,1)S(1)}, bf16[128,1280]{1,0:T(8,128)(2,1)S(1)}) custom-call(s32[4]{0:T(128)S(1)} %pad_add_fusion.place_ref.refs_0_, bf16[128,640]{1,0:T(8,128)(2,1)S(1)} %get-tuple-element.49.refs_1_, bf16[128,640]{1,0:T(8,128)(2,1)S(1)} %collective-permute-done.12.refs_2_, ...), custom_call_target="tpu_custom_call" | custom-call | flops 1677721600 | bytes 6553600 | tf_op jit(solution)/shard_map/pallas_call | solution.py:387
  294.5 5.5 %shard_map.94 = (bf16[128,1280]{1,0:T(8,128)(2,1)S(1)}, bf16[128,1280]{1,0:T(8,128)(2,1)S(1)}) custom-call(s32[4]{0:T(128)S(1)} %pad_add_fusion.place_ref.refs_0_, bf16[128,640]{1,0:T(8,128)(2,1)S(1)} %get-tuple-element.49.refs_1_, bf16[128,640]{1,0:T(8,128)(2,1)S(1)} %collective-permute-done.12.refs_2_, ...), custom_call_target="tpu_custom_call" | custom-call | flops 1677721600 | bytes 6553600 | tf_op jit(solution)/shard_map/pallas_call | solution.py:387
  301.0 1.8 collective-permute-done.37.refs_3_
  302.8 7.0 %collective-permute-done.44.refs_5_ = bf16[128,1280]{1,0:T(8,128)(2,1)S(1)} collective-permute-done((bf16[128,1280]{1,0:T(8,128)(2,1)S(1)}, bf16[128,1280]{1,0:T(8,128)(2,1)S(1)}, u32[]{:S(2)}, u32[]{:S(2)}) %collective-permute-start.44) | collective-permute-done | bytes 327712 | tf_op jit(solution)/shard_map/ppermute | solution.py:44
  309.9 7.0 %collective-permute-done.45.refs_7_ = bf16[128,1280]{1,0:T(8,128)(2,1)S(1)} collective-permute-done((bf16[128,1280]{1,0:T(8,128)(2,1)S(1)}, bf16[128,1280]{1,0:T(8,128)(2,1)S(1)}, u32[]{:S(2)}, u32[]{:S(2)}) %collective-permute-start.45) | collective-permute-done | bytes 327712 | tf_op jit(solution)/shard_map/ppermute | solution.py:44
  316.9 1.9 finish.1
  (79 shorter events, 12.9 us)
Async XLA Ops:
  2.5 24.6 %all-to-all-start = ((bf16[8,128,640]{2,1,0:T(8,128)(2,1)}), bf16[8,128,640]{2,1,0:T(8,128)(2,1)S(1)}, u32[]{:S(2)}, u32[]{:S(2)}) async-start(bf16[8,128,640]{2,1,0:T(8,128)(2,1)} %pack_first.1), calls=%async_computation | async-start | bytes 2621440 | tf_op jit(solution)/shard_map/all_to_all | solution.py:48
  27.1 1.1 copy-start.6
  28.2 34.8 %all-to-all-start.1 = ((bf16[8,256,640]{2,1,0:T(8,128)(2,1)}), bf16[8,256,640]{2,1,0:T(8,128)(2,1)S(1)}, u32[]{:S(2)}, u32[]{:S(2)}) async-start(bf16[8,256,640]{2,1,0:T(8,128)(2,1)} %pack_second.1), calls=%async_computation.1 | async-start | bytes 5242880 | tf_op jit(solution)/shard_map/all_to_all | solution.py:48
  31.9 40.0 %collective-permute-start = (bf16[8,128,640]{2,1,0:T(8,128)(2,1)}, bf16[8,128,640]{2,1,0:T(8,128)(2,1)}, u32[]{:S(2)}, u32[]{:S(2)}) collective-permute-start(bf16[8,128,640]{2,1,0:T(8,128)(2,1)} %copy-done.6), channel_id=1, source_target_pairs={{0,8},{8,0},{1,9},{9,1},{2,10},{10,2},{3,11},{11,3},{4,12},{12,4},... | collective-permute-start | bytes 3932168 | tf_op jit(solution)/shard_map/ppermute | solution.py:44
  62.9 70.5 %collective-permute-start.15 = (bf16[8,256,640]{2,1,0:T(8,128)(2,1)S(1)}, bf16[8,256,640]{2,1,0:T(8,128)(2,1)}, u32[]{:S(2)}, u32[]{:S(2)}) collective-permute-start(bf16[8,256,640]{2,1,0:T(8,128)(2,1)S(1)} %all-to-all-done.1.query_ref.near_ref), channel_id=1, source_target_pairs={{0,8},{8,0},{1,9},{9,1},{2,10},{10,2},{3,11},{11,3},{4,12},{12,4},... | collective-permute-start | bytes 7864328 | tf_op jit(solution)/shard_map/ppermute | solution.py:44
  65.5 1.4 copy-start
  67.0 1.4 copy-start.2
  68.4 1.4 copy-start.4
  69.8 2.1 copy-start.7
  79.5 10.4 %collective-permute-start.3 = (bf16[240,640]{1,0:T(8,128)(2,1)S(1)}, bf16[240,640]{1,0:T(8,128)(2,1)S(1)}, u32[]{:S(2)}, u32[]{:S(2)}) collective-permute-start(bf16[240,640]{1,0:T(8,128)(2,1)S(1)} %get-tuple-element.46), channel_id=1, source_target_pairs={{0,64},{32,96},{64,0},{96,32},{1,65},{33,97},{65,1},{97,33},{2,66}... | collective-permute-start | bytes 921608 | tf_op jit(solution)/shard_map/ppermute | solution.py:44
  82.3 14.3 %collective-permute-start.2 = (bf16[240,640]{1,0:T(8,128)(2,1)S(1)}, bf16[240,640]{1,0:T(8,128)(2,1)S(1)}, u32[]{:S(2)}, u32[]{:S(2)}) collective-permute-start(bf16[240,640]{1,0:T(8,128)(2,1)S(1)} %get-tuple-element.45), channel_id=1, source_target_pairs={{0,96},{32,0},{64,32},{96,64},{1,97},{33,1},{65,33},{97,65},{2,98}... | collective-permute-start | bytes 921608 | tf_op jit(solution)/shard_map/ppermute | solution.py:44
  83.2 13.7 %collective-permute-start.1 = (bf16[240,640]{1,0:T(8,128)(2,1)S(1)}, bf16[240,640]{1,0:T(8,128)(2,1)S(1)}, u32[]{:S(2)}, u32[]{:S(2)}) collective-permute-start(bf16[240,640]{1,0:T(8,128)(2,1)S(1)} %get-tuple-element.44), channel_id=1, source_target_pairs={{0,32},{32,64},{64,96},{96,0},{1,33},{33,65},{65,97},{97,1},{2,34}... | collective-permute-start | bytes 921608 | tf_op jit(solution)/shard_map/ppermute | solution.py:44
  97.1 9.8 %collective-permute-start.4 = (bf16[240,640]{1,0:T(8,128)(2,1)S(1)}, bf16[240,640]{1,0:T(8,128)(2,1)S(1)}, u32[]{:S(2)}, u32[]{:S(2)}) collective-permute-start(bf16[240,640]{1,0:T(8,128)(2,1)S(1)} %convert_element_type.39), channel_id=1, source_target_pairs={{0,16},{16,0},{1,17},{17,1},{2,18},{18,2},{3,19},{19,3},{4,20},{20... | collective-permute-start | bytes 921608 | tf_op jit(solution)/shard_map/ppermute | solution.py:44
  106.9 12.9 %collective-permute-start.5 = (bf16[240,640]{1,0:T(8,128)(2,1)S(1)}, bf16[240,640]{1,0:T(8,128)(2,1)S(1)}, u32[]{:S(2)}, u32[]{:S(2)}) collective-permute-start(bf16[240,640]{1,0:T(8,128)(2,1)S(1)} %add_convert_fusion.1.refs_4_), channel_id=1, source_target_pairs={{0,32},{32,64},{64,96},{96,0},{1,33},{33,65},{65,97},{97,1},{2,34}... | collective-permute-start | bytes 921608 | tf_op jit(solution)/shard_map/ppermute | solution.py:44
  108.3 15.2 %collective-permute-start.6 = (bf16[240,640]{1,0:T(8,128)(2,1)S(1)}, bf16[240,640]{1,0:T(8,128)(2,1)S(1)}, u32[]{:S(2)}, u32[]{:S(2)}) collective-permute-start(bf16[240,640]{1,0:T(8,128)(2,1)S(1)} %add_convert_fusion.1.refs_4_), channel_id=1, source_target_pairs={{0,64},{32,96},{64,0},{96,32},{1,65},{33,97},{65,1},{97,33},{2,66}... | collective-permute-start | bytes 921608 | tf_op jit(solution)/shard_map/ppermute | solution.py:44
  110.9 14.8 %collective-permute-start.7 = (bf16[240,640]{1,0:T(8,128)(2,1)S(1)}, bf16[240,640]{1,0:T(8,128)(2,1)}, u32[]{:S(2)}, u32[]{:S(2)}) collective-permute-start(bf16[240,640]{1,0:T(8,128)(2,1)S(1)} %add_convert_fusion.1.refs_4_), channel_id=1, source_target_pairs={{0,96},{32,0},{64,32},{96,64},{1,97},{33,1},{65,33},{97,65},{2,98}... | collective-permute-start | bytes 921608 | tf_op jit(solution)/shard_map/ppermute | solution.py:44
  111.9 1.4 copy-start.1
  113.4 1.4 copy-start.3
  114.8 1.4 copy-start.5
  117.6 10.2 %collective-permute-start.8 = (bf16[240,640]{1,0:T(8,128)(2,1)S(1)}, bf16[240,640]{1,0:T(8,128)(2,1)S(1)}, u32[]{:S(2)}, u32[]{:S(2)}) collective-permute-start(bf16[240,640]{1,0:T(8,128)(2,1)S(1)} %add_convert_fusion.1.refs_4_), channel_id=1, source_target_pairs={{0,8},{8,0},{1,9},{9,1},{2,10},{10,2},{3,11},{11,3},{4,12},{12,4},... | collective-permute-start | bytes 921608 | tf_op jit(solution)/shard_map/ppermute | solution.py:44
  119.9 8.0 %collective-permute-start.9 = (bf16[240,640]{1,0:T(8,128)(2,1)S(1)}, bf16[240,640]{1,0:T(8,128)(2,1)S(1)}, u32[]{:S(2)}, u32[]{:S(2)}) collective-permute-start(bf16[240,640]{1,0:T(8,128)(2,1)S(1)} %collective-permute-done.5.refs_5_), channel_id=1, source_target_pairs={{0,8},{8,0},{1,9},{9,1},{2,10},{10,2},{3,11},{11,3},{4,12},{12,4},... | collective-permute-start | bytes 921608 | tf_op jit(solution)/shard_map/ppermute | solution.py:44
  123.5 7.1 %collective-permute-start.10 = (bf16[240,640]{1,0:T(8,128)(2,1)S(1)}, bf16[240,640]{1,0:T(8,128)(2,1)S(1)}, u32[]{:S(2)}, u32[]{:S(2)}) collective-permute-start(bf16[240,640]{1,0:T(8,128)(2,1)S(1)} %collective-permute-done.6.refs_6_), channel_id=1, source_target_pairs={{0,8},{8,0},{1,9},{9,1},{2,10},{10,2},{3,11},{11,3},{4,12},{12,4},... | collective-permute-start | bytes 921608 | tf_op jit(solution)/shard_map/ppermute | solution.py:44
  125.7 4.9 %collective-permute-start.11 = (bf16[240,640]{1,0:T(8,128)(2,1)}, bf16[240,640]{1,0:T(8,128)(2,1)S(1)}, u32[]{:S(2)}, u32[]{:S(2)}) collective-permute-start(bf16[240,640]{1,0:T(8,128)(2,1)} %collective-permute-done.7.refs_7_), channel_id=1, source_target_pairs={{0,8},{8,0},{1,9},{9,1},{2,10},{10,2},{3,11},{11,3},{4,12},{12,4},... | collective-permute-start | bytes 921608 | tf_op jit(solution)/shard_map/ppermute | solution.py:44
  127.8 45.5 %collective-permute-start.30 = (bf16[320,2560]{1,0:T(8,128)(2,1)S(1)}, bf16[320,2560]{1,0:T(8,128)(2,1)S(1)}, u32[]{:S(2)}, u32[]{:S(2)}) collective-permute-start(bf16[320,2560]{1,0:T(8,128)(2,1)S(1)} %get-tuple-element.72), channel_id=1, source_target_pairs={{0,2},{2,4},{4,6},{6,0},{1,3},{3,5},{5,7},{7,1},{8,10},{10,12},{12... | collective-permute-start | bytes 4915208 | tf_op jit(solution)/shard_map/ppermute | solution.py:44
  127.9 59.0 %collective-permute-start.33 = (bf16[320,2560]{1,0:T(8,128)(2,1)S(1)}, bf16[320,2560]{1,0:T(8,128)(2,1)S(1)}, u32[]{:S(2)}, u32[]{:S(2)}) collective-permute-start(bf16[320,2560]{1,0:T(8,128)(2,1)S(1)} %get-tuple-element.71), channel_id=1, source_target_pairs={{0,6},{2,0},{4,2},{6,4},{1,7},{3,1},{5,3},{7,5},{8,14},{10,8},{12,... | collective-permute-start | bytes 4915208 | tf_op jit(solution)/shard_map/ppermute | solution.py:44
  141.2 9.4 %collective-permute-start.18 = (bf16[240,640]{1,0:T(8,128)(2,1)S(1)}, bf16[240,640]{1,0:T(8,128)(2,1)S(1)}, u32[]{:S(2)}, u32[]{:S(2)}) collective-permute-start(bf16[240,640]{1,0:T(8,128)(2,1)S(1)} %get-tuple-element.56), channel_id=1, source_target_pairs={{0,64},{32,96},{64,0},{96,32},{1,65},{33,97},{65,1},{97,33},{2,66}... | collective-permute-start | bytes 921608 | tf_op jit(solution)/shard_map/ppermute | solution.py:44
  143.7 13.5 %collective-permute-start.17 = (bf16[240,640]{1,0:T(8,128)(2,1)S(1)}, bf16[240,640]{1,0:T(8,128)(2,1)S(1)}, u32[]{:S(2)}, u32[]{:S(2)}) collective-permute-start(bf16[240,640]{1,0:T(8,128)(2,1)S(1)} %get-tuple-element.55), channel_id=1, source_target_pairs={{0,96},{32,0},{64,32},{96,64},{1,97},{33,1},{65,33},{97,65},{2,98}... | collective-permute-start | bytes 921608 | tf_op jit(solution)/shard_map/ppermute | solution.py:44
  144.7 13.8 %collective-permute-start.16 = (bf16[240,640]{1,0:T(8,128)(2,1)S(1)}, bf16[240,640]{1,0:T(8,128)(2,1)S(1)}, u32[]{:S(2)}, u32[]{:S(2)}) collective-permute-start(bf16[240,640]{1,0:T(8,128)(2,1)S(1)} %get-tuple-element.54), channel_id=1, source_target_pairs={{0,32},{32,64},{64,96},{96,0},{1,33},{33,65},{65,97},{97,1},{2,34}... | collective-permute-start | bytes 921608 | tf_op jit(solution)/shard_map/ppermute | solution.py:44
  158.6 35.2 %copy-start.8 = (f32[640]{0:T(1024)S(1)}, f32[640]{0:T(1024)}, u32[]{:S(2)}) copy-start(f32[640]{0:T(1024)} %param.16) | copy-start | bytes 7684
  158.8 9.9 %collective-permute-start.19 = (bf16[240,640]{1,0:T(8,128)(2,1)S(1)}, bf16[240,640]{1,0:T(8,128)(2,1)S(1)}, u32[]{:S(2)}, u32[]{:S(2)}) collective-permute-start(bf16[240,640]{1,0:T(8,128)(2,1)S(1)} %convert_element_type.45), channel_id=1, source_target_pairs={{0,16},{16,0},{1,17},{17,1},{2,18},{18,2},{3,19},{19,3},{4,20},{20... | collective-permute-start | bytes 921608 | tf_op jit(solution)/shard_map/ppermute | solution.py:44
  168.8 8.8 %collective-permute-start.20 = (bf16[240,640]{1,0:T(8,128)(2,1)S(1)}, bf16[240,640]{1,0:T(8,128)(2,1)S(1)}, u32[]{:S(2)}, u32[]{:S(2)}) collective-permute-start(bf16[240,640]{1,0:T(8,128)(2,1)S(1)} %add_convert_fusion.refs_5_), channel_id=1, source_target_pairs={{0,32},{32,64},{64,96},{96,0},{1,33},{33,65},{65,97},{97,1},{2,34}... | collective-permute-start | bytes 921608 | tf_op jit(solution)/shard_map/ppermute | solution.py:44
  169.9 14.7 %collective-permute-start.21 = (bf16[240,640]{1,0:T(8,128)(2,1)S(1)}, bf16[240,640]{1,0:T(8,128)(2,1)S(1)}, u32[]{:S(2)}, u32[]{:S(2)}) collective-permute-start(bf16[240,640]{1,0:T(8,128)(2,1)S(1)} %add_convert_fusion.refs_5_), channel_id=1, source_target_pairs={{0,64},{32,96},{64,0},{96,32},{1,65},{33,97},{65,1},{97,33},{2,66}... | collective-permute-start | bytes 921608 | tf_op jit(solution)/shard_map/ppermute | solution.py:44
  172.0 14.8 %collective-permute-start.22 = (bf16[240,640]{1,0:T(8,128)(2,1)S(1)}, bf16[240,640]{1,0:T(8,128)(2,1)S(1)}, u32[]{:S(2)}, u32[]{:S(2)}) collective-permute-start(bf16[240,640]{1,0:T(8,128)(2,1)S(1)} %add_convert_fusion.refs_5_), channel_id=1, source_target_pairs={{0,96},{32,0},{64,32},{96,64},{1,97},{33,1},{65,33},{97,65},{2,98}... | collective-permute-start | bytes 921608 | tf_op jit(solution)/shard_map/ppermute | solution.py:44
  173.3 13.6 %collective-permute-start.23 = (bf16[240,640]{1,0:T(8,128)(2,1)S(1)}, bf16[240,640]{1,0:T(8,128)(2,1)S(1)}, u32[]{:S(2)}, u32[]{:S(2)}) collective-permute-start(bf16[240,640]{1,0:T(8,128)(2,1)S(1)} %add_convert_fusion.refs_5_), channel_id=1, source_target_pairs={{0,8},{8,0},{1,9},{9,1},{2,10},{10,2},{3,11},{11,3},{4,12},{12,4},... | collective-permute-start | bytes 921608 | tf_op jit(solution)/shard_map/ppermute | solution.py:44
  177.5 12.1 %collective-permute-start.24 = (bf16[240,640]{1,0:T(8,128)(2,1)S(1)}, bf16[240,640]{1,0:T(8,128)(2,1)S(1)}, u32[]{:S(2)}, u32[]{:S(2)}) collective-permute-start(bf16[240,640]{1,0:T(8,128)(2,1)S(1)} %collective-permute-done.20.refs_6_), channel_id=1, source_target_pairs={{0,8},{8,0},{1,9},{9,1},{2,10},{10,2},{3,11},{11,3},{4,12},{12,4},... | collective-permute-start | bytes 921608 | tf_op jit(solution)/shard_map/ppermute | solution.py:44
  184.6 5.0 %collective-permute-start.25 = (bf16[240,640]{1,0:T(8,128)(2,1)S(1)}, bf16[240,640]{1,0:T(8,128)(2,1)S(1)}, u32[]{:S(2)}, u32[]{:S(2)}) collective-permute-start(bf16[240,640]{1,0:T(8,128)(2,1)S(1)} %collective-permute-done.21.refs_7_), channel_id=1, source_target_pairs={{0,8},{8,0},{1,9},{9,1},{2,10},{10,2},{3,11},{11,3},{4,12},{12,4},... | collective-permute-start | bytes 921608 | tf_op jit(solution)/shard_map/ppermute | solution.py:44
  186.8 5.5 %collective-permute-start.26 = (bf16[240,640]{1,0:T(8,128)(2,1)S(1)}, bf16[240,640]{1,0:T(8,128)(2,1)S(1)}, u32[]{:S(2)}, u32[]{:S(2)}) collective-permute-start(bf16[240,640]{1,0:T(8,128)(2,1)S(1)} %collective-permute-done.22.refs_8_), channel_id=1, source_target_pairs={{0,8},{8,0},{1,9},{9,1},{2,10},{10,2},{3,11},{11,3},{4,12},{12,4},... | collective-permute-start | bytes 921608 | tf_op jit(solution)/shard_map/ppermute | solution.py:44
  186.9 38.2 %collective-permute-start.31 = (bf16[320,2560]{1,0:T(8,128)(2,1)S(1)}, bf16[320,2560]{1,0:T(8,128)(2,1)S(1)}, u32[]{:S(2)}, u32[]{:S(2)}) collective-permute-start(bf16[320,2560]{1,0:T(8,128)(2,1)S(1)} %get-tuple-element.71), channel_id=1, source_target_pairs={{0,2},{2,4},{4,6},{6,0},{1,3},{3,5},{5,7},{7,1},{8,10},{10,12},{12... | collective-permute-start | bytes 4915208 | tf_op jit(solution)/shard_map/ppermute | solution.py:44
  187.0 42.6 %collective-permute-start.35 = (bf16[320,2560]{1,0:T(8,128)(2,1)S(1)}, bf16[320,2560]{1,0:T(8,128)(2,1)S(1)}, u32[]{:S(2)}, u32[]{:S(2)}) collective-permute-start(bf16[320,2560]{1,0:T(8,128)(2,1)S(1)} %get-tuple-element.72), channel_id=1, source_target_pairs={{0,6},{2,0},{4,2},{6,4},{1,7},{3,1},{5,3},{7,5},{8,14},{10,8},{12,... | collective-permute-start | bytes 4915208 | tf_op jit(solution)/shard_map/ppermute | solution.py:44
  189.6 70.6 %collective-permute-start.32 = (bf16[320,2560]{1,0:T(8,128)(2,1)S(1)}, bf16[320,2560]{1,0:T(8,128)(2,1)S(1)}, u32[]{:S(2)}, u32[]{:S(2)}) collective-permute-start(bf16[320,2560]{1,0:T(8,128)(2,1)S(1)} %collective-permute-done.30.refs_10_), channel_id=1, source_target_pairs={{0,2},{2,4},{4,6},{6,0},{1,3},{3,5},{5,7},{7,1},{8,10},{10,12},{12... | collective-permute-start | bytes 4915208 | tf_op jit(solution)/shard_map/ppermute | solution.py:44
  189.6 70.6 %collective-permute-start.34 = (bf16[320,2560]{1,0:T(8,128)(2,1)S(1)}, bf16[320,2560]{1,0:T(8,128)(2,1)S(1)}, u32[]{:S(2)}, u32[]{:S(2)}) collective-permute-start(bf16[320,2560]{1,0:T(8,128)(2,1)S(1)} %collective-permute-done.33.refs_15_), channel_id=1, source_target_pairs={{0,6},{2,0},{4,2},{6,4},{1,7},{3,1},{5,3},{7,5},{8,14},{10,8},{12,... | collective-permute-start | bytes 4915208 | tf_op jit(solution)/shard_map/ppermute | solution.py:44
  192.3 69.4 %collective-permute-start.38 = (bf16[320,2560]{1,0:T(8,128)(2,1)S(1)}, bf16[320,2560]{1,0:T(8,128)(2,1)S(1)}, u32[]{:S(2)}, u32[]{:S(2)}) collective-permute-start(bf16[320,2560]{1,0:T(8,128)(2,1)S(1)} %collective-permute-done.30.refs_10_), channel_id=1, source_target_pairs={{0,8},{8,0},{1,9},{9,1},{2,10},{10,2},{3,11},{11,3},{4,12},{12,4},... | collective-permute-start | bytes 4915208 | tf_op jit(solution)/shard_map/ppermute | solution.py:44
  193.8 82.0 %slice-start = ((s8[6553600]{0:T(1024)(128)(4,1)}), s8[4194304]{0:T(1024)(128)(4,1)S(1)}, s32[]{:S(2)}) async-start(s8[6553600]{0:T(1024)(128)(4,1)} %bitcast.5), calls=%async_computation.2 | async-start | bytes 8388608
  198.2 77.6 %slice-start.1 = ((s8[6553600]{0:T(1024)(128)(4,1)}), s8[2359296]{0:T(1024)(128)(4,1)S(1)}, s32[]{:S(2)}) async-start(s8[6553600]{0:T(1024)(128)(4,1)} %bitcast.5), calls=%async_computation.3 | async-start | bytes 4718592
  225.1 42.1 %collective-permute-start.12 = (bf16[128,640]{1,0:T(8,128)(2,1)S(1)}, bf16[128,640]{1,0:T(8,128)(2,1)S(1)}, u32[]{:S(2)}, u32[]{:S(2)}) collective-permute-start(bf16[128,640]{1,0:T(8,128)(2,1)S(1)} %get-tuple-element.50), channel_id=1, source_target_pairs={{0,2},{2,4},{4,6},{6,0},{1,3},{3,5},{5,7},{7,1},{8,10},{10,12},{12... | collective-permute-start | bytes 491528 | tf_op jit(solution)/shard_map/ppermute | solution.py:44
  229.5 37.7 %collective-permute-start.13 = (bf16[128,640]{1,0:T(8,128)(2,1)S(1)}, bf16[128,640]{1,0:T(8,128)(2,1)S(1)}, u32[]{:S(2)}, u32[]{:S(2)}) collective-permute-start(bf16[128,640]{1,0:T(8,128)(2,1)S(1)} %get-tuple-element.51), channel_id=1, source_target_pairs={{0,4},{2,6},{4,0},{6,2},{1,5},{3,7},{5,1},{7,3},{8,12},{10,14},{12... | collective-permute-start | bytes 491528 | tf_op jit(solution)/shard_map/ppermute | solution.py:44
  260.3 10.4 %collective-permute-start.14 = (bf16[128,640]{1,0:T(8,128)(2,1)S(1)}, bf16[128,640]{1,0:T(8,128)(2,1)S(1)}, u32[]{:S(2)}, u32[]{:S(2)}) collective-permute-start(bf16[128,640]{1,0:T(8,128)(2,1)S(1)} %get-tuple-element.52), channel_id=1, source_target_pairs={{0,6},{2,0},{4,2},{6,4},{1,7},{3,1},{5,3},{7,5},{8,14},{10,8},{12,... | collective-permute-start | bytes 491528 | tf_op jit(solution)/shard_map/ppermute | solution.py:44
  260.3 10.5 %collective-permute-start.27 = (bf16[128,640]{1,0:T(8,128)(2,1)S(1)}, bf16[128,640]{1,0:T(8,128)(2,1)S(1)}, u32[]{:S(2)}, u32[]{:S(2)}) collective-permute-start(bf16[128,640]{1,0:T(8,128)(2,1)S(1)} %get-tuple-element.60), channel_id=1, source_target_pairs={{0,2},{2,4},{4,6},{6,0},{1,3},{3,5},{5,7},{7,1},{8,10},{10,12},{12... | collective-permute-start | bytes 491528 | tf_op jit(solution)/shard_map/ppermute | solution.py:44
  261.7 12.2 %collective-permute-start.28 = (bf16[128,640]{1,0:T(8,128)(2,1)S(1)}, bf16[128,640]{1,0:T(8,128)(2,1)S(1)}, u32[]{:S(2)}, u32[]{:S(2)}) collective-permute-start(bf16[128,640]{1,0:T(8,128)(2,1)S(1)} %get-tuple-element.61), channel_id=1, source_target_pairs={{0,4},{2,6},{4,0},{6,2},{1,5},{3,7},{5,1},{7,3},{8,12},{10,14},{12... | collective-permute-start | bytes 491528 | tf_op jit(solution)/shard_map/ppermute | solution.py:44
  267.3 8.4 %collective-permute-start.29 = (bf16[128,640]{1,0:T(8,128)(2,1)S(1)}, bf16[128,640]{1,0:T(8,128)(2,1)S(1)}, u32[]{:S(2)}, u32[]{:S(2)}) collective-permute-start(bf16[128,640]{1,0:T(8,128)(2,1)S(1)} %get-tuple-element.62), channel_id=1, source_target_pairs={{0,6},{2,0},{4,2},{6,4},{1,7},{3,1},{5,3},{7,5},{8,14},{10,8},{12,... | collective-permute-start | bytes 491528 | tf_op jit(solution)/shard_map/ppermute | solution.py:44
  267.3 19.6 %collective-permute-start.39 = (bf16[320,2560]{1,0:T(8,128)(2,1)S(1)}, bf16[320,2560]{1,0:T(8,128)(2,1)S(1)}, u32[]{:S(2)}, u32[]{:S(2)}) collective-permute-start(bf16[320,2560]{1,0:T(8,128)(2,1)S(1)} %collective-permute-done.31.refs_11_), channel_id=1, source_target_pairs={{0,8},{8,0},{1,9},{9,1},{2,10},{10,2},{3,11},{11,3},{4,12},{12,4},... | collective-permute-start | bytes 4915208 | tf_op jit(solution)/shard_map/ppermute | solution.py:44
  270.6 16.8 %collective-permute-start.42 = (bf16[320,2560]{1,0:T(8,128)(2,1)S(1)}, bf16[320,2560]{1,0:T(8,128)(2,1)S(1)}, u32[]{:S(2)}, u32[]{:S(2)}) collective-permute-start(bf16[320,2560]{1,0:T(8,128)(2,1)S(1)} %collective-permute-done.35.refs_14_), channel_id=1, source_target_pairs={{0,8},{8,0},{1,9},{9,1},{2,10},{10,2},{3,11},{11,3},{4,12},{12,4},... | collective-permute-start | bytes 4915208 | tf_op jit(solution)/shard_map/ppermute | solution.py:44
  270.7 17.7 %collective-permute-start.43 = (bf16[320,2560]{1,0:T(8,128)(2,1)S(1)}, bf16[320,2560]{1,0:T(8,128)(2,1)S(1)}, u32[]{:S(2)}, u32[]{:S(2)}) collective-permute-start(bf16[320,2560]{1,0:T(8,128)(2,1)S(1)} %collective-permute-done.33.refs_15_), channel_id=1, source_target_pairs={{0,8},{8,0},{1,9},{9,1},{2,10},{10,2},{3,11},{11,3},{4,12},{12,4},... | collective-permute-start | bytes 4915208 | tf_op jit(solution)/shard_map/ppermute | solution.py:44
  274.0 14.4 %collective-permute-start.40 = (bf16[320,2560]{1,0:T(8,128)(2,1)S(1)}, bf16[320,2560]{1,0:T(8,128)(2,1)S(1)}, u32[]{:S(2)}, u32[]{:S(2)}) collective-permute-start(bf16[320,2560]{1,0:T(8,128)(2,1)S(1)} %collective-permute-done.32.refs_12_), channel_id=1, source_target_pairs={{0,8},{8,0},{1,9},{9,1},{2,10},{10,2},{3,11},{11,3},{4,12},{12,4},... | collective-permute-start | bytes 4915208 | tf_op jit(solution)/shard_map/ppermute | solution.py:44
  275.7 12.7 %collective-permute-start.41 = (bf16[320,2560]{1,0:T(8,128)(2,1)S(1)}, bf16[320,2560]{1,0:T(8,128)(2,1)S(1)}, u32[]{:S(2)}, u32[]{:S(2)}) collective-permute-start(bf16[320,2560]{1,0:T(8,128)(2,1)S(1)} %collective-permute-done.34.refs_13_), channel_id=1, source_target_pairs={{0,8},{8,0},{1,9},{9,1},{2,10},{10,2},{3,11},{11,3},{4,12},{12,4},... | collective-permute-start | bytes 4915208 | tf_op jit(solution)/shard_map/ppermute | solution.py:44
  286.8 14.2 %collective-permute-start.36 = (bf16[128,1280]{1,0:T(8,128)(2,1)S(1)}, bf16[128,1280]{1,0:T(8,128)(2,1)S(1)}, u32[]{:S(2)}, u32[]{:S(2)}) collective-permute-start(bf16[128,1280]{1,0:T(8,128)(2,1)S(1)} %get-tuple-element.64), channel_id=1, source_target_pairs={{0,1},{1,0},{2,3},{3,2},{4,5},{5,4},{6,7},{7,6},{8,9},{9,8},{10,11... | collective-permute-start | bytes 983048 | tf_op jit(solution)/shard_map/ppermute | solution.py:44
  287.5 15.4 %collective-permute-start.37 = (bf16[128,1280]{1,0:T(8,128)(2,1)S(1)}, bf16[128,1280]{1,0:T(8,128)(2,1)S(1)}, u32[]{:S(2)}, u32[]{:S(2)}) collective-permute-start(bf16[128,1280]{1,0:T(8,128)(2,1)S(1)} %get-tuple-element.66), channel_id=1, source_target_pairs={{0,1},{1,0},{2,3},{3,2},{4,5},{5,4},{6,7},{7,6},{8,9},{9,8},{10,11... | collective-permute-start | bytes 983048 | tf_op jit(solution)/shard_map/ppermute | solution.py:44
  293.9 16.0 %collective-permute-start.44 = (bf16[128,1280]{1,0:T(8,128)(2,1)S(1)}, bf16[128,1280]{1,0:T(8,128)(2,1)S(1)}, u32[]{:S(2)}, u32[]{:S(2)}) collective-permute-start(bf16[128,1280]{1,0:T(8,128)(2,1)S(1)} %get-tuple-element.68), channel_id=1, source_target_pairs={{0,1},{1,0},{2,3},{3,2},{4,5},{5,4},{6,7},{7,6},{8,9},{9,8},{10,11... | collective-permute-start | bytes 983048 | tf_op jit(solution)/shard_map/ppermute | solution.py:44
  300.0 16.9 %collective-permute-start.45 = (bf16[128,1280]{1,0:T(8,128)(2,1)S(1)}, bf16[128,1280]{1,0:T(8,128)(2,1)S(1)}, u32[]{:S(2)}, u32[]{:S(2)}) collective-permute-start(bf16[128,1280]{1,0:T(8,128)(2,1)S(1)} %get-tuple-element.70), channel_id=1, source_target_pairs={{0,1},{1,0},{2,3},{3,2},{4,5},{5,4},{6,7},{7,6},{8,9},{9,8},{10,11... | collective-permute-start | bytes 983048 | tf_op jit(solution)/shard_map/ppermute | solution.py:44
where the time goes:
time: 320 us; the launch traced here: 319 us
  waiting for transfers between devices  164 us (51%)
  starting transfers between devices  79.4 us (25%)
  Pallas kernels  63.1 us (20%)
  local copies, waits for them, and re-layouts  11.8 us (4%)
    ppermute x46, waiting for transfers between devices, shift(): lax.ppermute(array, axis, [(i, (i + by) % size) for i in range(size)])  120 us
    ppermute x46, starting transfers between devices, shift(): lax.ppermute(array, axis, [(i, (i + by) % size) for i in range(size)])  68.8 us
    all_to_all x2, waiting for transfers between devices, to_heads(): return lax.all_to_all(array, ('z', 'yl'), 0, 0, tiled=True)  43.5 us
    pallas_call x4, Pallas kernels, project(): pl.pallas_call(lambda *refs: project_body(side, part_of_side, *refs), gri...  21.9 us
    pallas_call x2, Pallas kernels, grads(): pl.pallas_call(grads_kernel, grid=(1,), in_specs=[SMEM] + [held] * 2 + [p...  15.3 us
    all_to_all x2, starting transfers between devices, to_heads(): return lax.all_to_all(array, ('z', 'yl'), 0, 0, tiled=True)  10.6 us
    unnamed x22, local copies, waits for them, and re-layouts  9.66 us
    pallas_call x2, Pallas kernels, apply_weights(): pl.pallas_call(apply_kernel, grid=(1,), in_specs=[SMEM, pl.BlockSpec((3,...  8.78 us
  transfers between devices with their start and end apart: 48, of which 19 were waited for; matrix products, arithmetic and copies ran while one was open for 1% of the time, Pallas kernels for 18%

commit v1 on v0

--- a/solution.py
+++ b/solution.py
@@ -16,8 +16,9 @@
 PART = 80
 PIECE = 240
 COLS = 2560
-SLAB = 1280
-TILE = 640
+LONG = 1536
+WIDTH = 1024
+TILE = 512
 
 
 VMEM = pl.BlockSpec(memory_space=pltpu.VMEM)
@@ -124,10 +125,13 @@
 
 
 def start_half_kernel(place_ref, gate_ref, up_ref, down_ref, high_ref, low_ref, turned):
-    half = pl.ds(pl.multiple_of(place_ref[0] * HALF, HALF), HALF)
+    core = place_ref[0]
+    half = pl.ds(pl.multiple_of(core * HALF, HALF), HALF)
+    tiles = pl.ds(pl.multiple_of(core * 256, 256), 384)
+    inside = pl.ds(pl.multiple_of(core * (HALF - 256), 64), HALF)
     for slot, ref in ((0, gate_ref), (1, up_ref)):
-        turned[...] = ref[0].T
-        high_ref[slot], low_ref[slot] = split(turned[half, :])
+        turned[...] = ref[0, :, tiles].T
+        high_ref[slot], low_ref[slot] = split(turned[inside, :])
     high_ref[2], low_ref[2] = split(down_ref[0, half, :])
 
 
@@ -137,7 +141,7 @@
         in_specs=[SMEM] + [VMEM] * 3,
         out_specs=[VMEM] * 2,
         out_shape=[pltpu.VMEM((3, HALF, HD), BF16)] * 2,
-        scratch_shapes=[pltpu.VMEM((HD, HD), F32)],
+        scratch_shapes=[pltpu.VMEM((384, HD), F32)],
         compiler_params=room(16),
         cost_estimate=cost(1 << 24, 3 * HD * HD * 6),
         name="start_half",
@@ -285,7 +289,7 @@
 
 
 def apply_kernel(place_ref, high_ref, low_ref, gain_ref, query_ref, *refs):
-    outs, (rows_in, rows_out) = refs[:4], refs[4:]
+    outs, trade_ref, (rows_in, rows_out) = refs[:4], refs[4], refs[5:]
     z, yl = place_ref[2], place_ref[3]
     for d in range(4):
         for dy in range(2):
@@ -307,6 +311,7 @@
     lax.fori_loop(0, 2, chunk, 0)
     for d in range(4):
         outs[d][...] = rows_out[d * 2 * TOK : (d + 1) * 2 * TOK, :]
+        trade_ref[d * TOK : (d + 1) * TOK, :] = rows_out[(2 * d + 1) * TOK : (2 * d + 2) * TOK, :]
 
 
 def apply_weights(block, place, weights, gain, queries):
@@ -320,8 +325,10 @@
             pl.BlockSpec((1, HD), lambda i: (0, 0)),
             pl.BlockSpec((8, TOK, HD), lambda i: (0, 2 + block, 0)),
         ],
-        out_specs=[pl.BlockSpec((2 * TOK, HD), lambda i: (0, 0))] * 4,
-        out_shape=[jax.ShapeDtypeStruct((2 * TOK, HD), BF16)] * 4,
+        out_specs=[pl.BlockSpec((2 * TOK, HD), lambda i: (0, 0))] * 4
+        + [pl.BlockSpec((4 * TOK, HD), lambda i: (0, 0))],
+        out_shape=[jax.ShapeDtypeStruct((2 * TOK, HD), BF16)] * 4
+        + [jax.ShapeDtypeStruct((4 * TOK, HD), BF16)],
         scratch_shapes=[pltpu.VMEM((8 * TOK, HD), BF16)] * 2,
         compiler_params=room(16),
         cost_estimate=cost(10 * 8 * TOK * HD * HD, 5 << 20),
@@ -329,22 +336,21 @@
     )(place, *weights, gain, queries)
 
 
-def project_body(side, part_of_side, place_ref, *refs):
-    rows, own, parts = refs[:8], refs[8], refs[9:15]
-    keep_ref, send_ref, both, slots, total, sems = refs[15:]
+def project_body(side, place_ref, *refs):
+    rows, own, parts = refs[:4], refs[4], refs[5:9]
+    keep_ref, send_ref, every, slots, sems = refs[9:]
     step = pl.program_id(0)
-    tiles = SLAB // TILE
-    base = part_of_side * SLAB
+    tiles = LONG // TILE
     half = place_ref[0] if side == 0 else 1 - place_ref[0]
 
     def copies(t):
         slot = lax.rem(t, 2)
-        cols = pl.ds(pl.multiple_of(base + t * TILE, TILE), TILE)
-        own_cols = pl.ds(pl.multiple_of(half * COLS + base + t * TILE, TILE), TILE)
+        cols = pl.ds(pl.multiple_of(t * TILE, TILE), TILE)
+        own_cols = pl.ds(pl.multiple_of(half * COLS + t * TILE, TILE), TILE)
         pairs = [(own.at[:, own_cols], slots.at[slot, pl.ds(0, HD)])]
-        for index, part in enumerate(parts):
-            start = HD + index * HALF
-            pairs.append((part.at[:, cols], slots.at[slot, pl.ds(start, HALF)]))
+        for part, start in zip(parts, (HD, 2 * HD, 2 * HD + HALF, 3 * HD)):
+            height = part.shape[0]
+            pairs.append((part.at[:, cols], slots.at[slot, pl.ds(start, height)]))
         return [
             pltpu.make_async_copy(source, target, sems.at[slot, index])
             for index, (source, target) in enumerate(pairs)
@@ -354,12 +360,8 @@
     def _():
         for copy in copies(step):
             copy.start()
-        for block in range(2):
-            for d in range(4):
-                piece = rows[block * 4 + d]
-                cols = slice(d * HD, (d + 1) * HD)
-                both[block * TOK : (block + 1) * TOK, cols] = piece[:TOK, :]
-                both[(2 + block) * TOK : (3 + block) * TOK, cols] = piece[TOK:, :]
+        for d in range(4):
+            every[:, d * HD : (d + 1) * HD] = rows[d][...]
 
     @pl.when(step + 1 < tiles)
     def _():
@@ -368,60 +370,102 @@
 
     for copy in copies(step):
         copy.wait()
-    slot = lax.rem(step, 2)
-
-    def depth(k, carry):
-        cols = pl.ds(pl.multiple_of(k * 512, 512), 512)
-        total[...] += nn(both[:, cols], slots[slot, cols, :])
-        return carry
-
-    total[...] = jnp.zeros_like(total)
-    lax.fori_loop(0, 5, depth, 0)
-    keep_ref[...] = total[: 2 * TOK, :].astype(BF16)
-    send_ref[...] = total[2 * TOK :, :].astype(BF16)
-
-
-def project(side, part_of_side, place, rows, own, parts):
-    tiles = SLAB // TILE
-    out = pl.BlockSpec((2 * TOK, TILE), lambda t, place_ref: (0, t))
-    return pl.pallas_call(
-        lambda *refs: project_body(side, part_of_side, *refs),
+    total = nn(every[...], slots[lax.rem(step, 2)])
+    keep_ref[...] = total[:TOK].astype(BF16)
+    send_ref[...] = total[TOK:].astype(BF16)
+
+
+def project(side, place, rows, own, parts):
+    tiles = LONG // TILE
+    out = pl.BlockSpec((TOK, TILE), lambda t, place_ref: (0, t))
+    return pl.pallas_call(
+        lambda *refs: project_body(side, *refs),
         grid_spec=pltpu.PrefetchScalarGridSpec(
             num_scalar_prefetch=1,
             grid=(tiles,),
-            in_specs=[pl.BlockSpec((2 * TOK, HD), lambda t, place_ref: (0, 0))] * 8
-            + [pl.BlockSpec(memory_space=pl.ANY)] * 7,
+            in_specs=[pl.BlockSpec((2 * TOK, HD), lambda t, place_ref: (0, 0))] * 4
+            + [pl.BlockSpec(memory_space=pl.ANY)] * 5,
             out_specs=[out, out],
             scratch_shapes=[
-                pltpu.VMEM((4 * TOK, 4 * HD), BF16),
+                pltpu.VMEM((2 * TOK, 4 * HD), BF16),
                 pltpu.VMEM((2, 4 * HD, TILE), BF16),
-                pltpu.VMEM((4 * TOK, TILE), F32),
-                pltpu.SemaphoreType.DMA((2, 7)),
+                pltpu.SemaphoreType.DMA((2, 5)),
             ],
         ),
-        out_shape=[jax.ShapeDtypeStruct((2 * TOK, SLAB), BF16)] * 2,
-        compiler_params=room(16),
-        cost_estimate=cost(2 * 256 * 2560 * SLAB, 2560 * SLAB * 2),
+        out_shape=[jax.ShapeDtypeStruct((TOK, LONG), BF16)] * 2,
+        compiler_params=room(16),
+        cost_estimate=cost(2 * 256 * 2560 * LONG, 2560 * LONG * 2),
     )(place, *rows, own, *parts)
+
+
+def pair_kernel(place_ref, *refs):
+    rows, got_ref, own, cross, cross_other = refs[:4], refs[4], refs[5], refs[6], refs[7]
+    outs, (every, held, sems) = refs[8:12], refs[12:]
+    copies = []
+    for side, part in enumerate((cross, cross_other)):
+        half = place_ref[0] if side == 0 else 1 - place_ref[0]
+        cols = pl.ds(pl.multiple_of(half * COLS + LONG, 512), WIDTH)
+        copies.append(
+            pltpu.make_async_copy(own.at[:, cols], held.at[side, pl.ds(0, HD)], sems.at[side, 0])
+        )
+        copies.append(pltpu.make_async_copy(part, held.at[side, pl.ds(HD, HD)], sems.at[side, 1]))
+    for copy in copies:
+        copy.start()
+    for d in range(4):
+        every[d * TOK : (d + 1) * TOK, :HD] = rows[d][:TOK, :]
+    every[:, HD:] = got_ref[...]
+    for copy in copies:
+        copy.wait()
+
+    def tile(index, carry):
+        side, t = index // 2, lax.rem(index, 2)
+        cols = pl.ds(pl.multiple_of(t * 512, 512), 512)
+        total = nn(every[...], held[side, :, cols]).astype(BF16)
+        out_cols = pl.ds(pl.multiple_of(index * 512, 512), 512)
+        for d in range(4):
+            outs[d][:, out_cols] = total[d * TOK : (d + 1) * TOK]
+        return carry
+
+    lax.fori_loop(0, 4, tile, 0)
+
+
+def pair_project(place, rows, got, own, cross, cross_other):
+    return pl.pallas_call(
+        pair_kernel,
+        in_specs=[SMEM] + [VMEM] * 5 + [pl.BlockSpec(memory_space=pl.ANY)] * 3,
+        out_specs=[VMEM] * 4,
+        out_shape=[jax.ShapeDtypeStruct((TOK, 2 * WIDTH), BF16)] * 4,
+        scratch_shapes=[
+            pltpu.VMEM((4 * TOK, 2 * HD), BF16),
+            pltpu.VMEM((2, 2 * HD, WIDTH), BF16),
+            pltpu.SemaphoreType.DMA((2, 2)),
+        ],
+        compiler_params=room(16),
+        cost_estimate=cost(2 * 256 * 1280 * 2 * WIDTH, 1280 * 2 * WIDTH * 2),
+        name="pair_project",
+    )(place, *rows, got, own, cross, cross_other)
 
 
 def finish_kernel(place_ref, *refs):
     out_ref = refs[-1]
-    for index in range(WIDE // SLAB):
-        keep, got = refs[index * 2 : index * 2 + 2]
-        side, part_of_side = divmod(index, COLS // SLAB)
-        half = place_ref[0] if side == 0 else 1 - place_ref[0]
-        cols = pl.ds(pl.multiple_of(half * COLS + part_of_side * SLAB, 128), SLAB)
-        for block in range(2):
-            rows = pl.ds(block * TOK, TOK)
-            total = keep[rows, :].astype(F32) + got[rows, :].astype(F32)
-            out_ref[block, :, cols] = total.astype(BF16)
+    for block in range(2):
+        parts = refs[block * 8 : block * 8 + 8]
+        for side in range(2):
+            half = place_ref[0] if side == 0 else 1 - place_ref[0]
+            start = half * COLS
+            total = parts[2 * side][...].astype(F32) + parts[2 * side + 1][...].astype(F32)
+            out_ref[block, :, pl.ds(pl.multiple_of(start, 512), LONG)] = total.astype(BF16)
+            cols = slice(side * WIDTH, (side + 1) * WIDTH)
+            total = parts[4][:, cols].astype(F32)
+            for part in parts[5:8]:
+                total = total + part[:, cols].astype(F32)
+            out_ref[block, :, pl.ds(pl.multiple_of(start + LONG, 512), WIDTH)] = total.astype(BF16)
 
 
 def finish(place, parts):
     return pl.pallas_call(
         finish_kernel,
-        in_specs=[SMEM] + [VMEM] * 8,
+        in_specs=[SMEM] + [VMEM] * 16,
         out_specs=VMEM,
         out_shape=jax.ShapeDtypeStruct((2, TOK, WIDE), BF16),
         compiler_params=room(16),
@@ -442,39 +486,42 @@
     second = to_heads(pack_second(keys, values, rates, queries))
     second_far = shift(second, "core", 1, 2)
 
-    low = lax.dynamic_slice(out_proj, (0, core * COLS), (HALF, COLS))
-    high = lax.dynamic_slice(out_proj, (HALF, core * COLS), (HALF, COLS))
-    before_low = shift(low, "z", 1, 4)
-    after_high = shift(high, "z", 3, 4)
-    before_high = shift(high, "z", 1, 4)
-    after_low = shift(low, "z", 3, 4)
-    far_low = shift(before_low, "z", 1, 4)
-    far_high = shift(after_high, "z", 3, 4)
-    own_side = (before_low, before_high, far_low, far_high, after_low, after_high)
-    other_near = [shift(own_side[i], "core", 1, 2) for i in (0, 1, 4, 5)]
-    other_far = [shift(part, "core", 1, 2) for part in (far_low, far_high)]
-    other_side = (*other_near[:2], *other_far, *other_near[2:])
+    mine = lax.dynamic_slice(out_proj, (0, core * COLS), (HD, LONG))
+    slab = lax.dynamic_slice(out_proj, (0, core * COLS + LONG), (HD, WIDTH))
+    cross = shift(slab, "yl", 1, 2)
+    cross_other = shift(cross, "core", 1, 2)
+    before = shift(mine, "z", 1, 4)
+    after = shift(mine, "z", 3, 4)
+    far_low = shift(before[:HALF], "z", 1, 4)
+    far_high = shift(after[HALF:], "z", 3, 4)
+    own_side = (before, far_low, far_high, after)
+    other_before, other_after = (shift(part, "core", 1, 2) for part in (before, after))
+    other_low, other_high = (shift(part, "core", 1, 2) for part in (far_low, far_high))
+    other_side = (other_before, other_low, other_high, other_after)
 
     halves = start_half(place, gate_fast, up_fast, down_fast)
     master, row_norm, col_norm = start_full(gate_fast, up_fast, down_fast)
 
     def spread(block, weights):
-        rows = apply_weights(block, place, weights, gain, second)
+        *rows, trade = apply_weights(block, place, weights, gain, second)
+        got = shift(trade, "yl", 1, 2)
         back = {d: shift(rows[d], "z", 4 - d, 4) for d in (2, 1, 3)}
-        return [rows[0], back[3], back[2], back[1]]
+        mine, *others = pair_project(place, rows, got, out_proj, cross, cross_other)
+        returned = {d: shift(others[d - 1], "z", 4 - d, 4) for d in (2, 1, 3)}
+        ordered = [rows[0], back[3], back[2], back[1]]
+        parts = []
+        for side, gathered in enumerate((own_side, other_side)):
+            keep, send = project(side, place, ordered, out_proj, gathered)
+            parts += [keep, shift(send, "yl", 1, 2)]
+        return parts + [mine] + [returned[d] for d in (1, 2, 3)]
 
     total = sum_over_ctx(grads(place, halves, first, first_far))
     weights = renorm(place, [master], row_norm, col_norm, total)
     parts = grads(place, weights, second, second_far)
     total = sum_over_ctx(parts)
-    rows = spread(0, weights)
+    mixed = spread(0, weights)
     weights = renorm(place, weights, row_norm, col_norm, total)
-    rows += spread(1, weights)
-    mixed = []
-    for side, gathered in enumerate((own_side, other_side)):
-        for part_of_side in range(COLS // SLAB):
-            keep, send = project(side, part_of_side, place, rows, out_proj, gathered)
-            mixed += [keep, shift(send, "yl", 1, 2)]
+    mixed += spread(1, weights)
     return finish(place, mixed)
 
 

time: 320 us -> 262 us (0.82)
  waiting for transfers between devices: 164 us -> 104 us
  local copies, waits for them, and re-layouts: 11.8 us -> 16.9 us
  starting transfers between devices: 79.4 us -> 75.4 us
    ppermute x46 -> x52, waiting for transfers between devices: 120 us -> 65.7 us  [shift(): lax.ppermute(array, axis, [(i, (i + by) % size) for i in range(size)])]
    all_to_all x2, waiting for transfers between devices: 43.5 us -> 38.1 us  [to_heads(): return lax.all_to_all(array, ('z', 'yl'), 0, 0, tiled=True)]
    ppermute x46 -> x52, starting transfers between devices: 68.8 us -> 64.2 us  [shift(): lax.ppermute(array, axis, [(i, (i + by) % size) for i in range(size)])]
    unnamed x22 -> x30, local copies, waits for them, and re-layouts: 9.66 us -> 11.1 us
    pallas_call x5 -> x7, Pallas kernels: 23.8 us -> 23.2 us  [the longest x4 14.7 us: project(): pl.pallas_call(lambda *refs: project_body(side, *refs), grid_spec=pltpu.P...]
  transfers between devices with their start and end apart: 48 -> 54, of which waited for: 19 -> 21; matrix products, arithmetic and copies ran while one was open for 1% -> 2% of each run, Pallas kernels for 18% -> 23%
where the time goes in v1:
time: 262 us; the launch traced here: 261 us
  waiting for transfers between devices  104 us (40%)
  starting transfers between devices  75.4 us (29%)
  Pallas kernels  64 us (24%)
  local copies, waits for them, and re-layouts  16.9 us (6%)
    ppermute x52, waiting for transfers between devices, shift(): lax.ppermute(array, axis, [(i, (i + by) % size) for i in range(size)])  65.7 us
    ppermute x52, starting transfers between devices, shift(): lax.ppermute(array, axis, [(i, (i + by) % size) for i in range(size)])  64.2 us
    all_to_all x2, waiting for transfers between devices, to_heads(): return lax.all_to_all(array, ('z', 'yl'), 0, 0, tiled=True)  38.1 us
    pallas_call x2, Pallas kernels, grads(): pl.pallas_call(grads_kernel, grid=(1,), in_specs=[SMEM] + [held] * 2 + [p...  16 us
    pallas_call x4, Pallas kernels, project(): pl.pallas_call(lambda *refs: project_body(side, *refs), grid_spec=pltpu.P...  14.7 us
    all_to_all x2, starting transfers between devices, to_heads(): return lax.all_to_all(array, ('z', 'yl'), 0, 0, tiled=True)  11.3 us
    unnamed x30, local copies, waits for them, and re-layouts  11.1 us
    pallas_call x2, Pallas kernels, apply_weights(): pl.pallas_call(apply_kernel, grid=(1,), in_specs=[SMEM, pl.BlockSpec((3,...  9.89 us
  transfers between devices with their start and end apart: 54, of which 21 were waited for; matrix products, arithmetic and copies ran while one was open for 2% of the time, Pallas kernels for 23%

profile of v1, /device:TPU:1, one launch (start us, length us, event | category | flops | bytes accessed | tf_op | source)
XLA Modules:
  0.0 261.0 jit_solution(3599492982820474293)
XLA Ops:
  0.0 2.5 pack_first.1
  2.5 6.9 %all-to-all-start = ((bf16[8,128,640]{2,1,0:T(8,128)(2,1)}), bf16[8,128,640]{2,1,0:T(8,128)(2,1)}, u32[]{:S(2)}, u32[]{:S(2)}) async-start(bf16[8,128,640]{2,1,0:T(8,128)(2,1)} %pack_first.1), calls=%async_computation | async-start | bytes 2621440 | tf_op jit(solution)/shard_map/all_to_all | solution.py:49
  9.4 3.5 %pack_second.1 = bf16[8,256,640]{2,1,0:T(8,128)(2,1)} custom-call(bf16[2,64,5120]{2,1,0:T(8,128)(2,1)} %key_ref.3, bf16[2,64,5120]{2,1,0:T(8,128)(2,1)} %value_ref.3, bf16[2,8,64]{2,1,0:T(8,128)(2,1)} %bitcast.8, bf16[2,64,5120]{2,1,0:T(8,128)(2,1)} %query_ref.1), custom_call_target="tpu_custom_call" | custom-call | flops 1048576 | bytes 5242880 | tf_op jit(solution)/shard_map/pack_second/pallas_call | solution.py:111
  12.9 14.3 %all-to-all-done.near_ref = bf16[8,128,640]{2,1,0:T(8,128)(2,1)} async-done(((bf16[8,128,640]{2,1,0:T(8,128)(2,1)}), bf16[8,128,640]{2,1,0:T(8,128)(2,1)}, u32[]{:S(2)}, u32[]{:S(2)}) %all-to-all-start) | async-done | bytes 1310752 | tf_op jit(solution)/shard_map/all_to_all | solution.py:49
  27.2 4.4 %all-to-all-start.1 = ((bf16[8,256,640]{2,1,0:T(8,128)(2,1)}), bf16[8,256,640]{2,1,0:T(8,128)(2,1)}, u32[]{:S(2)}, u32[]{:S(2)}) async-start(bf16[8,256,640]{2,1,0:T(8,128)(2,1)} %pack_second.1), calls=%async_computation.1 | async-start | bytes 5242880 | tf_op jit(solution)/shard_map/all_to_all | solution.py:49
  31.6 1.9 collective-permute-start
  33.6 1.4 copy-done.4
  35.0 1.6 start_half.1
  38.7 23.8 %all-to-all-done.1.query_ref.near_ref = bf16[8,256,640]{2,1,0:T(8,128)(2,1)} async-done(((bf16[8,256,640]{2,1,0:T(8,128)(2,1)}), bf16[8,256,640]{2,1,0:T(8,128)(2,1)}, u32[]{:S(2)}, u32[]{:S(2)}) %all-to-all-start.1) | async-done | bytes 2621472 | tf_op jit(solution)/shard_map/all_to_all | solution.py:49
  62.5 2.7 %collective-permute-start.31 = (bf16[8,256,640]{2,1,0:T(8,128)(2,1)}, bf16[8,256,640]{2,1,0:T(8,128)(2,1)}, u32[]{:S(2)}, u32[]{:S(2)}) collective-permute-start(bf16[8,256,640]{2,1,0:T(8,128)(2,1)} %all-to-all-done.1.query_ref.near_ref), channel_id=1, source_target_pairs={{0,8},{8,0},{1,9},{9,1},{2,10},{10,2},{3,11},{11,3},{4,12},{12,4},... | collective-permute-start | bytes 7864328 | tf_op jit(solution)/shard_map/ppermute | solution.py:45
  65.2 1.3 copy-done.9
  66.5 1.3 copy-done.11
  67.8 8.0 %grads.2 = (f32[240,640]{1,0:T(8,128)S(1)}, bf16[240,640]{1,0:T(8,128)(2,1)S(1)}, bf16[240,640]{1,0:T(8,128)(2,1)S(1)}, bf16[240,640]{1,0:T(8,128)(2,1)S(1)}) custom-call(s32[4]{0:T(128)S(1)} %pad_add_fusion.place_ref.refs_0_, bf16[3,320,640]{2,1,0:T(8,128)(2,1)S(1)} %copy-done.9, bf16[3,320,640]{2,1,0:T(8,128)(2,1)S(1)} %copy-done.11, ...), custom_call_target="tpu_custom_call" | custom-call | flops 2516582400 | bytes 8388608 | tf_op jit(solution)/shard_map/grads/pallas_call | solution.py:263
  77.0 1.5 collective-permute-start.2
  78.5 1.5 collective-permute-start.3
  80.0 5.8 %collective-permute-done.1 = bf16[240,640]{1,0:T(8,128)(2,1)S(1)} collective-permute-done((bf16[240,640]{1,0:T(8,128)(2,1)S(1)}, bf16[240,640]{1,0:T(8,128)(2,1)S(1)}, u32[]{:S(2)}, u32[]{:S(2)}) %collective-permute-start.1) | collective-permute-done | bytes 307232 | tf_op jit(solution)/shard_map/ppermute | solution.py:45
  85.9 7.6 %collective-permute-done.3 = bf16[240,640]{1,0:T(8,128)(2,1)S(1)} collective-permute-done((bf16[240,640]{1,0:T(8,128)(2,1)S(1)}, bf16[240,640]{1,0:T(8,128)(2,1)S(1)}, u32[]{:S(2)}, u32[]{:S(2)}) %collective-permute-start.3) | collective-permute-done | bytes 307232 | tf_op jit(solution)/shard_map/ppermute | solution.py:45
  93.6 2.7 %collective-permute-start.4 = (bf16[240,640]{1,0:T(8,128)(2,1)S(1)}, bf16[240,640]{1,0:T(8,128)(2,1)S(1)}, u32[]{:S(2)}, u32[]{:S(2)}) collective-permute-start(bf16[240,640]{1,0:T(8,128)(2,1)S(1)} %convert_element_type.39), channel_id=1, source_target_pairs={{0,16},{16,0},{1,17},{17,1},{2,18},{18,2},{3,19},{19,3},{4,20},{20... | collective-permute-start | bytes 921608 | tf_op jit(solution)/shard_map/ppermute | solution.py:45
  96.3 3.0 %constant_dynamic-slice_fusion.1 = bf16[640,1536]{1,0:T(8,128)(2,1)} fusion(bf16[640,5120]{1,0:T(8,128)(2,1)} %refs_5_.11, s32[]{:T(128)S(6)} %select_n.6), kind=kLoop, calls=%fused_computation.6 | loop fusion | bytes 3932164 | tf_op jit(solution)/shard_map/dynamic_slice | solution.py:489
  99.3 2.7 %collective-permute-start.17 = (bf16[640,1536]{1,0:T(8,128)(2,1)}, bf16[640,1536]{1,0:T(8,128)(2,1)}, u32[]{:S(2)}, u32[]{:S(2)}) collective-permute-start(bf16[640,1536]{1,0:T(8,128)(2,1)} %constant_dynamic-slice_fusion.1), channel_id=1, source_target_pairs={{0,6},{2,0},{4,2},{6,4},{1,7},{3,1},{5,3},{7,5},{8,14},{10,8},{12,... | collective-permute-start | bytes 5898248 | tf_op jit(solution)/shard_map/ppermute | solution.py:45
  103.8 2.2 collective-permute-start.7
  106.0 5.9 %collective-permute-done.6.refs_6_ = bf16[240,640]{1,0:T(8,128)(2,1)S(1)} collective-permute-done((bf16[240,640]{1,0:T(8,128)(2,1)S(1)}, bf16[240,640]{1,0:T(8,128)(2,1)S(1)}, u32[]{:S(2)}, u32[]{:S(2)}) %collective-permute-start.6) | collective-permute-done | bytes 307232 | tf_op jit(solution)/shard_map/ppermute | solution.py:45
  112.1 5.6 %collective-permute-done.7.refs_7_ = bf16[240,640]{1,0:T(8,128)(2,1)S(1)} collective-permute-done((bf16[240,640]{1,0:T(8,128)(2,1)S(1)}, bf16[240,640]{1,0:T(8,128)(2,1)S(1)}, u32[]{:S(2)}, u32[]{:S(2)}) %collective-permute-start.7) | collective-permute-done | bytes 307232 | tf_op jit(solution)/shard_map/ppermute | solution.py:45
  117.7 1.8 collective-permute-start.8
  119.4 3.6 %collective-permute-start.10 = (bf16[240,640]{1,0:T(8,128)(2,1)S(1)}, bf16[240,640]{1,0:T(8,128)(2,1)S(1)}, u32[]{:S(2)}, u32[]{:S(2)}) collective-permute-start(bf16[240,640]{1,0:T(8,128)(2,1)S(1)} %collective-permute-done.6.refs_6_), channel_id=1, source_target_pairs={{0,8},{8,0},{1,9},{9,1},{2,10},{10,2},{3,11},{11,3},{4,12},{12,4},... | collective-permute-start | bytes 921608 | tf_op jit(solution)/shard_map/ppermute | solution.py:45
  125.4 1.4 copy-done.1
  126.8 1.4 copy-done.3
  128.2 1.4 copy-done.5
  129.7 1.3 start_full.1
  131.0 1.5 constant_dynamic-slice_fusion
  133.3 3.0 %renorm.2 = (bf16[3,640,640]{2,1,0:T(8,128)(2,1)S(1)}, bf16[3,640,640]{2,1,0:T(8,128)(2,1)S(1)}) custom-call(s32[4]{0:T(128)S(1)} %pad_add_fusion.place_ref.refs_0_, f32[3,640,640]{2,1,0:T(8,128)S(1)} %get-tuple-element.48.refs_1_, f32[2,640,1]{2,1,0:T(8,128)S(1)} %get-tuple-element.49.refs_2_.refs_3_, f32[1,640]{1,0:T(1,128)S(1)} %get-tuple-element.50.refs_3_.refs_4_, ...), custom_call_target="tpu_custom_call" | custom-call | flops 16777216 | bytes 12288000 | tf_op jit(solution)/shard_map/renorm/pallas_call | solution.py:208
  136.3 8.0 %grads.3 = (f32[240,640]{1,0:T(8,128)S(1)}, bf16[240,640]{1,0:T(8,128)(2,1)S(1)}, bf16[240,640]{1,0:T(8,128)(2,1)S(1)}, bf16[240,640]{1,0:T(8,128)(2,1)S(1)}) custom-call(s32[4]{0:T(128)S(1)} %pad_add_fusion.place_ref.refs_0_, bf16[3,640,640]{2,1,0:T(8,128)(2,1)S(1)} %get-tuple-element.57.high_ref.refs_1_, ...), custom_call_target="tpu_custom_call" | custom-call | flops 2516582400 | bytes 8388608 | tf_op jit(solution)/shard_map/grads/pallas_call | solution.py:263
  147.2 2.5 collective-permute-start.18
  149.6 1.6 collective-permute-start.33
  151.2 2.8 %collective-permute-done.32 = bf16[240,640]{1,0:T(8,128)(2,1)S(1)} collective-permute-done((bf16[240,640]{1,0:T(8,128)(2,1)S(1)}, bf16[240,640]{1,0:T(8,128)(2,1)S(1)}, u32[]{:S(2)}, u32[]{:S(2)}) %collective-permute-start.32) | collective-permute-done | bytes 307232 | tf_op jit(solution)/shard_map/ppermute | solution.py:45
  154.5 2.7 %collective-permute-done.33 = bf16[240,640]{1,0:T(8,128)(2,1)S(1)} collective-permute-done((bf16[240,640]{1,0:T(8,128)(2,1)S(1)}, bf16[240,640]{1,0:T(8,128)(2,1)S(1)}, u32[]{:S(2)}, u32[]{:S(2)}) %collective-permute-start.33) | collective-permute-done | bytes 307232 | tf_op jit(solution)/shard_map/ppermute | solution.py:45
  157.2 5.8 %collective-permute-done.34 = bf16[240,640]{1,0:T(8,128)(2,1)S(1)} collective-permute-done((bf16[240,640]{1,0:T(8,128)(2,1)S(1)}, bf16[240,640]{1,0:T(8,128)(2,1)S(1)}, u32[]{:S(2)}, u32[]{:S(2)}) %collective-permute-start.34) | collective-permute-done | bytes 307232 | tf_op jit(solution)/shard_map/ppermute | solution.py:45
  163.2 2.7 %collective-permute-start.35 = (bf16[240,640]{1,0:T(8,128)(2,1)S(1)}, bf16[240,640]{1,0:T(8,128)(2,1)S(1)}, u32[]{:S(2)}, u32[]{:S(2)}) collective-permute-start(bf16[240,640]{1,0:T(8,128)(2,1)S(1)} %convert_element_type.45), channel_id=1, source_target_pairs={{0,16},{16,0},{1,17},{17,1},{2,18},{18,2},{3,19},{19,3},{4,20},{20... | collective-permute-start | bytes 921608 | tf_op jit(solution)/shard_map/ppermute | solution.py:45
  165.9 2.6 %collective-permute-start.20 = (bf16[640,1536]{1,0:T(8,128)(2,1)S(1)}, bf16[640,1536]{1,0:T(8,128)(2,1)S(1)}, u32[]{:S(2)}, u32[]{:S(2)}) collective-permute-start(bf16[640,1536]{1,0:T(8,128)(2,1)S(1)} %collective-permute-done.15.refs_6_), channel_id=1, source_target_pairs={{0,8},{8,0},{1,9},{9,1},{2,10},{10,2},{3,11},{11,3},{4,12},{12,4},... | collective-permute-start | bytes 5898248 | tf_op jit(solution)/shard_map/ppermute | solution.py:45
  168.6 5.0 %apply_weights.2 = (bf16[128,640]{1,0:T(8,128)(2,1)S(1)}, bf16[128,640]{1,0:T(8,128)(2,1)S(1)}, bf16[128,640]{1,0:T(8,128)(2,1)S(1)}, bf16[128,640]{1,0:T(8,128)(2,1)S(1)}, bf16[256,640]{1,0:T(8,128)(2,1)S(1)}) custom-call(s32[4]{0:T(128)S(1)} %pad_add_fusion.place_ref.refs_0_, bf16[3,640,640]{2,1,0:T(8,128)(2,1)S(1)} %get-tuple-element.57.high_ref.refs_1_, ...), custom_call_target="tpu_custom_call" | custom-call | flops 2097152000 | bytes 5242880 | tf_op jit(solution)/shard_map/apply_weights/pallas_call | solution.py:318
  174.0 1.8 collective-permute-start.13
  176.6 4.6 %collective-permute-done.12.refs_2_ = bf16[128,640]{1,0:T(8,128)(2,1)S(1)} collective-permute-done((bf16[128,640]{1,0:T(8,128)(2,1)S(1)}, bf16[128,640]{1,0:T(8,128)(2,1)S(1)}, u32[]{:S(2)}, u32[]{:S(2)}) %collective-permute-start.12) | collective-permute-done | bytes 163872 | tf_op jit(solution)/shard_map/ppermute | solution.py:45
  181.2 4.5 %collective-permute-start.36 = (bf16[240,640]{1,0:T(8,128)(2,1)S(1)}, bf16[240,640]{1,0:T(8,128)(2,1)S(1)}, u32[]{:S(2)}, u32[]{:S(2)}) collective-permute-start(bf16[240,640]{1,0:T(8,128)(2,1)S(1)} %add_convert_fusion.refs_5_), channel_id=1, source_target_pairs={{0,32},{32,64},{64,96},{96,0},{1,33},{33,65},{65,97},{97,1},{2,34}... | collective-permute-start | bytes 921608 | tf_op jit(solution)/shard_map/ppermute | solution.py:45
  185.7 2.8 %collective-permute-start.37 = (bf16[240,640]{1,0:T(8,128)(2,1)S(1)}, bf16[240,640]{1,0:T(8,128)(2,1)S(1)}, u32[]{:S(2)}, u32[]{:S(2)}) collective-permute-start(bf16[240,640]{1,0:T(8,128)(2,1)S(1)} %add_convert_fusion.refs_5_), channel_id=1, source_target_pairs={{0,64},{32,96},{64,0},{96,32},{1,65},{33,97},{65,1},{97,33},{2,66}... | collective-permute-start | bytes 921608 | tf_op jit(solution)/shard_map/ppermute | solution.py:45
  188.5 5.3 %collective-permute-done.36.refs_6_ = bf16[240,640]{1,0:T(8,128)(2,1)S(1)} collective-permute-done((bf16[240,640]{1,0:T(8,128)(2,1)S(1)}, bf16[240,640]{1,0:T(8,128)(2,1)S(1)}, u32[]{:S(2)}, u32[]{:S(2)}) %collective-permute-start.36) | collective-permute-done | bytes 307232 | tf_op jit(solution)/shard_map/ppermute | solution.py:45
  193.8 2.3 collective-permute-start.39
  196.0 5.2 %collective-permute-done.37.refs_7_ = bf16[240,640]{1,0:T(8,128)(2,1)S(1)} collective-permute-done((bf16[240,640]{1,0:T(8,128)(2,1)S(1)}, bf16[240,640]{1,0:T(8,128)(2,1)S(1)}, u32[]{:S(2)}, u32[]{:S(2)}) %collective-permute-start.37) | collective-permute-done | bytes 307232 | tf_op jit(solution)/shard_map/ppermute | solution.py:45
  201.3 2.1 collective-permute-start.40
  204.9 1.9 collective-permute-done.41.refs_11_
  207.7 4.3 %shard_map.91 = (bf16[64,1536]{1,0:T(8,128)(2,1)S(1)}, bf16[64,1536]{1,0:T(8,128)(2,1)S(1)}) custom-call(s32[4]{0:T(128)S(1)} %pad_add_fusion.place_ref.refs_0_, bf16[128,640]{1,0:T(8,128)(2,1)S(1)} %get-tuple-element.59.refs_1_.refs_0_, bf16[128,640]{1,0:T(8,128)(2,1)S(1)} %collective-permute-done.12.refs_2_, ...), custom_call_target="tpu_custom_call" | custom-call | flops 2013265920 | bytes 7864320 | tf_op jit(solution)/shard_map/pallas_call | solution.py:381
  212.0 3.0 %renorm.3 = (bf16[3,640,640]{2,1,0:T(8,128)(2,1)S(1)}, bf16[3,640,640]{2,1,0:T(8,128)(2,1)S(1)}) custom-call(s32[4]{0:T(128)S(1)} %pad_add_fusion.place_ref.refs_0_, bf16[3,640,640]{2,1,0:T(8,128)(2,1)S(1)} %get-tuple-element.57.high_ref.refs_1_, bf16[3,640,640]{2,1,0:T(8,128)(2,1)S(1)} %get-tuple-element.58.low_ref.refs_2_, ...), custom_call_target="tpu_custom_call" | custom-call | flops 16777216 | bytes 12288000 | tf_op jit(solution)/shard_map/renorm/pallas_call | solution.py:208
  215.3 4.9 %apply_weights.3 = (bf16[128,640]{1,0:T(8,128)(2,1)S(1)}, bf16[128,640]{1,0:T(8,128)(2,1)S(1)}, bf16[128,640]{1,0:T(8,128)(2,1)S(1)}, bf16[128,640]{1,0:T(8,128)(2,1)S(1)}, bf16[256,640]{1,0:T(8,128)(2,1)S(1)}) custom-call(s32[4]{0:T(128)S(1)} %pad_add_fusion.place_ref.refs_0_, bf16[3,640,640]{2,1,0:T(8,128)(2,1)S(1)} %get-tuple-element.76.high_ref, ...), custom_call_target="tpu_custom_call" | custom-call | flops 2097152000 | bytes 5242880 | tf_op jit(solution)/shard_map/apply_weights/pallas_call | solution.py:318
  221.8 2.4 collective-permute-start.45
  224.3 3.1 %shard_map.92 = (bf16[64,1536]{1,0:T(8,128)(2,1)S(1)}, bf16[64,1536]{1,0:T(8,128)(2,1)S(1)}) custom-call(s32[4]{0:T(128)S(1)} %pad_add_fusion.place_ref.refs_0_, bf16[128,640]{1,0:T(8,128)(2,1)S(1)} %get-tuple-element.59.refs_1_.refs_0_, bf16[128,640]{1,0:T(8,128)(2,1)S(1)} %collective-permute-done.12.refs_2_, ...), custom_call_target="tpu_custom_call" | custom-call | flops 2013265920 | bytes 7864320 | tf_op jit(solution)/shard_map/pallas_call | solution.py:381
  227.7 3.2 %pair_project.2 = (bf16[64,2048]{1,0:T(8,128)(2,1)S(1)}, bf16[64,2048]{1,0:T(8,128)(2,1)S(1)}, bf16[64,2048]{1,0:T(8,128)(2,1)S(1)}, bf16[64,2048]{1,0:T(8,128)(2,1)S(1)}) custom-call(s32[4]{0:T(128)S(1)} %pad_add_fusion.place_ref.refs_0_, bf16[128,640]{1,0:T(8,128)(2,1)S(1)} %get-tuple-element.59.refs_1_.refs_0_, ...), custom_call_target="tpu_custom_call" | custom-call | flops 1342177280 | bytes 5242880 | tf_op jit(solution)/shard_map/pair_project/pallas_call | solution.py:433
  232.8 1.8 collective-permute-start.29
  234.6 3.1 %shard_map.94 = (bf16[64,1536]{1,0:T(8,128)(2,1)S(1)}, bf16[64,1536]{1,0:T(8,128)(2,1)S(1)}) custom-call(s32[4]{0:T(128)S(1)} %pad_add_fusion.place_ref.refs_0_, bf16[128,640]{1,0:T(8,128)(2,1)S(1)} %get-tuple-element.78.refs_1_.refs_0_, bf16[128,640]{1,0:T(8,128)(2,1)S(1)} %collective-permute-done.43.refs_2_, ...), custom_call_target="tpu_custom_call" | custom-call | flops 2013265920 | bytes 7864320 | tf_op jit(solution)/shard_map/pallas_call | solution.py:381
  238.6 3.2 %pair_project.3 = (bf16[64,2048]{1,0:T(8,128)(2,1)S(1)}, bf16[64,2048]{1,0:T(8,128)(2,1)S(1)}, bf16[64,2048]{1,0:T(8,128)(2,1)S(1)}, bf16[64,2048]{1,0:T(8,128)(2,1)S(1)}) custom-call(s32[4]{0:T(128)S(1)} %pad_add_fusion.place_ref.refs_0_, bf16[128,640]{1,0:T(8,128)(2,1)S(1)} %get-tuple-element.78.refs_1_.refs_0_, ...), custom_call_target="tpu_custom_call" | custom-call | flops 1342177280 | bytes 5242880 | tf_op jit(solution)/shard_map/pair_project/pallas_call | solution.py:433
  241.9 1.9 collective-permute-start.49
  244.6 4.3 %shard_map.93 = (bf16[64,1536]{1,0:T(8,128)(2,1)S(1)}, bf16[64,1536]{1,0:T(8,128)(2,1)S(1)}) custom-call(s32[4]{0:T(128)S(1)} %pad_add_fusion.place_ref.refs_0_, bf16[128,640]{1,0:T(8,128)(2,1)S(1)} %get-tuple-element.78.refs_1_.refs_0_, bf16[128,640]{1,0:T(8,128)(2,1)S(1)} %collective-permute-done.43.refs_2_, ...), custom_call_target="tpu_custom_call" | custom-call | flops 2013265920 | bytes 7864320 | tf_op jit(solution)/shard_map/pallas_call | solution.py:381
  250.4 3.3 %collective-permute-done.47.refs_11_ = bf16[64,1536]{1,0:T(8,128)(2,1)S(1)} collective-permute-done((bf16[64,1536]{1,0:T(8,128)(2,1)S(1)}, bf16[64,1536]{1,0:T(8,128)(2,1)S(1)}, u32[]{:S(2)}, u32[]{:S(2)}) %collective-permute-start.47) | collective-permute-done | bytes 196640 | tf_op jit(solution)/shard_map/ppermute | solution.py:45
  253.8 2.4 collective-permute-done.46.refs_9_
  256.2 2.8 %collective-permute-done.51.refs_15_ = bf16[64,2048]{1,0:T(8,128)(2,1)S(1)} collective-permute-done((bf16[64,2048]{1,0:T(8,128)(2,1)S(1)}, bf16[64,2048]{1,0:T(8,128)(2,1)S(1)}, u32[]{:S(2)}, u32[]{:S(2)}) %collective-permute-start.51) | collective-permute-done | bytes 262176 | tf_op jit(solution)/shard_map/ppermute | solution.py:45
  259.0 2.0 finish.1
  (104 shorter events, 23.4 us)
Async XLA Ops:
  2.5 24.7 %all-to-all-start = ((bf16[8,128,640]{2,1,0:T(8,128)(2,1)}), bf16[8,128,640]{2,1,0:T(8,128)(2,1)}, u32[]{:S(2)}, u32[]{:S(2)}) async-start(bf16[8,128,640]{2,1,0:T(8,128)(2,1)} %pack_first.1), calls=%async_computation | async-start | bytes 2621440 | tf_op jit(solution)/shard_map/all_to_all | solution.py:49
  12.9 20.7 %copy-start = (f32[1,640,640]{2,1,0:T(8,128)S(1)}, f32[1,640,640]{2,1,0:T(8,128)}, u32[]{:S(2)}) copy-start(f32[1,640,640]{2,1,0:T(8,128)} %gate_ref.3) | copy-start | bytes 4915204
  12.9 20.7 %copy-start.2 = (f32[1,640,640]{2,1,0:T(8,128)S(1)}, f32[1,640,640]{2,1,0:T(8,128)}, u32[]{:S(2)}) copy-start(f32[1,640,640]{2,1,0:T(8,128)} %up_ref.3) | copy-start | bytes 4915204
  27.2 35.3 %all-to-all-start.1 = ((bf16[8,256,640]{2,1,0:T(8,128)(2,1)}), bf16[8,256,640]{2,1,0:T(8,128)(2,1)}, u32[]{:S(2)}, u32[]{:S(2)}) async-start(bf16[8,256,640]{2,1,0:T(8,128)(2,1)} %pack_second.1), calls=%async_computation.1 | async-start | bytes 5242880 | tf_op jit(solution)/shard_map/all_to_all | solution.py:49
  31.6 33.6 %collective-permute-start = (bf16[8,128,640]{2,1,0:T(8,128)(2,1)}, bf16[8,128,640]{2,1,0:T(8,128)(2,1)}, u32[]{:S(2)}, u32[]{:S(2)}) collective-permute-start(bf16[8,128,640]{2,1,0:T(8,128)(2,1)} %all-to-all-done.near_ref), channel_id=1, source_target_pairs={{0,8},{8,0},{1,9},{9,1},{2,10},{10,2},{3,11},{11,3},{4,12},{12,4},... | collective-permute-start | bytes 3932168 | tf_op jit(solution)/shard_map/ppermute | solution.py:45
  33.6 1.4 copy-start.4
  62.5 73.7 %collective-permute-start.31 = (bf16[8,256,640]{2,1,0:T(8,128)(2,1)}, bf16[8,256,640]{2,1,0:T(8,128)(2,1)}, u32[]{:S(2)}, u32[]{:S(2)}) collective-permute-start(bf16[8,256,640]{2,1,0:T(8,128)(2,1)} %all-to-all-done.1.query_ref.near_ref), channel_id=1, source_target_pairs={{0,8},{8,0},{1,9},{9,1},{2,10},{10,2},{3,11},{11,3},{4,12},{12,4},... | collective-permute-start | bytes 7864328 | tf_op jit(solution)/shard_map/ppermute | solution.py:45
  75.8 10.1 %collective-permute-start.1 = (bf16[240,640]{1,0:T(8,128)(2,1)S(1)}, bf16[240,640]{1,0:T(8,128)(2,1)S(1)}, u32[]{:S(2)}, u32[]{:S(2)}) collective-permute-start(bf16[240,640]{1,0:T(8,128)(2,1)S(1)} %get-tuple-element.54), channel_id=1, source_target_pairs={{0,32},{32,64},{64,96},{96,0},{1,33},{33,65},{65,97},{97,1},{2,34}... | collective-permute-start | bytes 921608 | tf_op jit(solution)/shard_map/ppermute | solution.py:45
  77.0 8.8 %collective-permute-start.2 = (bf16[240,640]{1,0:T(8,128)(2,1)S(1)}, bf16[240,640]{1,0:T(8,128)(2,1)S(1)}, u32[]{:S(2)}, u32[]{:S(2)}) collective-permute-start(bf16[240,640]{1,0:T(8,128)(2,1)S(1)} %get-tuple-element.55), channel_id=1, source_target_pairs={{0,96},{32,0},{64,32},{96,64},{1,97},{33,1},{65,33},{97,65},{2,98}... | collective-permute-start | bytes 921608 | tf_op jit(solution)/shard_map/ppermute | solution.py:45
  78.5 14.9 %collective-permute-start.3 = (bf16[240,640]{1,0:T(8,128)(2,1)S(1)}, bf16[240,640]{1,0:T(8,128)(2,1)S(1)}, u32[]{:S(2)}, u32[]{:S(2)}) collective-permute-start(bf16[240,640]{1,0:T(8,128)(2,1)S(1)} %get-tuple-element.56), channel_id=1, source_target_pairs={{0,64},{32,96},{64,0},{96,32},{1,65},{33,97},{65,1},{97,33},{2,66}... | collective-permute-start | bytes 921608 | tf_op jit(solution)/shard_map/ppermute | solution.py:45
  93.6 9.6 %collective-permute-start.4 = (bf16[240,640]{1,0:T(8,128)(2,1)S(1)}, bf16[240,640]{1,0:T(8,128)(2,1)S(1)}, u32[]{:S(2)}, u32[]{:S(2)}) collective-permute-start(bf16[240,640]{1,0:T(8,128)(2,1)S(1)} %convert_element_type.39), channel_id=1, source_target_pairs={{0,16},{16,0},{1,17},{17,1},{2,18},{18,2},{3,19},{19,3},{4,20},{20... | collective-permute-start | bytes 921608 | tf_op jit(solution)/shard_map/ppermute | solution.py:45
  99.3 46.1 %collective-permute-start.15 = (bf16[640,1536]{1,0:T(8,128)(2,1)}, bf16[640,1536]{1,0:T(8,128)(2,1)S(1)}, u32[]{:S(2)}, u32[]{:S(2)}) collective-permute-start(bf16[640,1536]{1,0:T(8,128)(2,1)} %constant_dynamic-slice_fusion.1), channel_id=1, source_target_pairs={{0,2},{2,4},{4,6},{6,0},{1,3},{3,5},{5,7},{7,1},{8,10},{10,12},{12... | collective-permute-start | bytes 5898248 | tf_op jit(solution)/shard_map/ppermute | solution.py:45
  99.3 46.6 %collective-permute-start.17 = (bf16[640,1536]{1,0:T(8,128)(2,1)}, bf16[640,1536]{1,0:T(8,128)(2,1)}, u32[]{:S(2)}, u32[]{:S(2)}) collective-permute-start(bf16[640,1536]{1,0:T(8,128)(2,1)} %constant_dynamic-slice_fusion.1), channel_id=1, source_target_pairs={{0,6},{2,0},{4,2},{6,4},{1,7},{3,1},{5,3},{7,5},{8,14},{10,8},{12,... | collective-permute-start | bytes 5898248 | tf_op jit(solution)/shard_map/ppermute | solution.py:45
  103.3 8.7 %collective-permute-start.6 = (bf16[240,640]{1,0:T(8,128)(2,1)S(1)}, bf16[240,640]{1,0:T(8,128)(2,1)S(1)}, u32[]{:S(2)}, u32[]{:S(2)}) collective-permute-start(bf16[240,640]{1,0:T(8,128)(2,1)S(1)} %add_convert_fusion.1.refs_4_), channel_id=1, source_target_pairs={{0,64},{32,96},{64,0},{96,32},{1,65},{33,97},{65,1},{97,33},{2,66}... | collective-permute-start | bytes 921608 | tf_op jit(solution)/shard_map/ppermute | solution.py:45
  103.8 13.8 %collective-permute-start.7 = (bf16[240,640]{1,0:T(8,128)(2,1)S(1)}, bf16[240,640]{1,0:T(8,128)(2,1)S(1)}, u32[]{:S(2)}, u32[]{:S(2)}) collective-permute-start(bf16[240,640]{1,0:T(8,128)(2,1)S(1)} %add_convert_fusion.1.refs_4_), channel_id=1, source_target_pairs={{0,96},{32,0},{64,32},{96,64},{1,97},{33,1},{65,33},{97,65},{2,98}... | collective-permute-start | bytes 921608 | tf_op jit(solution)/shard_map/ppermute | solution.py:45
  112.0 7.5 %collective-permute-start.5 = (bf16[240,640]{1,0:T(8,128)(2,1)S(1)}, bf16[240,640]{1,0:T(8,128)(2,1)S(1)}, u32[]{:S(2)}, u32[]{:S(2)}) collective-permute-start(bf16[240,640]{1,0:T(8,128)(2,1)S(1)} %add_convert_fusion.1.refs_4_), channel_id=1, source_target_pairs={{0,32},{32,64},{64,96},{96,0},{1,33},{33,65},{65,97},{97,1},{2,34}... | collective-permute-start | bytes 921608 | tf_op jit(solution)/shard_map/ppermute | solution.py:45
  117.7 5.4 %collective-permute-start.8 = (bf16[240,640]{1,0:T(8,128)(2,1)S(1)}, bf16[240,640]{1,0:T(8,128)(2,1)S(1)}, u32[]{:S(2)}, u32[]{:S(2)}) collective-permute-start(bf16[240,640]{1,0:T(8,128)(2,1)S(1)} %add_convert_fusion.1.refs_4_), channel_id=1, source_target_pairs={{0,8},{8,0},{1,9},{9,1},{2,10},{10,2},{3,11},{11,3},{4,12},{12,4},... | collective-permute-start | bytes 921608 | tf_op jit(solution)/shard_map/ppermute | solution.py:45
  119.4 4.8 %collective-permute-start.10 = (bf16[240,640]{1,0:T(8,128)(2,1)S(1)}, bf16[240,640]{1,0:T(8,128)(2,1)S(1)}, u32[]{:S(2)}, u32[]{:S(2)}) collective-permute-start(bf16[240,640]{1,0:T(8,128)(2,1)S(1)} %collective-permute-done.6.refs_6_), channel_id=1, source_target_pairs={{0,8},{8,0},{1,9},{9,1},{2,10},{10,2},{3,11},{11,3},{4,12},{12,4},... | collective-permute-start | bytes 921608 | tf_op jit(solution)/shard_map/ppermute | solution.py:45
  123.0 9.4 %collective-permute-start.11 = (bf16[240,640]{1,0:T(8,128)(2,1)S(1)}, bf16[240,640]{1,0:T(8,128)(2,1)}, u32[]{:S(2)}, u32[]{:S(2)}) collective-permute-start(bf16[240,640]{1,0:T(8,128)(2,1)S(1)} %collective-permute-done.7.refs_7_), channel_id=1, source_target_pairs={{0,8},{8,0},{1,9},{9,1},{2,10},{10,2},{3,11},{11,3},{4,12},{12,4},... | collective-permute-start | bytes 921608 | tf_op jit(solution)/shard_map/ppermute | solution.py:45
  125.0 8.3 %collective-permute-start.9 = (bf16[240,640]{1,0:T(8,128)(2,1)S(1)}, bf16[240,640]{1,0:T(8,128)(2,1)}, u32[]{:S(2)}, u32[]{:S(2)}) collective-permute-start(bf16[240,640]{1,0:T(8,128)(2,1)S(1)} %collective-permute-done.5.refs_5_), channel_id=1, source_target_pairs={{0,8},{8,0},{1,9},{9,1},{2,10},{10,2},{3,11},{11,3},{4,12},{12,4},... | collective-permute-start | bytes 921608 | tf_op jit(solution)/shard_map/ppermute | solution.py:45
  125.4 1.4 copy-start.1
  126.8 1.4 copy-start.3
  128.2 1.4 copy-start.5
  131.0 2.3 copy-start.7
  132.5 41.1 %collective-permute-start.26 = (bf16[640,1024]{1,0:T(8,128)(2,1)S(1)}, bf16[640,1024]{1,0:T(8,128)(2,1)S(1)}, u32[]{:S(2)}, u32[]{:S(2)}) collective-permute-start(bf16[640,1024]{1,0:T(8,128)(2,1)S(1)} %constant_dynamic-slice_fusion), channel_id=1, source_target_pairs={{0,1},{1,0},{2,3},{3,2},{4,5},{5,4},{6,7},{7,6},{8,9},{9,8},{10,11... | collective-permute-start | bytes 3932168 | tf_op jit(solution)/shard_map/ppermute | solution.py:45
  144.3 9.7 %collective-permute-start.32 = (bf16[240,640]{1,0:T(8,128)(2,1)S(1)}, bf16[240,640]{1,0:T(8,128)(2,1)S(1)}, u32[]{:S(2)}, u32[]{:S(2)}) collective-permute-start(bf16[240,640]{1,0:T(8,128)(2,1)S(1)} %get-tuple-element.73), channel_id=1, source_target_pairs={{0,32},{32,64},{64,96},{96,0},{1,33},{33,65},{65,97},{97,1},{2,34}... | collective-permute-start | bytes 921608 | tf_op jit(solution)/shard_map/ppermute | solution.py:45
  145.5 28.3 %collective-permute-start.16 = (bf16[320,1536]{1,0:T(8,128)(2,1)S(1)}, bf16[320,1536]{1,0:T(8,128)(2,1)S(1)}, u32[]{:S(2)}, u32[]{:S(2)}) collective-permute-start(bf16[320,1536]{1,0:T(8,128)(2,1)S(1)} %slice.8), channel_id=1, source_target_pairs={{0,2},{2,4},{4,6},{6,0},{1,3},{3,5},{5,7},{7,1},{8,10},{10,12},{12... | collective-permute-start | bytes 2949128 | tf_op jit(solution)/shard_map/ppermute | solution.py:45
  147.1 18.8 %copy-start.12 = (f32[640]{0:T(1024)S(1)}, f32[640]{0:T(1024)}, u32[]{:S(2)}) copy-start(f32[640]{0:T(1024)} %param.16) | copy-start | bytes 7684
  147.2 26.8 %collective-permute-start.18 = (bf16[320,1536]{1,0:T(8,128)(2,1)S(1)}, bf16[320,1536]{1,0:T(8,128)(2,1)S(1)}, u32[]{:S(2)}, u32[]{:S(2)}) collective-permute-start(bf16[320,1536]{1,0:T(8,128)(2,1)S(1)} %slice.9), channel_id=1, source_target_pairs={{0,6},{2,0},{4,2},{6,4},{1,7},{3,1},{5,3},{7,5},{8,14},{10,8},{12,... | collective-permute-start | bytes 2949128 | tf_op jit(solution)/shard_map/ppermute | solution.py:45
  149.6 7.6 %collective-permute-start.33 = (bf16[240,640]{1,0:T(8,128)(2,1)S(1)}, bf16[240,640]{1,0:T(8,128)(2,1)S(1)}, u32[]{:S(2)}, u32[]{:S(2)}) collective-permute-start(bf16[240,640]{1,0:T(8,128)(2,1)S(1)} %get-tuple-element.74), channel_id=1, source_target_pairs={{0,96},{32,0},{64,32},{96,64},{1,97},{33,1},{65,33},{97,65},{2,98}... | collective-permute-start | bytes 921608 | tf_op jit(solution)/shard_map/ppermute | solution.py:45
  154.0 9.1 %collective-permute-start.34 = (bf16[240,640]{1,0:T(8,128)(2,1)S(1)}, bf16[240,640]{1,0:T(8,128)(2,1)S(1)}, u32[]{:S(2)}, u32[]{:S(2)}) collective-permute-start(bf16[240,640]{1,0:T(8,128)(2,1)S(1)} %get-tuple-element.75), channel_id=1, source_target_pairs={{0,64},{32,96},{64,0},{96,32},{1,65},{33,97},{65,1},{97,33},{2,66}... | collective-permute-start | bytes 921608 | tf_op jit(solution)/shard_map/ppermute | solution.py:45
  163.0 44.6 %slice-start = ((s8[6553600]{0:T(1024)(128)(4,1)}), s8[4194304]{0:T(1024)(128)(4,1)S(1)}, s32[]{:S(2)}) async-start(s8[6553600]{0:T(1024)(128)(4,1)} %bitcast.5), calls=%async_computation.2 | async-start | bytes 8388608
  163.2 12.5 %collective-permute-start.35 = (bf16[240,640]{1,0:T(8,128)(2,1)S(1)}, bf16[240,640]{1,0:T(8,128)(2,1)S(1)}, u32[]{:S(2)}, u32[]{:S(2)}) collective-permute-start(bf16[240,640]{1,0:T(8,128)(2,1)S(1)} %convert_element_type.45), channel_id=1, source_target_pairs={{0,16},{16,0},{1,17},{17,1},{2,18},{18,2},{3,19},{19,3},{4,20},{20... | collective-permute-start | bytes 921608 | tf_op jit(solution)/shard_map/ppermute | solution.py:45
  165.9 41.7 %slice-start.1 = ((s8[6553600]{0:T(1024)(128)(4,1)}), s8[2359296]{0:T(1024)(128)(4,1)S(1)}, s32[]{:S(2)}) async-start(s8[6553600]{0:T(1024)(128)(4,1)} %bitcast.5), calls=%async_computation.3 | async-start | bytes 4718592
  165.9 55.6 %collective-permute-start.20 = (bf16[640,1536]{1,0:T(8,128)(2,1)S(1)}, bf16[640,1536]{1,0:T(8,128)(2,1)S(1)}, u32[]{:S(2)}, u32[]{:S(2)}) collective-permute-start(bf16[640,1536]{1,0:T(8,128)(2,1)S(1)} %collective-permute-done.15.refs_6_), channel_id=1, source_target_pairs={{0,8},{8,0},{1,9},{9,1},{2,10},{10,2},{3,11},{11,3},{4,12},{12,4},... | collective-permute-start | bytes 5898248 | tf_op jit(solution)/shard_map/ppermute | solution.py:45
  173.6 48.3 %collective-permute-start.23 = (bf16[640,1536]{1,0:T(8,128)(2,1)}, bf16[640,1536]{1,0:T(8,128)(2,1)S(1)}, u32[]{:S(2)}, u32[]{:S(2)}) collective-permute-start(bf16[640,1536]{1,0:T(8,128)(2,1)} %collective-permute-done.17.refs_9_), channel_id=1, source_target_pairs={{0,8},{8,0},{1,9},{9,1},{2,10},{10,2},{3,11},{11,3},{4,12},{12,4},... | collective-permute-start | bytes 5898248 | tf_op jit(solution)/shard_map/ppermute | solution.py:45
  173.8 7.4 %collective-permute-start.12 = (bf16[128,640]{1,0:T(8,128)(2,1)S(1)}, bf16[128,640]{1,0:T(8,128)(2,1)S(1)}, u32[]{:S(2)}, u32[]{:S(2)}) collective-permute-start(bf16[128,640]{1,0:T(8,128)(2,1)S(1)} %get-tuple-element.60.refs_3_), channel_id=1, source_target_pairs={{0,2},{2,4},{4,6},{6,0},{1,3},{3,5},{5,7},{7,1},{8,10},{10,12},{12... | collective-permute-start | bytes 491528 | tf_op jit(solution)/shard_map/ppermute | solution.py:45
  174.0 11.8 %collective-permute-start.13 = (bf16[128,640]{1,0:T(8,128)(2,1)S(1)}, bf16[128,640]{1,0:T(8,128)(2,1)S(1)}, u32[]{:S(2)}, u32[]{:S(2)}) collective-permute-start(bf16[128,640]{1,0:T(8,128)(2,1)S(1)} %get-tuple-element.61.refs_2_), channel_id=1, source_target_pairs={{0,4},{2,6},{4,0},{6,2},{1,5},{3,7},{5,1},{7,3},{8,12},{10,14},{12... | collective-permute-start | bytes 491528 | tf_op jit(solution)/shard_map/ppermute | solution.py:45
  175.7 12.8 %collective-permute-start.14 = (bf16[128,640]{1,0:T(8,128)(2,1)S(1)}, bf16[128,640]{1,0:T(8,128)(2,1)S(1)}, u32[]{:S(2)}, u32[]{:S(2)}) collective-permute-start(bf16[128,640]{1,0:T(8,128)(2,1)S(1)} %get-tuple-element.62.refs_1_), channel_id=1, source_target_pairs={{0,6},{2,0},{4,2},{6,4},{1,7},{3,1},{5,3},{7,5},{8,14},{10,8},{12,... | collective-permute-start | bytes 491528 | tf_op jit(solution)/shard_map/ppermute | solution.py:45
  181.2 12.6 %collective-permute-start.36 = (bf16[240,640]{1,0:T(8,128)(2,1)S(1)}, bf16[240,640]{1,0:T(8,128)(2,1)S(1)}, u32[]{:S(2)}, u32[]{:S(2)}) collective-permute-start(bf16[240,640]{1,0:T(8,128)(2,1)S(1)} %add_convert_fusion.refs_5_), channel_id=1, source_target_pairs={{0,32},{32,64},{64,96},{96,0},{1,33},{33,65},{65,97},{97,1},{2,34}... | collective-permute-start | bytes 921608 | tf_op jit(solution)/shard_map/ppermute | solution.py:45
  185.7 15.5 %collective-permute-start.37 = (bf16[240,640]{1,0:T(8,128)(2,1)S(1)}, bf16[240,640]{1,0:T(8,128)(2,1)S(1)}, u32[]{:S(2)}, u32[]{:S(2)}) collective-permute-start(bf16[240,640]{1,0:T(8,128)(2,1)S(1)} %add_convert_fusion.refs_5_), channel_id=1, source_target_pairs={{0,64},{32,96},{64,0},{96,32},{1,65},{33,97},{65,1},{97,33},{2,66}... | collective-permute-start | bytes 921608 | tf_op jit(solution)/shard_map/ppermute | solution.py:45
  188.5 14.8 %collective-permute-start.38 = (bf16[240,640]{1,0:T(8,128)(2,1)S(1)}, bf16[240,640]{1,0:T(8,128)(2,1)S(1)}, u32[]{:S(2)}, u32[]{:S(2)}) collective-permute-start(bf16[240,640]{1,0:T(8,128)(2,1)S(1)} %add_convert_fusion.refs_5_), channel_id=1, source_target_pairs={{0,96},{32,0},{64,32},{96,64},{1,97},{33,1},{65,33},{97,65},{2,98}... | collective-permute-start | bytes 921608 | tf_op jit(solution)/shard_map/ppermute | solution.py:45
  193.8 9.6 %collective-permute-start.39 = (bf16[240,640]{1,0:T(8,128)(2,1)S(1)}, bf16[240,640]{1,0:T(8,128)(2,1)S(1)}, u32[]{:S(2)}, u32[]{:S(2)}) collective-permute-start(bf16[240,640]{1,0:T(8,128)(2,1)S(1)} %add_convert_fusion.refs_5_), channel_id=1, source_target_pairs={{0,8},{8,0},{1,9},{9,1},{2,10},{10,2},{3,11},{11,3},{4,12},{12,4},... | collective-permute-start | bytes 921608 | tf_op jit(solution)/shard_map/ppermute | solution.py:45
  201.3 3.3 %collective-permute-start.40 = (bf16[240,640]{1,0:T(8,128)(2,1)S(1)}, bf16[240,640]{1,0:T(8,128)(2,1)S(1)}, u32[]{:S(2)}, u32[]{:S(2)}) collective-permute-start(bf16[240,640]{1,0:T(8,128)(2,1)S(1)} %collective-permute-done.36.refs_6_), channel_id=1, source_target_pairs={{0,8},{8,0},{1,9},{9,1},{2,10},{10,2},{3,11},{11,3},{4,12},{12,4},... | collective-permute-start | bytes 921608 | tf_op jit(solution)/shard_map/ppermute | solution.py:45
  203.3 11.6 %collective-permute-start.27 = (bf16[640,1024]{1,0:T(8,128)(2,1)S(1)}, bf16[640,1024]{1,0:T(8,128)(2,1)S(1)}, u32[]{:S(2)}, u32[]{:S(2)}) collective-permute-start(bf16[640,1024]{1,0:T(8,128)(2,1)S(1)} %collective-permute-done.26.refs_6_), channel_id=1, source_target_pairs={{0,8},{8,0},{1,9},{9,1},{2,10},{10,2},{3,11},{11,3},{4,12},{12,4},... | collective-permute-start | bytes 3932168 | tf_op jit(solution)/shard_map/ppermute | solution.py:45
  203.3 3.5 %collective-permute-start.41 = (bf16[240,640]{1,0:T(8,128)(2,1)S(1)}, bf16[240,640]{1,0:T(8,128)(2,1)S(1)}, u32[]{:S(2)}, u32[]{:S(2)}) collective-permute-start(bf16[240,640]{1,0:T(8,128)(2,1)S(1)} %collective-permute-done.37.refs_7_), channel_id=1, source_target_pairs={{0,8},{8,0},{1,9},{9,1},{2,10},{10,2},{3,11},{11,3},{4,12},{12,4},... | collective-permute-start | bytes 921608 | tf_op jit(solution)/shard_map/ppermute | solution.py:45
  204.5 2.8 %collective-permute-start.42 = (bf16[240,640]{1,0:T(8,128)(2,1)S(1)}, bf16[240,640]{1,0:T(8,128)(2,1)S(1)}, u32[]{:S(2)}, u32[]{:S(2)}) collective-permute-start(bf16[240,640]{1,0:T(8,128)(2,1)S(1)} %collective-permute-done.38.refs_8_), channel_id=1, source_target_pairs={{0,8},{8,0},{1,9},{9,1},{2,10},{10,2},{3,11},{11,3},{4,12},{12,4},... | collective-permute-start | bytes 921608 | tf_op jit(solution)/shard_map/ppermute | solution.py:45
  206.8 13.4 %collective-permute-start.21 = (bf16[320,1536]{1,0:T(8,128)(2,1)S(1)}, bf16[320,1536]{1,0:T(8,128)(2,1)S(1)}, u32[]{:S(2)}, u32[]{:S(2)}) collective-permute-start(bf16[320,1536]{1,0:T(8,128)(2,1)S(1)} %collective-permute-done.16.refs_7_), channel_id=1, source_target_pairs={{0,8},{8,0},{1,9},{9,1},{2,10},{10,2},{3,11},{11,3},{4,12},{12,4},... | collective-permute-start | bytes 2949128 | tf_op jit(solution)/shard_map/ppermute | solution.py:45
  207.3 14.2 %collective-permute-start.22 = (bf16[320,1536]{1,0:T(8,128)(2,1)S(1)}, bf16[320,1536]{1,0:T(8,128)(2,1)S(1)}, u32[]{:S(2)}, u32[]{:S(2)}) collective-permute-start(bf16[320,1536]{1,0:T(8,128)(2,1)S(1)} %collective-permute-done.18.refs_8_), channel_id=1, source_target_pairs={{0,8},{8,0},{1,9},{9,1},{2,10},{10,2},{3,11},{11,3},{4,12},{12,4},... | collective-permute-start | bytes 2949128 | tf_op jit(solution)/shard_map/ppermute | solution.py:45
  214.9 12.4 %collective-permute-start.25 = (bf16[256,640]{1,0:T(8,128)(2,1)S(1)}, bf16[256,640]{1,0:T(8,128)(2,1)S(1)}, u32[]{:S(2)}, u32[]{:S(2)}) collective-permute-start(bf16[256,640]{1,0:T(8,128)(2,1)S(1)} %get-tuple-element.67), channel_id=1, source_target_pairs={{0,1},{1,0},{2,3},{3,2},{4,5},{5,4},{6,7},{7,6},{8,9},{9,8},{10,11... | collective-permute-start | bytes 983048 | tf_op jit(solution)/shard_map/ppermute | solution.py:45
  220.3 17.4 %collective-permute-start.48 = (bf16[256,640]{1,0:T(8,128)(2,1)S(1)}, bf16[256,640]{1,0:T(8,128)(2,1)S(1)}, u32[]{:S(2)}, u32[]{:S(2)}) collective-permute-start(bf16[256,640]{1,0:T(8,128)(2,1)S(1)} %get-tuple-element.86), channel_id=1, source_target_pairs={{0,1},{1,0},{2,3},{3,2},{4,5},{5,4},{6,7},{7,6},{8,9},{9,8},{10,11... | collective-permute-start | bytes 983048 | tf_op jit(solution)/shard_map/ppermute | solution.py:45
  221.5 10.2 %collective-permute-start.43 = (bf16[128,640]{1,0:T(8,128)(2,1)S(1)}, bf16[128,640]{1,0:T(8,128)(2,1)S(1)}, u32[]{:S(2)}, u32[]{:S(2)}) collective-permute-start(bf16[128,640]{1,0:T(8,128)(2,1)S(1)} %get-tuple-element.79.refs_3_), channel_id=1, source_target_pairs={{0,2},{2,4},{4,6},{6,0},{1,3},{3,5},{5,7},{7,1},{8,10},{10,12},{12... | collective-permute-start | bytes 491528 | tf_op jit(solution)/shard_map/ppermute | solution.py:45
  221.5 10.7 %collective-permute-start.44 = (bf16[128,640]{1,0:T(8,128)(2,1)S(1)}, bf16[128,640]{1,0:T(8,128)(2,1)S(1)}, u32[]{:S(2)}, u32[]{:S(2)}) collective-permute-start(bf16[128,640]{1,0:T(8,128)(2,1)S(1)} %get-tuple-element.80.refs_2_), channel_id=1, source_target_pairs={{0,4},{2,6},{4,0},{6,2},{1,5},{3,7},{5,1},{7,3},{8,12},{10,14},{12... | collective-permute-start | bytes 491528 | tf_op jit(solution)/shard_map/ppermute | solution.py:45
  221.8 11.0 %collective-permute-start.45 = (bf16[128,640]{1,0:T(8,128)(2,1)S(1)}, bf16[128,640]{1,0:T(8,128)(2,1)S(1)}, u32[]{:S(2)}, u32[]{:S(2)}) collective-permute-start(bf16[128,640]{1,0:T(8,128)(2,1)S(1)} %get-tuple-element.81.refs_1_), channel_id=1, source_target_pairs={{0,6},{2,0},{4,2},{6,4},{1,7},{3,1},{5,3},{7,5},{8,14},{10,8},{12,... | collective-permute-start | bytes 491528 | tf_op jit(solution)/shard_map/ppermute | solution.py:45
  227.3 14.5 %collective-permute-start.19 = (bf16[64,1536]{1,0:T(8,128)(2,1)S(1)}, bf16[64,1536]{1,0:T(8,128)(2,1)S(1)}, u32[]{:S(2)}, u32[]{:S(2)}) collective-permute-start(bf16[64,1536]{1,0:T(8,128)(2,1)S(1)} %get-tuple-element.64), channel_id=1, source_target_pairs={{0,1},{1,0},{2,3},{3,2},{4,5},{5,4},{6,7},{7,6},{8,9},{9,8},{10,11... | collective-permute-start | bytes 589832 | tf_op jit(solution)/shard_map/ppermute | solution.py:45
  231.7 12.1 %collective-permute-start.24 = (bf16[64,1536]{1,0:T(8,128)(2,1)S(1)}, bf16[64,1536]{1,0:T(8,128)(2,1)S(1)}, u32[]{:S(2)}, u32[]{:S(2)}) collective-permute-start(bf16[64,1536]{1,0:T(8,128)(2,1)S(1)} %get-tuple-element.66), channel_id=1, source_target_pairs={{0,1},{1,0},{2,3},{3,2},{4,5},{5,4},{6,7},{7,6},{8,9},{9,8},{10,11... | collective-permute-start | bytes 589832 | tf_op jit(solution)/shard_map/ppermute | solution.py:45
  232.2 11.6 %collective-permute-start.28 = (bf16[64,2048]{1,0:T(8,128)(2,1)S(1)}, bf16[64,2048]{1,0:T(8,128)(2,1)S(1)}, u32[]{:S(2)}, u32[]{:S(2)}) collective-permute-start(bf16[64,2048]{1,0:T(8,128)(2,1)S(1)} %get-tuple-element.69), channel_id=1, source_target_pairs={{0,6},{2,0},{4,2},{6,4},{1,7},{3,1},{5,3},{7,5},{8,14},{10,8},{12,... | collective-permute-start | bytes 786440 | tf_op jit(solution)/shard_map/ppermute | solution.py:45
  232.8 16.1 %collective-permute-start.29 = (bf16[64,2048]{1,0:T(8,128)(2,1)S(1)}, bf16[64,2048]{1,0:T(8,128)(2,1)S(1)}, u32[]{:S(2)}, u32[]{:S(2)}) collective-permute-start(bf16[64,2048]{1,0:T(8,128)(2,1)S(1)} %get-tuple-element.70), channel_id=1, source_target_pairs={{0,4},{2,6},{4,0},{6,2},{1,5},{3,7},{5,1},{7,3},{8,12},{10,14},{12... | collective-permute-start | bytes 786440 | tf_op jit(solution)/shard_map/ppermute | solution.py:45
  237.7 12.2 %collective-permute-start.30 = (bf16[64,2048]{1,0:T(8,128)(2,1)S(1)}, bf16[64,2048]{1,0:T(8,128)(2,1)S(1)}, u32[]{:S(2)}, u32[]{:S(2)}) collective-permute-start(bf16[64,2048]{1,0:T(8,128)(2,1)S(1)} %get-tuple-element.71), channel_id=1, source_target_pairs={{0,2},{2,4},{4,6},{6,0},{1,3},{3,5},{5,7},{7,1},{8,10},{10,12},{12... | collective-permute-start | bytes 786440 | tf_op jit(solution)/shard_map/ppermute | solution.py:45
  241.9 14.3 %collective-permute-start.49 = (bf16[64,2048]{1,0:T(8,128)(2,1)S(1)}, bf16[64,2048]{1,0:T(8,128)(2,1)S(1)}, u32[]{:S(2)}, u32[]{:S(2)}) collective-permute-start(bf16[64,2048]{1,0:T(8,128)(2,1)S(1)} %get-tuple-element.88), channel_id=1, source_target_pairs={{0,6},{2,0},{4,2},{6,4},{1,7},{3,1},{5,3},{7,5},{8,14},{10,8},{12,... | collective-permute-start | bytes 786440 | tf_op jit(solution)/shard_map/ppermute | solution.py:45
  243.8 12.4 %collective-permute-start.50 = (bf16[64,2048]{1,0:T(8,128)(2,1)S(1)}, bf16[64,2048]{1,0:T(8,128)(2,1)S(1)}, u32[]{:S(2)}, u32[]{:S(2)}) collective-permute-start(bf16[64,2048]{1,0:T(8,128)(2,1)S(1)} %get-tuple-element.89), channel_id=1, source_target_pairs={{0,4},{2,6},{4,0},{6,2},{1,5},{3,7},{5,1},{7,3},{8,12},{10,14},{12... | collective-permute-start | bytes 786440 | tf_op jit(solution)/shard_map/ppermute | solution.py:45
  243.8 15.2 %collective-permute-start.51 = (bf16[64,2048]{1,0:T(8,128)(2,1)S(1)}, bf16[64,2048]{1,0:T(8,128)(2,1)S(1)}, u32[]{:S(2)}, u32[]{:S(2)}) collective-permute-start(bf16[64,2048]{1,0:T(8,128)(2,1)S(1)} %get-tuple-element.90), channel_id=1, source_target_pairs={{0,2},{2,4},{4,6},{6,0},{1,3},{3,5},{5,7},{7,1},{8,10},{10,12},{12... | collective-permute-start | bytes 786440 | tf_op jit(solution)/shard_map/ppermute | solution.py:45
  248.9 4.9 %collective-permute-start.47 = (bf16[64,1536]{1,0:T(8,128)(2,1)S(1)}, bf16[64,1536]{1,0:T(8,128)(2,1)S(1)}, u32[]{:S(2)}, u32[]{:S(2)}) collective-permute-start(bf16[64,1536]{1,0:T(8,128)(2,1)S(1)} %get-tuple-element.85), channel_id=1, source_target_pairs={{0,1},{1,0},{2,3},{3,2},{4,5},{5,4},{6,7},{7,6},{8,9},{9,8},{10,11... | collective-permute-start | bytes 589832 | tf_op jit(solution)/shard_map/ppermute | solution.py:45
  249.9 6.3 %collective-permute-start.46 = (bf16[64,1536]{1,0:T(8,128)(2,1)S(1)}, bf16[64,1536]{1,0:T(8,128)(2,1)S(1)}, u32[]{:S(2)}, u32[]{:S(2)}) collective-permute-start(bf16[64,1536]{1,0:T(8,128)(2,1)S(1)} %get-tuple-element.83), channel_id=1, source_target_pairs={{0,1},{1,0},{2,3},{3,2},{4,5},{5,4},{6,7},{7,6},{8,9},{9,8},{10,11... | collective-permute-start | bytes 589832 | tf_op jit(solution)/shard_map/ppermute | solution.py:45
  (5 other events, 5.3 us)

commit v2 on v1

--- a/solution.py
+++ b/solution.py
@@ -124,24 +124,37 @@
     )(keys, values, rates, queries)
 
 
-def start_half_kernel(place_ref, gate_ref, up_ref, down_ref, high_ref, low_ref, turned):
+def start_half_kernel(place_ref, gate_ref, up_ref, down_ref, high_ref, low_ref, loaded, turned, sems):
     core = place_ref[0]
     half = pl.ds(pl.multiple_of(core * HALF, HALF), HALF)
     tiles = pl.ds(pl.multiple_of(core * 256, 256), 384)
     inside = pl.ds(pl.multiple_of(core * (HALF - 256), 64), HALF)
-    for slot, ref in ((0, gate_ref), (1, up_ref)):
-        turned[...] = ref[0, :, tiles].T
+    copies = [
+        pltpu.make_async_copy(gate_ref.at[0, :, tiles], loaded.at[0], sems.at[0]),
+        pltpu.make_async_copy(up_ref.at[0, :, tiles], loaded.at[1], sems.at[1]),
+        pltpu.make_async_copy(down_ref.at[0, half], turned.at[pl.ds(384, HALF)], sems.at[2]),
+    ]
+    for copy in copies:
+        copy.start()
+    for slot in range(2):
+        copies[slot].wait()
+        turned[:384, :] = loaded[slot].T
         high_ref[slot], low_ref[slot] = split(turned[inside, :])
-    high_ref[2], low_ref[2] = split(down_ref[0, half, :])
+    copies[2].wait()
+    high_ref[2], low_ref[2] = split(turned[384:, :])
 
 
 def start_half(place, gate, up, down):
     return pl.pallas_call(
         start_half_kernel,
-        in_specs=[SMEM] + [VMEM] * 3,
+        in_specs=[SMEM] + [pl.BlockSpec(memory_space=pltpu.HBM)] * 3,
         out_specs=[VMEM] * 2,
-        out_shape=[pltpu.VMEM((3, HALF, HD), BF16)] * 2,
-        scratch_shapes=[pltpu.VMEM((384, HD), F32)],
+        out_shape=[jax.ShapeDtypeStruct((3, HALF, HD), BF16)] * 2,
+        scratch_shapes=[
+            pltpu.VMEM((2, HD, 384), F32),
+            pltpu.VMEM((384 + HALF, HD), F32),
+            pltpu.SemaphoreType.DMA((3,)),
+        ],
         compiler_params=room(16),
         cost_estimate=cost(1 << 24, 3 * HD * HD * 6),
         name="start_half",
@@ -176,9 +189,13 @@
 
 def renorm_kernel(count, place_ref, *refs):
     old_refs, (row_norm_ref, col_norm_ref) = refs[:count], refs[count : count + 2]
-    pieces, (high_ref, low_ref, down_ref) = refs[count + 2 : count + 10], refs[count + 10 :]
+    pieces, outs, down_ref = refs[count + 2 : count + 10], refs[count + 10 : -1], refs[-1]
     core, x = place_ref[0], place_ref[1]
     squares = jnp.zeros((8, HD), F32)
+
+    def store(where, matrix):
+        for out, part in zip(outs, split(matrix)):
+            out[where] = part
 
     def moved_rows(slot, rows, step):
         total = step.astype(F32)
@@ -196,20 +213,20 @@
             scale = row_norm_ref[slot, rows, :] * lax.rsqrt(
                 jnp.sum(moved * moved, axis=1, keepdims=True) + 1e-6
             )
-            high_ref[slot, rows, :], low_ref[slot, rows, :] = split(moved * scale)
+            store((slot, rows, slice(None)), moved * scale)
         moved = moved_rows(2, rows, piece[2 * PART :, :])
         down_ref[rows, :] = moved
         squares = squares + jnp.sum((moved * moved).reshape(PART // 8, 8, HD), axis=0)
     scale = col_norm_ref[...] * lax.rsqrt(jnp.sum(squares, axis=0, keepdims=True) + 1e-6)
-    high_ref[2], low_ref[2] = split(down_ref[...] * scale)
-
-
-def renorm(place, weights, row_norm, col_norm, pieces):
+    store(2, down_ref[...] * scale)
+
+
+def renorm(place, weights, row_norm, col_norm, pieces, last=False):
     return pl.pallas_call(
         lambda *refs: renorm_kernel(len(weights), *refs),
         in_specs=[SMEM] + [VMEM] * (10 + len(weights)),
-        out_specs=[VMEM] * 2,
-        out_shape=[pltpu.VMEM((3, HD, HD), BF16)] * 2,
+        out_specs=[VMEM] * (1 if last else 2),
+        out_shape=[pltpu.VMEM((3, HD, HD), BF16)] * (1 if last else 2),
         scratch_shapes=[pltpu.VMEM((HD, HD), F32)],
         compiler_params=room(16),
         cost_estimate=cost(1 << 24, 3 * HD * HD * 10),
@@ -218,13 +235,25 @@
 
 
 def grads_kernel(place_ref, high_ref, low_ref, near_ref, far_ref, *refs):
-    outs, (tokens, inner, total) = refs[:4], refs[4:]
+    outs, (tokens, inner, total), loaded = refs[:4], refs[4:7], refs[7:]
     core, x = place_ref[0], place_ref[1]
+    copies = []
+    if loaded:
+        held, sems = loaded
+        copies = [
+            pltpu.make_async_copy(ref, held.at[index], sems.at[index])
+            for index, ref in enumerate((high_ref, low_ref))
+        ]
+        high_ref, low_ref = held.at[0], held.at[1]
+    for copy in copies:
+        copy.start()
     for side, ref in enumerate((near_ref, far_ref)):
         for index in range(8):
             rows = pl.ds((side * 8 + index) * TOK, TOK)
             tokens[0, rows, :] = ref[index, :TOK, :]
             tokens[1, rows, :] = ref[index, TOK : 2 * TOK, :]
+    for copy in copies:
+        copy.wait()
     height = high_ref.shape[1]
     half = pl.ds(pl.multiple_of(core * (height - HALF), HALF), HALF)
 
@@ -260,6 +289,10 @@
 def grads(place, weights, near, far):
     part = pl.BlockSpec((8, 2 * TOK, HD), lambda i: (0, 0, 0))
     held = pl.BlockSpec(weights[0].shape, lambda i: (0, 0, 0))
+    extra = []
+    if weights[0].shape[1] == HALF:
+        held = pl.BlockSpec(memory_space=pltpu.HBM)
+        extra = [pltpu.VMEM((2, 3, HALF, HD), BF16), pltpu.SemaphoreType.DMA((2,))]
     return pl.pallas_call(
         grads_kernel,
         grid=(1,),
@@ -270,9 +303,10 @@
             pltpu.VMEM((2, 16 * TOK, HD), BF16),
             pltpu.VMEM((3, HALF, 16 * TOK), BF16),
             pltpu.VMEM((3, HALF, HD), F32),
-        ],
+        ]
+        + extra,
         cost_estimate=cost(12 * 16 * TOK * HALF * HD, 8 << 20),
-        compiler_params=room(16),
+        compiler_params=None if extra else room(20),
         name="grads",
     )(place, *weights, near, far)
 
@@ -288,7 +322,7 @@
     return pieces + [far[d] for d in range(4)]
 
 
-def apply_kernel(place_ref, high_ref, low_ref, gain_ref, query_ref, *refs):
+def apply_kernel(place_ref, high_ref, gain_ref, query_ref, *refs):
     outs, trade_ref, (rows_in, rows_out) = refs[:4], refs[4], refs[5:]
     z, yl = place_ref[2], place_ref[3]
     for d in range(4):
@@ -300,8 +334,8 @@
     def chunk(step, carry):
         rows = pl.ds(pl.multiple_of(step * 4 * TOK, 4 * TOK), 4 * TOK)
         query = rows_in[rows, :]
-        gate = nt(query, high_ref[0]) + nt(query, low_ref[0])
-        up = nt(query, high_ref[1]) + nt(query, low_ref[1])
+        gate = nt(query, high_ref[0])
+        up = nt(query, high_ref[1])
         hidden = (gate * jax.nn.sigmoid(gate) * up).astype(BF16)
         out = nn(hidden, high_ref[2])
         mean = jnp.sum(out * out, axis=1, keepdims=True) * (1.0 / HD)
@@ -321,7 +355,6 @@
         in_specs=[
             SMEM,
             pl.BlockSpec((3, HD, HD), lambda i: (0, 0, 0)),
-            pl.BlockSpec((2, HD, HD), lambda i: (0, 0, 0)),
             pl.BlockSpec((1, HD), lambda i: (0, 0)),
             pl.BlockSpec((8, TOK, HD), lambda i: (0, 2 + block, 0)),
         ],
@@ -331,9 +364,9 @@
         + [jax.ShapeDtypeStruct((4 * TOK, HD), BF16)],
         scratch_shapes=[pltpu.VMEM((8 * TOK, HD), BF16)] * 2,
         compiler_params=room(16),
-        cost_estimate=cost(10 * 8 * TOK * HD * HD, 5 << 20),
+        cost_estimate=cost(6 * 8 * TOK * HD * HD, 5 << 20),
         name="apply_weights",
-    )(place, *weights, gain, queries)
+    )(place, weights[0], gain, queries)
 
 
 def project_body(side, place_ref, *refs):
@@ -447,31 +480,33 @@
 
 
 def finish_kernel(place_ref, *refs):
-    out_ref = refs[-1]
-    for block in range(2):
-        parts = refs[block * 8 : block * 8 + 8]
-        for side in range(2):
-            half = place_ref[0] if side == 0 else 1 - place_ref[0]
-            start = half * COLS
-            total = parts[2 * side][...].astype(F32) + parts[2 * side + 1][...].astype(F32)
-            out_ref[block, :, pl.ds(pl.multiple_of(start, 512), LONG)] = total.astype(BF16)
-            cols = slice(side * WIDTH, (side + 1) * WIDTH)
-            total = parts[4][:, cols].astype(F32)
-            for part in parts[5:8]:
-                total = total + part[:, cols].astype(F32)
-            out_ref[block, :, pl.ds(pl.multiple_of(start + LONG, 512), WIDTH)] = total.astype(BF16)
-
-
-def finish(place, parts):
+    parts, out_ref = refs[:8], refs[-1]
+    for side in range(2):
+        half = place_ref[0] if side == 0 else 1 - place_ref[0]
+        start = half * COLS
+        total = parts[2 * side][...].astype(F32) + parts[2 * side + 1][...].astype(F32)
+        out_ref[0, :, pl.ds(pl.multiple_of(start, 512), LONG)] = total.astype(BF16)
+        cols = slice(side * WIDTH, (side + 1) * WIDTH)
+        total = parts[4][:, cols].astype(F32)
+        for part in parts[5:8]:
+            total = total + part[:, cols].astype(F32)
+        out_ref[0, :, pl.ds(pl.multiple_of(start + LONG, 512), WIDTH)] = total.astype(BF16)
+
+
+def finish(block, place, parts, held=None):
+    held = [] if held is None else [held]
+    whole = [pl.BlockSpec(part.shape, lambda i: (0, 0)) for part in parts]
     return pl.pallas_call(
         finish_kernel,
-        in_specs=[SMEM] + [VMEM] * 16,
-        out_specs=VMEM,
+        grid=(1,),
+        in_specs=[SMEM] + whole + [pl.BlockSpec(memory_space=pl.ANY)] * len(held),
+        out_specs=pl.BlockSpec((1, TOK, WIDE), lambda i: (block, 0, 0)),
         out_shape=jax.ShapeDtypeStruct((2, TOK, WIDE), BF16),
-        compiler_params=room(16),
-        cost_estimate=cost(1 << 20, 6 << 20),
+        input_output_aliases={9: 0} if held else {},
+        compiler_params=room(16),
+        cost_estimate=cost(1 << 20, 3 << 20),
         name="finish",
-    )(place, *parts)
+    )(place, *parts, *held)
 
 
 def per_device(queries, keys, values, rates, gate_fast, up_fast, down_fast, out_gain, out_proj):
@@ -519,10 +554,10 @@
     weights = renorm(place, [master], row_norm, col_norm, total)
     parts = grads(place, weights, second, second_far)
     total = sum_over_ctx(parts)
-    mixed = spread(0, weights)
-    weights = renorm(place, weights, row_norm, col_norm, total)
-    mixed += spread(1, weights)
-    return finish(place, mixed)
+    parts = spread(0, weights)
+    out = finish(0, place, parts)
+    weights = renorm(place, weights, row_norm, col_norm, total, True)
+    return finish(1, place, spread(1, weights), out)
 
 
 def solution(mesh):

time: 262 us -> 265 us (1.011)
  waiting for transfers between devices: 104 us -> 115 us
  local copies, waits for them, and re-layouts: 16.9 us -> 9.34 us
    ppermute x52, waiting for transfers between devices: 65.7 us -> 78.7 us  [shift(): lax.ppermute(array, axis, [(i, (i + by) % size) for i in range(size)])]
    unnamed x30 -> x28, local copies, waits for them, and re-layouts: 11.1 us -> 5.08 us
  transfers between devices with their start and end apart: 54 -> 54, of which waited for: 21 -> 22; matrix products, arithmetic and copies ran while one was open for 2% -> 2% of each run, Pallas kernels for 23% -> 22%
where the time goes in v2:
time: 265 us; the launch traced here: 264 us
  waiting for transfers between devices  115 us (43%)
  starting transfers between devices  76.2 us (29%)
  Pallas kernels  61.8 us (23%)
  local copies, waits for them, and re-layouts  9.34 us (4%)
    ppermute x52, waiting for transfers between devices, shift(): lax.ppermute(array, axis, [(i, (i + by) % size) for i in range(size)])  78.7 us
    ppermute x52, starting transfers between devices, shift(): lax.ppermute(array, axis, [(i, (i + by) % size) for i in range(size)])  64.9 us
    all_to_all x2, waiting for transfers between devices, to_heads(): return lax.all_to_all(array, ('z', 'yl'), 0, 0, tiled=True)  36.1 us
    pallas_call x2, Pallas kernels, grads(): pl.pallas_call(grads_kernel, grid=(1,), in_specs=[SMEM] + [held] * 2 + [p...  18.5 us
    pallas_call x4, Pallas kernels, project(): pl.pallas_call(lambda *refs: project_body(side, *refs), grid_spec=pltpu.P...  12.2 us
    all_to_all x2, starting transfers between devices, to_heads(): return lax.all_to_all(array, ('z', 'yl'), 0, 0, tiled=True)  11.3 us
    pallas_call x2, Pallas kernels, apply_weights(): pl.pallas_call(apply_kernel, grid=(1,), in_specs=[SMEM, pl.BlockSpec((3,...  7.35 us
    pallas_call x2, Pallas kernels, pair_project(): pl.pallas_call(pair_kernel, in_specs=[SMEM] + [VMEM] * 5 + [pl.BlockSpec(...  6.47 us
  transfers between devices with their start and end apart: 54, of which 22 were waited for; matrix products, arithmetic and copies ran while one was open for 2% of the time, Pallas kernels for 22%

profile of v2, /device:TPU:1, one launch (start us, length us, event | category | flops | bytes accessed | tf_op | source)
XLA Modules:
  0.0 264.4 jit_solution(13112455328887800505)
XLA Ops:
  0.0 2.5 pack_first.1
  2.5 6.9 %all-to-all-start = ((bf16[8,128,640]{2,1,0:T(8,128)(2,1)}), bf16[8,128,640]{2,1,0:T(8,128)(2,1)S(1)}, u32[]{:S(2)}, u32[]{:S(2)}) async-start(bf16[8,128,640]{2,1,0:T(8,128)(2,1)} %pack_first.1), calls=%async_computation | async-start | bytes 2621440 | tf_op jit(solution)/shard_map/all_to_all | solution.py:49
  9.4 3.5 %pack_second.1 = bf16[8,256,640]{2,1,0:T(8,128)(2,1)} custom-call(bf16[2,64,5120]{2,1,0:T(8,128)(2,1)} %key_ref.3, bf16[2,64,5120]{2,1,0:T(8,128)(2,1)} %value_ref.3, bf16[2,8,64]{2,1,0:T(8,128)(2,1)} %bitcast.8, bf16[2,64,5120]{2,1,0:T(8,128)(2,1)} %query_ref.1), custom_call_target="tpu_custom_call" | custom-call | flops 1048576 | bytes 5242880 | tf_op jit(solution)/shard_map/pack_second/pallas_call | solution.py:111
  12.9 14.2 %all-to-all-done.near_ref = bf16[8,128,640]{2,1,0:T(8,128)(2,1)S(1)} async-done(((bf16[8,128,640]{2,1,0:T(8,128)(2,1)}), bf16[8,128,640]{2,1,0:T(8,128)(2,1)S(1)}, u32[]{:S(2)}, u32[]{:S(2)}) %all-to-all-start) | async-done | bytes 1310752 | tf_op jit(solution)/shard_map/all_to_all | solution.py:49
  27.1 4.4 %all-to-all-start.1 = ((bf16[8,256,640]{2,1,0:T(8,128)(2,1)}), bf16[8,256,640]{2,1,0:T(8,128)(2,1)}, u32[]{:S(2)}, u32[]{:S(2)}) async-start(bf16[8,256,640]{2,1,0:T(8,128)(2,1)} %pack_second.1), calls=%async_computation.1 | async-start | bytes 5242880 | tf_op jit(solution)/shard_map/all_to_all | solution.py:49
  31.5 1.9 collective-permute-start
  33.5 1.4 copy-done.1
  34.9 1.4 copy-done.3
  36.4 2.0 start_half.1
  38.4 1.1 copy-done.8
  40.5 21.9 %all-to-all-done.1.near_ref.query_ref = bf16[8,256,640]{2,1,0:T(8,128)(2,1)} async-done(((bf16[8,256,640]{2,1,0:T(8,128)(2,1)}), bf16[8,256,640]{2,1,0:T(8,128)(2,1)}, u32[]{:S(2)}, u32[]{:S(2)}) %all-to-all-start.1) | async-done | bytes 2621472 | tf_op jit(solution)/shard_map/all_to_all | solution.py:49
  62.4 2.7 %collective-permute-start.12 = (bf16[8,256,640]{2,1,0:T(8,128)(2,1)}, bf16[8,256,640]{2,1,0:T(8,128)(2,1)}, u32[]{:S(2)}, u32[]{:S(2)}) collective-permute-start(bf16[8,256,640]{2,1,0:T(8,128)(2,1)} %all-to-all-done.1.near_ref.query_ref), channel_id=1, source_target_pairs={{0,8},{8,0},{1,9},{9,1},{2,10},{10,2},{3,11},{11,3},{4,12},{12,4},... | collective-permute-start | bytes 7864328 | tf_op jit(solution)/shard_map/ppermute | solution.py:45
  65.1 10.3 %grads.2 = (f32[240,640]{1,0:T(8,128)S(1)}, bf16[240,640]{1,0:T(8,128)(2,1)S(1)}, bf16[240,640]{1,0:T(8,128)(2,1)}, bf16[240,640]{1,0:T(8,128)(2,1)}) custom-call(s32[4]{0:T(128)} %copy-done.6, bf16[3,320,640]{2,1,0:T(8,128)(2,1)} %copy-done.8, bf16[3,320,640]{2,1,0:T(8,128)(2,1)} %copy-done.9, bf16[8,128,640]{2,1,0:T(8,128)(2,1)} %copy-done.10, ...), custom_call_target="tpu_custom_call" | custom-call | flops 2516582400 | bytes 8388608 | tf_op jit(solution)/shard_map/grads/pallas_call | solution.py:296
  75.5 2.8 %collective-permute-start.3 = (bf16[240,640]{1,0:T(8,128)(2,1)}, bf16[240,640]{1,0:T(8,128)(2,1)}, u32[]{:S(2)}, u32[]{:S(2)}) collective-permute-start(bf16[240,640]{1,0:T(8,128)(2,1)} %get-tuple-element.54), channel_id=1, source_target_pairs={{0,64},{32,96},{64,0},{96,32},{1,65},{33,97},{65,1},{97,33},{2,66}... | collective-permute-start | bytes 921608 | tf_op jit(solution)/shard_map/ppermute | solution.py:45
  79.7 2.5 constant_dynamic-slice_fusion
  82.7 3.5 %collective-permute-done.3 = bf16[240,640]{1,0:T(8,128)(2,1)} collective-permute-done((bf16[240,640]{1,0:T(8,128)(2,1)}, bf16[240,640]{1,0:T(8,128)(2,1)}, u32[]{:S(2)}, u32[]{:S(2)}) %collective-permute-start.3) | collective-permute-done | bytes 307232 | tf_op jit(solution)/shard_map/ppermute | solution.py:45
  86.2 6.7 %collective-permute-done.2 = bf16[240,640]{1,0:T(8,128)(2,1)} collective-permute-done((bf16[240,640]{1,0:T(8,128)(2,1)}, bf16[240,640]{1,0:T(8,128)(2,1)}, u32[]{:S(2)}, u32[]{:S(2)}) %collective-permute-start.2) | collective-permute-done | bytes 307232 | tf_op jit(solution)/shard_map/ppermute | solution.py:45
  93.1 1.5 convert_add_fusion.1
  94.7 2.7 %collective-permute-start.4 = (bf16[240,640]{1,0:T(8,128)(2,1)S(1)}, bf16[240,640]{1,0:T(8,128)(2,1)S(1)}, u32[]{:S(2)}, u32[]{:S(2)}) collective-permute-start(bf16[240,640]{1,0:T(8,128)(2,1)S(1)} %convert_element_type.39), channel_id=1, source_target_pairs={{0,16},{16,0},{1,17},{17,1},{2,18},{18,2},{3,19},{19,3},{4,20},{20... | collective-permute-start | bytes 921608 | tf_op jit(solution)/shard_map/ppermute | solution.py:45
  97.4 1.7 constant_dynamic-slice_fusion.1
  99.1 2.7 %collective-permute-start.29 = (bf16[640,1536]{1,0:T(8,128)(2,1)S(1)}, bf16[640,1536]{1,0:T(8,128)(2,1)S(1)}, u32[]{:S(2)}, u32[]{:S(2)}) collective-permute-start(bf16[640,1536]{1,0:T(8,128)(2,1)S(1)} %constant_dynamic-slice_fusion.1), channel_id=1, source_target_pairs={{0,6},{2,0},{4,2},{6,4},{1,7},{3,1},{5,3},{7,5},{8,14},{10,8},{12,... | collective-permute-start | bytes 5898248 | tf_op jit(solution)/shard_map/ppermute | solution.py:45
  101.8 18.4 %collective-permute-done.4 = bf16[240,640]{1,0:T(8,128)(2,1)S(1)} collective-permute-done((bf16[240,640]{1,0:T(8,128)(2,1)S(1)}, bf16[240,640]{1,0:T(8,128)(2,1)S(1)}, u32[]{:S(2)}, u32[]{:S(2)}) %collective-permute-start.4) | collective-permute-done | bytes 307232 | tf_op jit(solution)/shard_map/ppermute | solution.py:45
  120.6 2.9 %collective-permute-start.6 = (bf16[240,640]{1,0:T(8,128)(2,1)S(1)}, bf16[240,640]{1,0:T(8,128)(2,1)S(1)}, u32[]{:S(2)}, u32[]{:S(2)}) collective-permute-start(bf16[240,640]{1,0:T(8,128)(2,1)S(1)} %add_convert_fusion.1.refs_4_), channel_id=1, source_target_pairs={{0,64},{32,96},{64,0},{96,32},{1,65},{33,97},{65,1},{97,33},{2,66}... | collective-permute-start | bytes 921608 | tf_op jit(solution)/shard_map/ppermute | solution.py:45
  123.6 5.1 %collective-permute-done.5.refs_5_ = bf16[240,640]{1,0:T(8,128)(2,1)S(1)} collective-permute-done((bf16[240,640]{1,0:T(8,128)(2,1)S(1)}, bf16[240,640]{1,0:T(8,128)(2,1)S(1)}, u32[]{:S(2)}, u32[]{:S(2)}) %collective-permute-start.5) | collective-permute-done | bytes 307232 | tf_op jit(solution)/shard_map/ppermute | solution.py:45
  129.5 6.3 %collective-permute-done.6.refs_6_ = bf16[240,640]{1,0:T(8,128)(2,1)S(1)} collective-permute-done((bf16[240,640]{1,0:T(8,128)(2,1)S(1)}, bf16[240,640]{1,0:T(8,128)(2,1)S(1)}, u32[]{:S(2)}, u32[]{:S(2)}) %collective-permute-start.6) | collective-permute-done | bytes 307232 | tf_op jit(solution)/shard_map/ppermute | solution.py:45
  135.8 2.6 collective-permute-start.8
  138.4 1.2 collective-permute-start.9
  141.7 1.3 start_full.1
  143.0 2.5 renorm.2
  145.5 8.2 %grads.3 = (f32[240,640]{1,0:T(8,128)S(1)}, bf16[240,640]{1,0:T(8,128)(2,1)S(1)}, bf16[240,640]{1,0:T(8,128)(2,1)S(1)}, bf16[240,640]{1,0:T(8,128)(2,1)S(1)}) custom-call(s32[4]{0:T(128)S(1)} %copy-done.7, bf16[3,640,640]{2,1,0:T(8,128)(2,1)S(1)} %get-tuple-element.55.high_ref.refs_1_, bf16[3,640,640]{2,1,0:T(8,128)(2,1)S(1)} %get-tuple-element.56.low_ref.refs_2_, ...), custom_call_target="tpu_custom_call" | custom-call | flops 2516582400 | bytes 8388608 | tf_op jit(solution)/shard_map/grads/pallas_call | solution.py:296
  155.1 1.8 collective-permute-start.14
  157.6 6.5 %collective-permute-done.15 = bf16[240,640]{1,0:T(8,128)(2,1)S(1)} collective-permute-done((bf16[240,640]{1,0:T(8,128)(2,1)S(1)}, bf16[240,640]{1,0:T(8,128)(2,1)S(1)}, u32[]{:S(2)}, u32[]{:S(2)}) %collective-permute-start.15) | collective-permute-done | bytes 307232 | tf_op jit(solution)/shard_map/ppermute | solution.py:45
  164.9 6.0 %collective-permute-done.14 = bf16[240,640]{1,0:T(8,128)(2,1)S(1)} collective-permute-done((bf16[240,640]{1,0:T(8,128)(2,1)S(1)}, bf16[240,640]{1,0:T(8,128)(2,1)S(1)}, u32[]{:S(2)}, u32[]{:S(2)}) %collective-permute-start.14) | collective-permute-done | bytes 307232 | tf_op jit(solution)/shard_map/ppermute | solution.py:45
  172.9 3.7 %apply_weights.3 = (bf16[128,640]{1,0:T(8,128)(2,1)S(1)}, bf16[128,640]{1,0:T(8,128)(2,1)S(1)}, bf16[128,640]{1,0:T(8,128)(2,1)S(1)}, bf16[128,640]{1,0:T(8,128)(2,1)S(1)}, bf16[256,640]{1,0:T(8,128)(2,1)S(1)}) custom-call(s32[4]{0:T(128)S(1)} %copy-done.7, bf16[3,640,640]{2,1,0:T(8,128)(2,1)S(1)} %get-tuple-element.55.high_ref.refs_1_, ...), custom_call_target="tpu_custom_call" | custom-call | flops 1258291200 | bytes 5242880 | tf_op jit(solution)/shard_map/apply_weights/pallas_call | solution.py:352
  176.6 2.3 collective-permute-done.28.refs_7_
  178.9 1.9 collective-permute-done.16
  181.4 4.3 %collective-permute-done.30.refs_8_ = bf16[320,1536]{1,0:T(8,128)(2,1)S(1)} collective-permute-done((bf16[320,1536]{1,0:T(8,128)(2,1)S(1)}, bf16[320,1536]{1,0:T(8,128)(2,1)S(1)}, u32[]{:S(2)}, u32[]{:S(2)}) %collective-permute-start.30) | collective-permute-done | bytes 983072 | tf_op jit(solution)/shard_map/ppermute | solution.py:45
  185.8 1.1 collective-permute-start.17
  186.9 3.5 %collective-permute-start.18 = (bf16[240,640]{1,0:T(8,128)(2,1)S(1)}, bf16[240,640]{1,0:T(8,128)(2,1)S(1)}, u32[]{:S(2)}, u32[]{:S(2)}) collective-permute-start(bf16[240,640]{1,0:T(8,128)(2,1)S(1)} %add_convert_fusion.refs_5_), channel_id=1, source_target_pairs={{0,64},{32,96},{64,0},{96,32},{1,65},{33,97},{65,1},{97,33},{2,66}... | collective-permute-start | bytes 921608 | tf_op jit(solution)/shard_map/ppermute | solution.py:45
  190.4 1.3 collective-permute-start.45
  191.7 3.2 %collective-permute-done.45.refs_4_ = bf16[128,640]{1,0:T(8,128)(2,1)S(1)} collective-permute-done((bf16[128,640]{1,0:T(8,128)(2,1)S(1)}, bf16[128,640]{1,0:T(8,128)(2,1)S(1)}, u32[]{:S(2)}, u32[]{:S(2)}) %collective-permute-start.45) | collective-permute-done | bytes 163872 | tf_op jit(solution)/shard_map/ppermute | solution.py:45
  194.9 3.1 %collective-permute-start.19 = (bf16[240,640]{1,0:T(8,128)(2,1)S(1)}, bf16[240,640]{1,0:T(8,128)(2,1)S(1)}, u32[]{:S(2)}, u32[]{:S(2)}) collective-permute-start(bf16[240,640]{1,0:T(8,128)(2,1)S(1)} %add_convert_fusion.refs_5_), channel_id=1, source_target_pairs={{0,96},{32,0},{64,32},{96,64},{1,97},{33,1},{65,33},{97,65},{2,98}... | collective-permute-start | bytes 921608 | tf_op jit(solution)/shard_map/ppermute | solution.py:45
  198.0 3.1 %collective-permute-start.20 = (bf16[240,640]{1,0:T(8,128)(2,1)S(1)}, bf16[240,640]{1,0:T(8,128)(2,1)S(1)}, u32[]{:S(2)}, u32[]{:S(2)}) collective-permute-start(bf16[240,640]{1,0:T(8,128)(2,1)S(1)} %add_convert_fusion.refs_5_), channel_id=1, source_target_pairs={{0,8},{8,0},{1,9},{9,1},{2,10},{10,2},{3,11},{11,3},{4,12},{12,4},... | collective-permute-start | bytes 921608 | tf_op jit(solution)/shard_map/ppermute | solution.py:45
  201.1 3.3 %collective-permute-start.21 = (bf16[240,640]{1,0:T(8,128)(2,1)S(1)}, bf16[240,640]{1,0:T(8,128)(2,1)S(1)}, u32[]{:S(2)}, u32[]{:S(2)}) collective-permute-start(bf16[240,640]{1,0:T(8,128)(2,1)S(1)} %collective-permute-done.17.refs_6_), channel_id=1, source_target_pairs={{0,8},{8,0},{1,9},{9,1},{2,10},{10,2},{3,11},{11,3},{4,12},{12,4},... | collective-permute-start | bytes 921608 | tf_op jit(solution)/shard_map/ppermute | solution.py:45
  204.4 2.4 collective-permute-start.33
  207.4 3.5 %collective-permute-done.22.refs_11_ = bf16[240,640]{1,0:T(8,128)(2,1)S(1)} collective-permute-done((bf16[240,640]{1,0:T(8,128)(2,1)S(1)}, bf16[240,640]{1,0:T(8,128)(2,1)S(1)}, u32[]{:S(2)}, u32[]{:S(2)}) %collective-permute-start.22) | collective-permute-done | bytes 307232 | tf_op jit(solution)/shard_map/ppermute | solution.py:45
  211.3 1.2 collective-permute-done.23.refs_12_
  212.8 3.0 %shard_map.93 = (bf16[64,1536]{1,0:T(8,128)(2,1)S(1)}, bf16[64,1536]{1,0:T(8,128)(2,1)S(1)}) custom-call(s32[4]{0:T(128)S(1)} %copy-done.7, bf16[128,640]{1,0:T(8,128)(2,1)S(1)} %get-tuple-element.74.refs_1_.refs_0_, bf16[128,640]{1,0:T(8,128)(2,1)S(1)} %collective-permute-done.43.refs_2_, bf16[128,640]{1,0:T(8,128)(2,1)S(1)} %collective-permute-done.44.refs_3_, ...), custom_call_target="tpu_custom_call" | custom-call | flops 2013265920 | bytes 7864320 | tf_op jit(solution)/shard_map/pallas_call | solution.py:414
  215.8 2.3 renorm.3.high_ref
  218.1 3.7 %apply_weights.2 = (bf16[128,640]{1,0:T(8,128)(2,1)S(1)}, bf16[128,640]{1,0:T(8,128)(2,1)S(1)}, bf16[128,640]{1,0:T(8,128)(2,1)S(1)}, bf16[128,640]{1,0:T(8,128)(2,1)S(1)}, bf16[256,640]{1,0:T(8,128)(2,1)S(1)}) custom-call(s32[4]{0:T(128)S(1)} %copy-done.7, bf16[3,640,640]{2,1,0:T(8,128)(2,1)S(1)} %renorm.3.high_ref, f32[1,640]{1,0:T(1,128)S(1)} %reshape.3.gain_ref, ...), custom_call_target="tpu_custom_call" | custom-call | flops 1258291200 | bytes 5242880 | tf_op jit(solution)/shard_map/apply_weights/pallas_call | solution.py:352
  221.8 1.6 collective-permute-start.24
  223.4 3.1 %collective-permute-start.25 = (bf16[128,640]{1,0:T(8,128)(2,1)S(1)}, bf16[128,640]{1,0:T(8,128)(2,1)S(1)}, u32[]{:S(2)}, u32[]{:S(2)}) collective-permute-start(bf16[128,640]{1,0:T(8,128)(2,1)S(1)} %get-tuple-element.63.refs_2_), channel_id=1, source_target_pairs={{0,4},{2,6},{4,0},{6,2},{1,5},{3,7},{5,1},{7,3},{8,12},{10,14},{12... | collective-permute-start | bytes 491528 | tf_op jit(solution)/shard_map/ppermute | solution.py:45
  227.3 3.1 %shard_map.94 = (bf16[64,1536]{1,0:T(8,128)(2,1)S(1)}, bf16[64,1536]{1,0:T(8,128)(2,1)S(1)}) custom-call(s32[4]{0:T(128)S(1)} %copy-done.7, bf16[128,640]{1,0:T(8,128)(2,1)S(1)} %get-tuple-element.74.refs_1_.refs_0_, bf16[128,640]{1,0:T(8,128)(2,1)S(1)} %collective-permute-done.43.refs_2_, bf16[128,640]{1,0:T(8,128)(2,1)S(1)} %collective-permute-done.44.refs_3_, ...), custom_call_target="tpu_custom_call" | custom-call | flops 2013265920 | bytes 7864320 | tf_op jit(solution)/shard_map/pallas_call | solution.py:414
  231.1 3.2 %pair_project.3 = (bf16[64,2048]{1,0:T(8,128)(2,1)S(1)}, bf16[64,2048]{1,0:T(8,128)(2,1)S(1)}, bf16[64,2048]{1,0:T(8,128)(2,1)S(1)}, bf16[64,2048]{1,0:T(8,128)(2,1)S(1)}) custom-call(s32[4]{0:T(128)S(1)} %copy-done.7, bf16[128,640]{1,0:T(8,128)(2,1)S(1)} %get-tuple-element.74.refs_1_.refs_0_, bf16[128,640]{1,0:T(8,128)(2,1)S(1)} %get-tuple-element.77.refs_1_, ...), custom_call_target="tpu_custom_call" | custom-call | flops 1342177280 | bytes 5242880 | tf_op jit(solution)/shard_map/pair_project/pallas_call | solution.py:466
  236.0 2.4 collective-permute-start.50
  238.4 3.1 %shard_map.91 = (bf16[64,1536]{1,0:T(8,128)(2,1)S(1)}, bf16[64,1536]{1,0:T(8,128)(2,1)S(1)}) custom-call(s32[4]{0:T(128)S(1)} %copy-done.7, bf16[128,640]{1,0:T(8,128)(2,1)S(1)} %get-tuple-element.61.refs_1_.refs_0_, bf16[128,640]{1,0:T(8,128)(2,1)S(1)} %collective-permute-done.24.refs_2_, bf16[128,640]{1,0:T(8,128)(2,1)S(1)} %collective-permute-done.25.refs_3_, ...), custom_call_target="tpu_custom_call" | custom-call | flops 2013265920 | bytes 7864320 | tf_op jit(solution)/shard_map/pallas_call | solution.py:414
  241.6 3.2 %pair_project.2 = (bf16[64,2048]{1,0:T(8,128)(2,1)S(1)}, bf16[64,2048]{1,0:T(8,128)(2,1)S(1)}, bf16[64,2048]{1,0:T(8,128)(2,1)S(1)}, bf16[64,2048]{1,0:T(8,128)(2,1)S(1)}) custom-call(s32[4]{0:T(128)S(1)} %copy-done.7, bf16[128,640]{1,0:T(8,128)(2,1)S(1)} %get-tuple-element.61.refs_1_.refs_0_, bf16[128,640]{1,0:T(8,128)(2,1)S(1)} %get-tuple-element.64.refs_1_, ...), custom_call_target="tpu_custom_call" | custom-call | flops 1342177280 | bytes 5242880 | tf_op jit(solution)/shard_map/pair_project/pallas_call | solution.py:466
  244.8 2.7 %collective-permute-start.40 = (bf16[64,2048]{1,0:T(8,128)(2,1)S(1)}, bf16[64,2048]{1,0:T(8,128)(2,1)S(1)}, u32[]{:S(2)}, u32[]{:S(2)}) collective-permute-start(bf16[64,2048]{1,0:T(8,128)(2,1)S(1)} %get-tuple-element.71), channel_id=1, source_target_pairs={{0,6},{2,0},{4,2},{6,4},{1,7},{3,1},{5,3},{7,5},{8,14},{10,8},{12,... | collective-permute-start | bytes 786440 | tf_op jit(solution)/shard_map/ppermute | solution.py:45
  248.3 3.1 %shard_map.92 = (bf16[64,1536]{1,0:T(8,128)(2,1)S(1)}, bf16[64,1536]{1,0:T(8,128)(2,1)S(1)}) custom-call(s32[4]{0:T(128)S(1)} %copy-done.7, bf16[128,640]{1,0:T(8,128)(2,1)S(1)} %get-tuple-element.61.refs_1_.refs_0_, bf16[128,640]{1,0:T(8,128)(2,1)S(1)} %collective-permute-done.24.refs_2_, bf16[128,640]{1,0:T(8,128)(2,1)S(1)} %collective-permute-done.25.refs_3_, ...), custom_call_target="tpu_custom_call" | custom-call | flops 2013265920 | bytes 7864320 | tf_op jit(solution)/shard_map/pallas_call | solution.py:414
  252.9 1.6 finish.2.refs_8_
  254.5 1.7 collective-permute-done.31.refs_1_
  256.2 2.1 collective-permute-done.36.refs_3_
  258.3 4.5 %collective-permute-done.42.refs_7_ = bf16[64,2048]{1,0:T(8,128)(2,1)S(1)} collective-permute-done((bf16[64,2048]{1,0:T(8,128)(2,1)S(1)}, bf16[64,2048]{1,0:T(8,128)(2,1)S(1)}, u32[]{:S(2)}, u32[]{:S(2)}) %collective-permute-start.42) | collective-permute-done | bytes 262176 | tf_op jit(solution)/shard_map/ppermute | solution.py:45
  262.8 1.6 finish.3
  (103 shorter events, 19.0 us)
Async XLA Ops:
  2.5 24.6 %all-to-all-start = ((bf16[8,128,640]{2,1,0:T(8,128)(2,1)}), bf16[8,128,640]{2,1,0:T(8,128)(2,1)S(1)}, u32[]{:S(2)}, u32[]{:S(2)}) async-start(bf16[8,128,640]{2,1,0:T(8,128)(2,1)} %pack_first.1), calls=%async_computation | async-start | bytes 2621440 | tf_op jit(solution)/shard_map/all_to_all | solution.py:49
  12.9 20.6 %copy-start = (f32[1,640,640]{2,1,0:T(8,128)S(1)}, f32[1,640,640]{2,1,0:T(8,128)}, u32[]{:S(2)}) copy-start(f32[1,640,640]{2,1,0:T(8,128)} %gate_ref.3) | copy-start | bytes 4915204
  27.1 4.4 %copy-start.10 = (bf16[8,128,640]{2,1,0:T(8,128)(2,1)}, bf16[8,128,640]{2,1,0:T(8,128)(2,1)S(1)}, u32[]{:S(2)}) copy-start(bf16[8,128,640]{2,1,0:T(8,128)(2,1)S(1)} %all-to-all-done.near_ref) | copy-start | bytes 3932164
  27.1 35.3 %all-to-all-start.1 = ((bf16[8,256,640]{2,1,0:T(8,128)(2,1)}), bf16[8,256,640]{2,1,0:T(8,128)(2,1)}, u32[]{:S(2)}, u32[]{:S(2)}) async-start(bf16[8,256,640]{2,1,0:T(8,128)(2,1)} %pack_second.1), calls=%async_computation.1 | async-start | bytes 5242880 | tf_op jit(solution)/shard_map/all_to_all | solution.py:49
  31.5 33.6 %collective-permute-start = (bf16[8,128,640]{2,1,0:T(8,128)(2,1)S(1)}, bf16[8,128,640]{2,1,0:T(8,128)(2,1)}, u32[]{:S(2)}, u32[]{:S(2)}) collective-permute-start(bf16[8,128,640]{2,1,0:T(8,128)(2,1)S(1)} %all-to-all-done.near_ref), channel_id=1, source_target_pairs={{0,8},{8,0},{1,9},{9,1},{2,10},{10,2},{3,11},{11,3},{4,12},{12,4},... | collective-permute-start | bytes 3932168 | tf_op jit(solution)/shard_map/ppermute | solution.py:45
  36.4 2.0 copy-start.6
  62.4 83.1 %collective-permute-start.12 = (bf16[8,256,640]{2,1,0:T(8,128)(2,1)}, bf16[8,256,640]{2,1,0:T(8,128)(2,1)}, u32[]{:S(2)}, u32[]{:S(2)}) collective-permute-start(bf16[8,256,640]{2,1,0:T(8,128)(2,1)} %all-to-all-done.1.near_ref.query_ref), channel_id=1, source_target_pairs={{0,8},{8,0},{1,9},{9,1},{2,10},{10,2},{3,11},{11,3},{4,12},{12,4},... | collective-permute-start | bytes 7864328 | tf_op jit(solution)/shard_map/ppermute | solution.py:45
  75.4 4.3 %copy-start.5 = (f32[240,640]{1,0:T(8,128)}, f32[240,640]{1,0:T(8,128)S(1)}, u32[]{:S(2)}) copy-start(f32[240,640]{1,0:T(8,128)S(1)} %get-tuple-element.51) | copy-start | bytes 1843204
  75.5 10.8 %collective-permute-start.3 = (bf16[240,640]{1,0:T(8,128)(2,1)}, bf16[240,640]{1,0:T(8,128)(2,1)}, u32[]{:S(2)}, u32[]{:S(2)}) collective-permute-start(bf16[240,640]{1,0:T(8,128)(2,1)} %get-tuple-element.54), channel_id=1, source_target_pairs={{0,64},{32,96},{64,0},{96,32},{1,65},{33,97},{65,1},{97,33},{2,66}... | collective-permute-start | bytes 921608 | tf_op jit(solution)/shard_map/ppermute | solution.py:45
  78.3 14.6 %collective-permute-start.2 = (bf16[240,640]{1,0:T(8,128)(2,1)}, bf16[240,640]{1,0:T(8,128)(2,1)}, u32[]{:S(2)}, u32[]{:S(2)}) collective-permute-start(bf16[240,640]{1,0:T(8,128)(2,1)} %get-tuple-element.53), channel_id=1, source_target_pairs={{0,96},{32,0},{64,32},{96,64},{1,97},{33,1},{65,33},{97,65},{2,98}... | collective-permute-start | bytes 921608 | tf_op jit(solution)/shard_map/ppermute | solution.py:45
  79.1 14.0 %collective-permute-start.1 = (bf16[240,640]{1,0:T(8,128)(2,1)S(1)}, bf16[240,640]{1,0:T(8,128)(2,1)}, u32[]{:S(2)}, u32[]{:S(2)}) collective-permute-start(bf16[240,640]{1,0:T(8,128)(2,1)S(1)} %get-tuple-element.52), channel_id=1, source_target_pairs={{0,32},{32,64},{64,96},{96,0},{1,33},{33,65},{65,97},{97,1},{2,34}... | collective-permute-start | bytes 921608 | tf_op jit(solution)/shard_map/ppermute | solution.py:45
  82.2 38.4 %collective-permute-start.38 = (bf16[640,1024]{1,0:T(8,128)(2,1)}, bf16[640,1024]{1,0:T(8,128)(2,1)S(1)}, u32[]{:S(2)}, u32[]{:S(2)}) collective-permute-start(bf16[640,1024]{1,0:T(8,128)(2,1)} %constant_dynamic-slice_fusion), channel_id=1, source_target_pairs={{0,1},{1,0},{2,3},{3,2},{4,5},{5,4},{6,7},{7,6},{8,9},{9,8},{10,11... | collective-permute-start | bytes 3932168 | tf_op jit(solution)/shard_map/ppermute | solution.py:45
  94.6 47.0 %copy-start.2 = (f32[1,640,640]{2,1,0:T(8,128)S(1)}, f32[1,640,640]{2,1,0:T(8,128)}, u32[]{:S(2)}) copy-start(f32[1,640,640]{2,1,0:T(8,128)} %up_ref.3) | copy-start | bytes 4915204
  94.6 47.0 %copy-start.4 = (f32[1,640,640]{2,1,0:T(8,128)S(1)}, f32[1,640,640]{2,1,0:T(8,128)}, u32[]{:S(2)}) copy-start(f32[1,640,640]{2,1,0:T(8,128)} %down_ref.3) | copy-start | bytes 4915204
  94.7 25.5 %collective-permute-start.4 = (bf16[240,640]{1,0:T(8,128)(2,1)S(1)}, bf16[240,640]{1,0:T(8,128)(2,1)S(1)}, u32[]{:S(2)}, u32[]{:S(2)}) collective-permute-start(bf16[240,640]{1,0:T(8,128)(2,1)S(1)} %convert_element_type.39), channel_id=1, source_target_pairs={{0,16},{16,0},{1,17},{17,1},{2,18},{18,2},{3,19},{19,3},{4,20},{20... | collective-permute-start | bytes 921608 | tf_op jit(solution)/shard_map/ppermute | solution.py:45
  99.0 55.7 %collective-permute-start.27 = (bf16[640,1536]{1,0:T(8,128)(2,1)S(1)}, bf16[640,1536]{1,0:T(8,128)(2,1)S(1)}, u32[]{:S(2)}, u32[]{:S(2)}) collective-permute-start(bf16[640,1536]{1,0:T(8,128)(2,1)S(1)} %constant_dynamic-slice_fusion.1), channel_id=1, source_target_pairs={{0,2},{2,4},{4,6},{6,0},{1,3},{3,5},{5,7},{7,1},{8,10},{10,12},{12... | collective-permute-start | bytes 5898248 | tf_op jit(solution)/shard_map/ppermute | solution.py:45
  99.1 57.8 %collective-permute-start.29 = (bf16[640,1536]{1,0:T(8,128)(2,1)S(1)}, bf16[640,1536]{1,0:T(8,128)(2,1)S(1)}, u32[]{:S(2)}, u32[]{:S(2)}) collective-permute-start(bf16[640,1536]{1,0:T(8,128)(2,1)S(1)} %constant_dynamic-slice_fusion.1), channel_id=1, source_target_pairs={{0,6},{2,0},{4,2},{6,4},{1,7},{3,1},{5,3},{7,5},{8,14},{10,8},{12,... | collective-permute-start | bytes 5898248 | tf_op jit(solution)/shard_map/ppermute | solution.py:45
  120.2 22.8 %copy-start.7 = (s32[4]{0:T(128)S(1)}, s32[4]{0:T(128)}, u32[]{:S(2)}) copy-start(s32[4]{0:T(128)} %copy-done.6) | copy-start | bytes 52
  120.3 8.4 %collective-permute-start.5 = (bf16[240,640]{1,0:T(8,128)(2,1)S(1)}, bf16[240,640]{1,0:T(8,128)(2,1)S(1)}, u32[]{:S(2)}, u32[]{:S(2)}) collective-permute-start(bf16[240,640]{1,0:T(8,128)(2,1)S(1)} %add_convert_fusion.1.refs_4_), channel_id=1, source_target_pairs={{0,32},{32,64},{64,96},{96,0},{1,33},{33,65},{65,97},{97,1},{2,34}... | collective-permute-start | bytes 921608 | tf_op jit(solution)/shard_map/ppermute | solution.py:45
  120.6 15.2 %collective-permute-start.6 = (bf16[240,640]{1,0:T(8,128)(2,1)S(1)}, bf16[240,640]{1,0:T(8,128)(2,1)S(1)}, u32[]{:S(2)}, u32[]{:S(2)}) collective-permute-start(bf16[240,640]{1,0:T(8,128)(2,1)S(1)} %add_convert_fusion.1.refs_4_), channel_id=1, source_target_pairs={{0,64},{32,96},{64,0},{96,32},{1,65},{33,97},{65,1},{97,33},{2,66}... | collective-permute-start | bytes 921608 | tf_op jit(solution)/shard_map/ppermute | solution.py:45
  128.7 9.7 %collective-permute-start.7 = (bf16[240,640]{1,0:T(8,128)(2,1)S(1)}, bf16[240,640]{1,0:T(8,128)(2,1)S(1)}, u32[]{:S(2)}, u32[]{:S(2)}) collective-permute-start(bf16[240,640]{1,0:T(8,128)(2,1)S(1)} %add_convert_fusion.1.refs_4_), channel_id=1, source_target_pairs={{0,96},{32,0},{64,32},{96,64},{1,97},{33,1},{65,33},{97,65},{2,98}... | collective-permute-start | bytes 921608 | tf_op jit(solution)/shard_map/ppermute | solution.py:45
  135.8 3.8 %collective-permute-start.8 = (bf16[240,640]{1,0:T(8,128)(2,1)S(1)}, bf16[240,640]{1,0:T(8,128)(2,1)S(1)}, u32[]{:S(2)}, u32[]{:S(2)}) collective-permute-start(bf16[240,640]{1,0:T(8,128)(2,1)S(1)} %add_convert_fusion.1.refs_4_), channel_id=1, source_target_pairs={{0,8},{8,0},{1,9},{9,1},{2,10},{10,2},{3,11},{11,3},{4,12},{12,4},... | collective-permute-start | bytes 921608 | tf_op jit(solution)/shard_map/ppermute | solution.py:45
  138.4 2.5 collective-permute-start.9
  139.6 1.7 collective-permute-start.10
  140.9 2.2 collective-permute-start.11
  141.3 31.5 %collective-permute-start.39 = (bf16[640,1024]{1,0:T(8,128)(2,1)S(1)}, bf16[640,1024]{1,0:T(8,128)(2,1)S(1)}, u32[]{:S(2)}, u32[]{:S(2)}) collective-permute-start(bf16[640,1024]{1,0:T(8,128)(2,1)S(1)} %collective-permute-done.38.refs_6_), channel_id=1, source_target_pairs={{0,8},{8,0},{1,9},{9,1},{2,10},{10,2},{3,11},{11,3},{4,12},{12,4},... | collective-permute-start | bytes 3932168 | tf_op jit(solution)/shard_map/ppermute | solution.py:45
  145.5 67.2 %slice-start = ((s8[6553600]{0:T(1024)(128)(4,1)}), s8[2359296]{0:T(1024)(128)(4,1)S(1)}, s32[]{:S(2)}) async-start(s8[6553600]{0:T(1024)(128)(4,1)} %bitcast.5), calls=%async_computation.2 | async-start | bytes 4718592
  153.7 59.0 %slice-start.1 = ((s8[6553600]{0:T(1024)(128)(4,1)}), s8[4194304]{0:T(1024)(128)(4,1)S(1)}, s32[]{:S(2)}) async-start(s8[6553600]{0:T(1024)(128)(4,1)} %bitcast.5), calls=%async_computation.3 | async-start | bytes 8388608
  153.7 10.3 %collective-permute-start.15 = (bf16[240,640]{1,0:T(8,128)(2,1)S(1)}, bf16[240,640]{1,0:T(8,128)(2,1)S(1)}, u32[]{:S(2)}, u32[]{:S(2)}) collective-permute-start(bf16[240,640]{1,0:T(8,128)(2,1)S(1)} %get-tuple-element.60), channel_id=1, source_target_pairs={{0,64},{32,96},{64,0},{96,32},{1,65},{33,97},{65,1},{97,33},{2,66}... | collective-permute-start | bytes 921608 | tf_op jit(solution)/shard_map/ppermute | solution.py:45
  154.8 24.2 %collective-permute-start.28 = (bf16[320,1536]{1,0:T(8,128)(2,1)S(1)}, bf16[320,1536]{1,0:T(8,128)(2,1)S(1)}, u32[]{:S(2)}, u32[]{:S(2)}) collective-permute-start(bf16[320,1536]{1,0:T(8,128)(2,1)S(1)} %slice.8), channel_id=1, source_target_pairs={{0,2},{2,4},{4,6},{6,0},{1,3},{3,5},{5,7},{7,1},{8,10},{10,12},{12... | collective-permute-start | bytes 2949128 | tf_op jit(solution)/shard_map/ppermute | solution.py:45
  155.1 15.8 %collective-permute-start.14 = (bf16[240,640]{1,0:T(8,128)(2,1)S(1)}, bf16[240,640]{1,0:T(8,128)(2,1)S(1)}, u32[]{:S(2)}, u32[]{:S(2)}) collective-permute-start(bf16[240,640]{1,0:T(8,128)(2,1)S(1)} %get-tuple-element.59), channel_id=1, source_target_pairs={{0,96},{32,0},{64,32},{96,64},{1,97},{33,1},{65,33},{97,65},{2,98}... | collective-permute-start | bytes 921608 | tf_op jit(solution)/shard_map/ppermute | solution.py:45
  156.9 14.2 %collective-permute-start.13 = (bf16[240,640]{1,0:T(8,128)(2,1)S(1)}, bf16[240,640]{1,0:T(8,128)(2,1)S(1)}, u32[]{:S(2)}, u32[]{:S(2)}) collective-permute-start(bf16[240,640]{1,0:T(8,128)(2,1)S(1)} %get-tuple-element.58), channel_id=1, source_target_pairs={{0,32},{32,64},{64,96},{96,0},{1,33},{33,65},{65,97},{97,1},{2,34}... | collective-permute-start | bytes 921608 | tf_op jit(solution)/shard_map/ppermute | solution.py:45
  157.6 14.2 %copy-start.11 = (f32[640]{0:T(1024)S(1)}, f32[640]{0:T(1024)}, u32[]{:S(2)}) copy-start(f32[640]{0:T(1024)} %param.16) | copy-start | bytes 7684
  164.0 21.7 %collective-permute-start.30 = (bf16[320,1536]{1,0:T(8,128)(2,1)S(1)}, bf16[320,1536]{1,0:T(8,128)(2,1)S(1)}, u32[]{:S(2)}, u32[]{:S(2)}) collective-permute-start(bf16[320,1536]{1,0:T(8,128)(2,1)S(1)} %slice.9), channel_id=1, source_target_pairs={{0,6},{2,0},{4,2},{6,4},{1,7},{3,1},{5,3},{7,5},{8,14},{10,8},{12,... | collective-permute-start | bytes 2949128 | tf_op jit(solution)/shard_map/ppermute | solution.py:45
  171.3 9.6 %collective-permute-start.16 = (bf16[240,640]{1,0:T(8,128)(2,1)S(1)}, bf16[240,640]{1,0:T(8,128)(2,1)S(1)}, u32[]{:S(2)}, u32[]{:S(2)}) collective-permute-start(bf16[240,640]{1,0:T(8,128)(2,1)S(1)} %convert_element_type.45), channel_id=1, source_target_pairs={{0,16},{16,0},{1,17},{17,1},{2,18},{18,2},{3,19},{19,3},{4,20},{20... | collective-permute-start | bytes 921608 | tf_op jit(solution)/shard_map/ppermute | solution.py:45
  171.8 50.0 %collective-permute-start.32 = (bf16[640,1536]{1,0:T(8,128)(2,1)S(1)}, bf16[640,1536]{1,0:T(8,128)(2,1)S(1)}, u32[]{:S(2)}, u32[]{:S(2)}) collective-permute-start(bf16[640,1536]{1,0:T(8,128)(2,1)S(1)} %collective-permute-done.27.refs_6_), channel_id=1, source_target_pairs={{0,8},{8,0},{1,9},{9,1},{2,10},{10,2},{3,11},{11,3},{4,12},{12,4},... | collective-permute-start | bytes 5898248 | tf_op jit(solution)/shard_map/ppermute | solution.py:45
  172.8 53.6 %collective-permute-start.35 = (bf16[640,1536]{1,0:T(8,128)(2,1)S(1)}, bf16[640,1536]{1,0:T(8,128)(2,1)S(1)}, u32[]{:S(2)}, u32[]{:S(2)}) collective-permute-start(bf16[640,1536]{1,0:T(8,128)(2,1)S(1)} %collective-permute-done.29.refs_9_), channel_id=1, source_target_pairs={{0,8},{8,0},{1,9},{9,1},{2,10},{10,2},{3,11},{11,3},{4,12},{12,4},... | collective-permute-start | bytes 5898248 | tf_op jit(solution)/shard_map/ppermute | solution.py:45
  178.9 8.0 %collective-permute-start.43 = (bf16[128,640]{1,0:T(8,128)(2,1)S(1)}, bf16[128,640]{1,0:T(8,128)(2,1)S(1)}, u32[]{:S(2)}, u32[]{:S(2)}) collective-permute-start(bf16[128,640]{1,0:T(8,128)(2,1)S(1)} %get-tuple-element.75.refs_3_), channel_id=1, source_target_pairs={{0,2},{2,4},{4,6},{6,0},{1,3},{3,5},{5,7},{7,1},{8,10},{10,12},{12... | collective-permute-start | bytes 491528 | tf_op jit(solution)/shard_map/ppermute | solution.py:45
  180.9 9.5 %collective-permute-start.44 = (bf16[128,640]{1,0:T(8,128)(2,1)S(1)}, bf16[128,640]{1,0:T(8,128)(2,1)S(1)}, u32[]{:S(2)}, u32[]{:S(2)}) collective-permute-start(bf16[128,640]{1,0:T(8,128)(2,1)S(1)} %get-tuple-element.76.refs_2_), channel_id=1, source_target_pairs={{0,4},{2,6},{4,0},{6,2},{1,5},{3,7},{5,1},{7,3},{8,12},{10,14},{12... | collective-permute-start | bytes 491528 | tf_op jit(solution)/shard_map/ppermute | solution.py:45
  185.8 12.2 %collective-permute-start.17 = (bf16[240,640]{1,0:T(8,128)(2,1)S(1)}, bf16[240,640]{1,0:T(8,128)(2,1)S(1)}, u32[]{:S(2)}, u32[]{:S(2)}) collective-permute-start(bf16[240,640]{1,0:T(8,128)(2,1)S(1)} %add_convert_fusion.refs_5_), channel_id=1, source_target_pairs={{0,32},{32,64},{64,96},{96,0},{1,33},{33,65},{65,97},{97,1},{2,34}... | collective-permute-start | bytes 921608 | tf_op jit(solution)/shard_map/ppermute | solution.py:45
  186.9 14.2 %collective-permute-start.18 = (bf16[240,640]{1,0:T(8,128)(2,1)S(1)}, bf16[240,640]{1,0:T(8,128)(2,1)S(1)}, u32[]{:S(2)}, u32[]{:S(2)}) collective-permute-start(bf16[240,640]{1,0:T(8,128)(2,1)S(1)} %add_convert_fusion.refs_5_), channel_id=1, source_target_pairs={{0,64},{32,96},{64,0},{96,32},{1,65},{33,97},{65,1},{97,33},{2,66}... | collective-permute-start | bytes 921608 | tf_op jit(solution)/shard_map/ppermute | solution.py:45
  190.4 4.5 %collective-permute-start.45 = (bf16[128,640]{1,0:T(8,128)(2,1)S(1)}, bf16[128,640]{1,0:T(8,128)(2,1)S(1)}, u32[]{:S(2)}, u32[]{:S(2)}) collective-permute-start(bf16[128,640]{1,0:T(8,128)(2,1)S(1)} %get-tuple-element.77.refs_1_), channel_id=1, source_target_pairs={{0,6},{2,0},{4,2},{6,4},{1,7},{3,1},{5,3},{7,5},{8,14},{10,8},{12,... | collective-permute-start | bytes 491528 | tf_op jit(solution)/shard_map/ppermute | solution.py:45
  194.9 9.5 %collective-permute-start.19 = (bf16[240,640]{1,0:T(8,128)(2,1)S(1)}, bf16[240,640]{1,0:T(8,128)(2,1)S(1)}, u32[]{:S(2)}, u32[]{:S(2)}) collective-permute-start(bf16[240,640]{1,0:T(8,128)(2,1)S(1)} %add_convert_fusion.refs_5_), channel_id=1, source_target_pairs={{0,96},{32,0},{64,32},{96,64},{1,97},{33,1},{65,33},{97,65},{2,98}... | collective-permute-start | bytes 921608 | tf_op jit(solution)/shard_map/ppermute | solution.py:45
  198.0 8.9 %collective-permute-start.20 = (bf16[240,640]{1,0:T(8,128)(2,1)S(1)}, bf16[240,640]{1,0:T(8,128)(2,1)S(1)}, u32[]{:S(2)}, u32[]{:S(2)}) collective-permute-start(bf16[240,640]{1,0:T(8,128)(2,1)S(1)} %add_convert_fusion.refs_5_), channel_id=1, source_target_pairs={{0,8},{8,0},{1,9},{9,1},{2,10},{10,2},{3,11},{11,3},{4,12},{12,4},... | collective-permute-start | bytes 921608 | tf_op jit(solution)/shard_map/ppermute | solution.py:45
  201.1 5.7 %collective-permute-start.21 = (bf16[240,640]{1,0:T(8,128)(2,1)S(1)}, bf16[240,640]{1,0:T(8,128)(2,1)S(1)}, u32[]{:S(2)}, u32[]{:S(2)}) collective-permute-start(bf16[240,640]{1,0:T(8,128)(2,1)S(1)} %collective-permute-done.17.refs_6_), channel_id=1, source_target_pairs={{0,8},{8,0},{1,9},{9,1},{2,10},{10,2},{3,11},{11,3},{4,12},{12,4},... | collective-permute-start | bytes 921608 | tf_op jit(solution)/shard_map/ppermute | solution.py:45
  204.4 18.9 %collective-permute-start.33 = (bf16[320,1536]{1,0:T(8,128)(2,1)S(1)}, bf16[320,1536]{1,0:T(8,128)(2,1)S(1)}, u32[]{:S(2)}, u32[]{:S(2)}) collective-permute-start(bf16[320,1536]{1,0:T(8,128)(2,1)S(1)} %collective-permute-done.28.refs_7_), channel_id=1, source_target_pairs={{0,8},{8,0},{1,9},{9,1},{2,10},{10,2},{3,11},{11,3},{4,12},{12,4},... | collective-permute-start | bytes 2949128 | tf_op jit(solution)/shard_map/ppermute | solution.py:45
  206.9 19.6 %collective-permute-start.34 = (bf16[320,1536]{1,0:T(8,128)(2,1)S(1)}, bf16[320,1536]{1,0:T(8,128)(2,1)S(1)}, u32[]{:S(2)}, u32[]{:S(2)}) collective-permute-start(bf16[320,1536]{1,0:T(8,128)(2,1)S(1)} %collective-permute-done.30.refs_8_), channel_id=1, source_target_pairs={{0,8},{8,0},{1,9},{9,1},{2,10},{10,2},{3,11},{11,3},{4,12},{12,4},... | collective-permute-start | bytes 2949128 | tf_op jit(solution)/shard_map/ppermute | solution.py:45
  206.9 4.0 %collective-permute-start.22 = (bf16[240,640]{1,0:T(8,128)(2,1)S(1)}, bf16[240,640]{1,0:T(8,128)(2,1)S(1)}, u32[]{:S(2)}, u32[]{:S(2)}) collective-permute-start(bf16[240,640]{1,0:T(8,128)(2,1)S(1)} %collective-permute-done.18.refs_7_), channel_id=1, source_target_pairs={{0,8},{8,0},{1,9},{9,1},{2,10},{10,2},{3,11},{11,3},{4,12},{12,4},... | collective-permute-start | bytes 921608 | tf_op jit(solution)/shard_map/ppermute | solution.py:45
  210.9 1.6 collective-permute-start.23
  212.5 17.9 %collective-permute-start.48 = (bf16[256,640]{1,0:T(8,128)(2,1)S(1)}, bf16[256,640]{1,0:T(8,128)(2,1)S(1)}, u32[]{:S(2)}, u32[]{:S(2)}) collective-permute-start(bf16[256,640]{1,0:T(8,128)(2,1)S(1)} %get-tuple-element.82), channel_id=1, source_target_pairs={{0,1},{1,0},{2,3},{3,2},{4,5},{5,4},{6,7},{7,6},{8,9},{9,8},{10,11... | collective-permute-start | bytes 983048 | tf_op jit(solution)/shard_map/ppermute | solution.py:45
  221.8 12.6 %collective-permute-start.24 = (bf16[128,640]{1,0:T(8,128)(2,1)S(1)}, bf16[128,640]{1,0:T(8,128)(2,1)S(1)}, u32[]{:S(2)}, u32[]{:S(2)}) collective-permute-start(bf16[128,640]{1,0:T(8,128)(2,1)S(1)} %get-tuple-element.62.refs_3_), channel_id=1, source_target_pairs={{0,2},{2,4},{4,6},{6,0},{1,3},{3,5},{5,7},{7,1},{8,10},{10,12},{12... | collective-permute-start | bytes 491528 | tf_op jit(solution)/shard_map/ppermute | solution.py:45
  223.4 11.9 %collective-permute-start.25 = (bf16[128,640]{1,0:T(8,128)(2,1)S(1)}, bf16[128,640]{1,0:T(8,128)(2,1)S(1)}, u32[]{:S(2)}, u32[]{:S(2)}) collective-permute-start(bf16[128,640]{1,0:T(8,128)(2,1)S(1)} %get-tuple-element.63.refs_2_), channel_id=1, source_target_pairs={{0,4},{2,6},{4,0},{6,2},{1,5},{3,7},{5,1},{7,3},{8,12},{10,14},{12... | collective-permute-start | bytes 491528 | tf_op jit(solution)/shard_map/ppermute | solution.py:45
  226.4 9.6 %collective-permute-start.26 = (bf16[128,640]{1,0:T(8,128)(2,1)S(1)}, bf16[128,640]{1,0:T(8,128)(2,1)S(1)}, u32[]{:S(2)}, u32[]{:S(2)}) collective-permute-start(bf16[128,640]{1,0:T(8,128)(2,1)S(1)} %get-tuple-element.64.refs_1_), channel_id=1, source_target_pairs={{0,6},{2,0},{4,2},{6,4},{1,7},{3,1},{5,3},{7,5},{8,14},{10,8},{12,... | collective-permute-start | bytes 491528 | tf_op jit(solution)/shard_map/ppermute | solution.py:45
  226.4 15.1 %collective-permute-start.37 = (bf16[256,640]{1,0:T(8,128)(2,1)S(1)}, bf16[256,640]{1,0:T(8,128)(2,1)S(1)}, u32[]{:S(2)}, u32[]{:S(2)}) collective-permute-start(bf16[256,640]{1,0:T(8,128)(2,1)S(1)} %get-tuple-element.69), channel_id=1, source_target_pairs={{0,1},{1,0},{2,3},{3,2},{4,5},{5,4},{6,7},{7,6},{8,9},{9,8},{10,11... | collective-permute-start | bytes 983048 | tf_op jit(solution)/shard_map/ppermute | solution.py:45
  230.4 14.4 %collective-permute-start.46 = (bf16[64,1536]{1,0:T(8,128)(2,1)S(1)}, bf16[64,1536]{1,0:T(8,128)(2,1)S(1)}, u32[]{:S(2)}, u32[]{:S(2)}) collective-permute-start(bf16[64,1536]{1,0:T(8,128)(2,1)S(1)} %get-tuple-element.79), channel_id=1, source_target_pairs={{0,1},{1,0},{2,3},{3,2},{4,5},{5,4},{6,7},{7,6},{8,9},{9,8},{10,11... | collective-permute-start | bytes 589832 | tf_op jit(solution)/shard_map/ppermute | solution.py:45
  234.4 13.2 %collective-permute-start.47 = (bf16[64,1536]{1,0:T(8,128)(2,1)S(1)}, bf16[64,1536]{1,0:T(8,128)(2,1)S(1)}, u32[]{:S(2)}, u32[]{:S(2)}) collective-permute-start(bf16[64,1536]{1,0:T(8,128)(2,1)S(1)} %get-tuple-element.81), channel_id=1, source_target_pairs={{0,1},{1,0},{2,3},{3,2},{4,5},{5,4},{6,7},{7,6},{8,9},{9,8},{10,11... | collective-permute-start | bytes 589832 | tf_op jit(solution)/shard_map/ppermute | solution.py:45
  235.3 12.3 %collective-permute-start.49 = (bf16[64,2048]{1,0:T(8,128)(2,1)S(1)}, bf16[64,2048]{1,0:T(8,128)(2,1)S(1)}, u32[]{:S(2)}, u32[]{:S(2)}) collective-permute-start(bf16[64,2048]{1,0:T(8,128)(2,1)S(1)} %get-tuple-element.84), channel_id=1, source_target_pairs={{0,6},{2,0},{4,2},{6,4},{1,7},{3,1},{5,3},{7,5},{8,14},{10,8},{12,... | collective-permute-start | bytes 786440 | tf_op jit(solution)/shard_map/ppermute | solution.py:45
  236.0 15.3 %collective-permute-start.50 = (bf16[64,2048]{1,0:T(8,128)(2,1)S(1)}, bf16[64,2048]{1,0:T(8,128)(2,1)S(1)}, u32[]{:S(2)}, u32[]{:S(2)}) collective-permute-start(bf16[64,2048]{1,0:T(8,128)(2,1)S(1)} %get-tuple-element.85), channel_id=1, source_target_pairs={{0,4},{2,6},{4,0},{6,2},{1,5},{3,7},{5,1},{7,3},{8,12},{10,14},{12... | collective-permute-start | bytes 786440 | tf_op jit(solution)/shard_map/ppermute | solution.py:45
  241.5 10.6 %collective-permute-start.51 = (bf16[64,2048]{1,0:T(8,128)(2,1)S(1)}, bf16[64,2048]{1,0:T(8,128)(2,1)S(1)}, u32[]{:S(2)}, u32[]{:S(2)}) collective-permute-start(bf16[64,2048]{1,0:T(8,128)(2,1)S(1)} %get-tuple-element.86), channel_id=1, source_target_pairs={{0,2},{2,4},{4,6},{6,0},{1,3},{3,5},{5,7},{7,1},{8,10},{10,12},{12... | collective-permute-start | bytes 786440 | tf_op jit(solution)/shard_map/ppermute | solution.py:45
  244.8 13.5 %collective-permute-start.40 = (bf16[64,2048]{1,0:T(8,128)(2,1)S(1)}, bf16[64,2048]{1,0:T(8,128)(2,1)S(1)}, u32[]{:S(2)}, u32[]{:S(2)}) collective-permute-start(bf16[64,2048]{1,0:T(8,128)(2,1)S(1)} %get-tuple-element.71), channel_id=1, source_target_pairs={{0,6},{2,0},{4,2},{6,4},{1,7},{3,1},{5,3},{7,5},{8,14},{10,8},{12,... | collective-permute-start | bytes 786440 | tf_op jit(solution)/shard_map/ppermute | solution.py:45
  247.6 10.8 %collective-permute-start.41 = (bf16[64,2048]{1,0:T(8,128)(2,1)S(1)}, bf16[64,2048]{1,0:T(8,128)(2,1)S(1)}, u32[]{:S(2)}, u32[]{:S(2)}) collective-permute-start(bf16[64,2048]{1,0:T(8,128)(2,1)S(1)} %get-tuple-element.72), channel_id=1, source_target_pairs={{0,4},{2,6},{4,0},{6,2},{1,5},{3,7},{5,1},{7,3},{8,12},{10,14},{12... | collective-permute-start | bytes 786440 | tf_op jit(solution)/shard_map/ppermute | solution.py:45
  247.6 15.2 %collective-permute-start.42 = (bf16[64,2048]{1,0:T(8,128)(2,1)S(1)}, bf16[64,2048]{1,0:T(8,128)(2,1)S(1)}, u32[]{:S(2)}, u32[]{:S(2)}) collective-permute-start(bf16[64,2048]{1,0:T(8,128)(2,1)S(1)} %get-tuple-element.73), channel_id=1, source_target_pairs={{0,2},{2,4},{4,6},{6,0},{1,3},{3,5},{5,7},{7,1},{8,10},{10,12},{12... | collective-permute-start | bytes 786440 | tf_op jit(solution)/shard_map/ppermute | solution.py:45
  251.3 4.9 %collective-permute-start.31 = (bf16[64,1536]{1,0:T(8,128)(2,1)S(1)}, bf16[64,1536]{1,0:T(8,128)(2,1)S(1)}, u32[]{:S(2)}, u32[]{:S(2)}) collective-permute-start(bf16[64,1536]{1,0:T(8,128)(2,1)S(1)} %get-tuple-element.66), channel_id=1, source_target_pairs={{0,1},{1,0},{2,3},{3,2},{4,5},{5,4},{6,7},{7,6},{8,9},{9,8},{10,11... | collective-permute-start | bytes 589832 | tf_op jit(solution)/shard_map/ppermute | solution.py:45
  252.1 6.2 %collective-permute-start.36 = (bf16[64,1536]{1,0:T(8,128)(2,1)S(1)}, bf16[64,1536]{1,0:T(8,128)(2,1)S(1)}, u32[]{:S(2)}, u32[]{:S(2)}) collective-permute-start(bf16[64,1536]{1,0:T(8,128)(2,1)S(1)} %get-tuple-element.68), channel_id=1, source_target_pairs={{0,1},{1,0},{2,3},{3,2},{4,5},{5,4},{6,7},{7,6},{8,9},{9,8},{10,11... | collective-permute-start | bytes 589832 | tf_op jit(solution)/shard_map/ppermute | solution.py:45
  (4 other events, 5.0 us)

commit v3 on v2

--- a/solution.py
+++ b/solution.py
@@ -235,7 +235,7 @@
 
 
 def grads_kernel(place_ref, high_ref, low_ref, near_ref, far_ref, *refs):
-    outs, (tokens, inner, total), loaded = refs[:4], refs[4:7], refs[7:]
+    outs, (inner, total), loaded = refs[:4], refs[4:6], refs[6:]
     core, x = place_ref[0], place_ref[1]
     copies = []
     if loaded:
@@ -247,11 +247,6 @@
         high_ref, low_ref = held.at[0], held.at[1]
     for copy in copies:
         copy.start()
-    for side, ref in enumerate((near_ref, far_ref)):
-        for index in range(8):
-            rows = pl.ds((side * 8 + index) * TOK, TOK)
-            tokens[0, rows, :] = ref[index, :TOK, :]
-            tokens[1, rows, :] = ref[index, TOK : 2 * TOK, :]
     for copy in copies:
         copy.wait()
     height = high_ref.shape[1]
@@ -260,23 +255,29 @@
     def product(slot, rows):
         return nt(high_ref[slot, half, :], rows) + nt(low_ref[slot, half, :], rows)
 
-    def chunk(step, carry):
-        rows = pl.ds(pl.multiple_of(step * 256, 256), 256)
-        key = tokens[0, rows, :]
-        gate = product(0, key)
-        up = product(1, key)
-        back = product(2, tokens[1, rows, :])
-        sigma = jax.nn.sigmoid(gate)
-        silu = gate * sigma
-        inner[0, :, rows] = (back * up * sigma * (1.0 + gate * (1.0 - sigma))).astype(BF16)
-        inner[1, :, rows] = (back * silu).astype(BF16)
-        inner[2, :, rows] = (silu * up).astype(BF16)
-        return carry
-
-    lax.fori_loop(0, 4, chunk, 0)
+    for side, ref in enumerate((near_ref, far_ref)):
+
+        def chunk(step, carry, side=side, ref=ref):
+            four = pl.ds(step * 4, 4)
+            rows = pl.ds(pl.multiple_of(side * 512 + step * 256, 256), 256)
+            key = ref[four, :TOK, :].reshape(4 * TOK, HD)
+            gate = product(0, key)
+            up = product(1, key)
+            back = product(2, ref[four, TOK : 2 * TOK, :].reshape(4 * TOK, HD))
+            sigma = jax.nn.sigmoid(gate)
+            silu = gate * sigma
+            inner[0, :, rows] = (back * up * sigma * (1.0 + gate * (1.0 - sigma))).astype(BF16)
+            inner[1, :, rows] = (back * silu).astype(BF16)
+            inner[2, :, rows] = (silu * up).astype(BF16)
+            return carry
+
+        lax.fori_loop(0, 2, chunk, 0)
 
     def finish(slot, carry):
-        total[slot] = nn(inner[slot], tokens[slot // 2])
+        kind = pl.ds(pl.multiple_of(slot // 2 * TOK, TOK), TOK)
+        near = nn(inner[slot, :, :512], near_ref[:, kind, :].reshape(8 * TOK, HD))
+        far = nn(inner[slot, :, 512:], far_ref[:, kind, :].reshape(8 * TOK, HD))
+        total[slot] = near + far
         return carry
 
     lax.fori_loop(0, 3, finish, 0)
@@ -300,7 +301,6 @@
         out_specs=[pl.BlockSpec((PIECE, HD), lambda i: (0, 0))] * 4,
         out_shape=[pltpu.VMEM((PIECE, HD), F32 if d == 0 else BF16) for d in range(4)],
         scratch_shapes=[
-            pltpu.VMEM((2, 16 * TOK, HD), BF16),
             pltpu.VMEM((3, HALF, 16 * TOK), BF16),
             pltpu.VMEM((3, HALF, HD), F32),
         ]
@@ -428,6 +428,7 @@
         out_shape=[jax.ShapeDtypeStruct((TOK, LONG), BF16)] * 2,
         compiler_params=room(16),
         cost_estimate=cost(2 * 256 * 2560 * LONG, 2560 * LONG * 2),
+        name="project",
     )(place, *rows, own, *parts)
 
 

time: 265 us -> 265 us (level)
  no operation moved by 1% of the time
where the time goes in v3:
time: 265 us; the launch traced here: 264 us
  waiting for transfers between devices  115 us (43%)
  starting transfers between devices  76.3 us (29%)
  Pallas kernels  61.7 us (23%)
  local copies, waits for them, and re-layouts  9.34 us (4%)
    ppermute x52, waiting for transfers between devices, shift(): lax.ppermute(array, axis, [(i, (i + by) % size) for i in range(size)])  78.6 us
    ppermute x52, starting transfers between devices, shift(): lax.ppermute(array, axis, [(i, (i + by) % size) for i in range(size)])  65 us
    all_to_all x2, waiting for transfers between devices, to_heads(): return lax.all_to_all(array, ('z', 'yl'), 0, 0, tiled=True)  36.1 us
    pallas_call x2, Pallas kernels, grads(): pl.pallas_call(grads_kernel, grid=(1,), in_specs=[SMEM] + [held] * 2 + [p...  18.3 us
    pallas_call x4, Pallas kernels, project(): pl.pallas_call(lambda *refs: project_body(side, *refs), grid_spec=pltpu.P...  12.2 us
    all_to_all x2, starting transfers between devices, to_heads(): return lax.all_to_all(array, ('z', 'yl'), 0, 0, tiled=True)  11.3 us
    pallas_call x2, Pallas kernels, apply_weights(): pl.pallas_call(apply_kernel, grid=(1,), in_specs=[SMEM, pl.BlockSpec((3,...  7.35 us
    pallas_call x2, Pallas kernels, pair_project(): pl.pallas_call(pair_kernel, in_specs=[SMEM] + [VMEM] * 5 + [pl.BlockSpec(...  6.48 us
  transfers between devices with their start and end apart: 54, of which 22 were waited for; matrix products, arithmetic and copies ran while one was open for 2% of the time, Pallas kernels for 22%

profile of v3, /device:TPU:1, one launch (start us, length us, event | category | flops | bytes accessed | tf_op | source)
XLA Modules:
  0.0 264.2 jit_solution(14178024853059670057)
XLA Ops:
  0.0 2.5 pack_first.1
  2.5 6.9 %all-to-all-start = ((bf16[8,128,640]{2,1,0:T(8,128)(2,1)}), bf16[8,128,640]{2,1,0:T(8,128)(2,1)S(1)}, u32[]{:S(2)}, u32[]{:S(2)}) async-start(bf16[8,128,640]{2,1,0:T(8,128)(2,1)} %pack_first.1), calls=%async_computation | async-start | bytes 2621440 | tf_op jit(solution)/shard_map/all_to_all | solution.py:49
  9.4 3.5 %pack_second.1 = bf16[8,256,640]{2,1,0:T(8,128)(2,1)} custom-call(bf16[2,64,5120]{2,1,0:T(8,128)(2,1)} %key_ref.3, bf16[2,64,5120]{2,1,0:T(8,128)(2,1)} %value_ref.3, bf16[2,8,64]{2,1,0:T(8,128)(2,1)} %bitcast.8, bf16[2,64,5120]{2,1,0:T(8,128)(2,1)} %query_ref.1), custom_call_target="tpu_custom_call" | custom-call | flops 1048576 | bytes 5242880 | tf_op jit(solution)/shard_map/pack_second/pallas_call | solution.py:111
  12.9 14.2 %all-to-all-done.near_ref = bf16[8,128,640]{2,1,0:T(8,128)(2,1)S(1)} async-done(((bf16[8,128,640]{2,1,0:T(8,128)(2,1)}), bf16[8,128,640]{2,1,0:T(8,128)(2,1)S(1)}, u32[]{:S(2)}, u32[]{:S(2)}) %all-to-all-start) | async-done | bytes 1310752 | tf_op jit(solution)/shard_map/all_to_all | solution.py:49
  27.1 4.4 %all-to-all-start.1 = ((bf16[8,256,640]{2,1,0:T(8,128)(2,1)}), bf16[8,256,640]{2,1,0:T(8,128)(2,1)}, u32[]{:S(2)}, u32[]{:S(2)}) async-start(bf16[8,256,640]{2,1,0:T(8,128)(2,1)} %pack_second.1), calls=%async_computation.1 | async-start | bytes 5242880 | tf_op jit(solution)/shard_map/all_to_all | solution.py:49
  31.5 1.9 collective-permute-start
  33.5 1.4 copy-done.1
  34.9 1.4 copy-done.3
  36.4 2.0 start_half.1
  40.5 21.9 %all-to-all-done.1.near_ref.query_ref = bf16[8,256,640]{2,1,0:T(8,128)(2,1)} async-done(((bf16[8,256,640]{2,1,0:T(8,128)(2,1)}), bf16[8,256,640]{2,1,0:T(8,128)(2,1)}, u32[]{:S(2)}, u32[]{:S(2)}) %all-to-all-start.1) | async-done | bytes 2621472 | tf_op jit(solution)/shard_map/all_to_all | solution.py:49
  62.4 2.7 %collective-permute-start.12 = (bf16[8,256,640]{2,1,0:T(8,128)(2,1)}, bf16[8,256,640]{2,1,0:T(8,128)(2,1)}, u32[]{:S(2)}, u32[]{:S(2)}) collective-permute-start(bf16[8,256,640]{2,1,0:T(8,128)(2,1)} %all-to-all-done.1.near_ref.query_ref), channel_id=1, source_target_pairs={{0,8},{8,0},{1,9},{9,1},{2,10},{10,2},{3,11},{11,3},{4,12},{12,4},... | collective-permute-start | bytes 7864328 | tf_op jit(solution)/shard_map/ppermute | solution.py:45
  65.1 10.3 %grads.2 = (f32[240,640]{1,0:T(8,128)S(1)}, bf16[240,640]{1,0:T(8,128)(2,1)S(1)}, bf16[240,640]{1,0:T(8,128)(2,1)}, bf16[240,640]{1,0:T(8,128)(2,1)}) custom-call(s32[4]{0:T(128)} %copy-done.6, bf16[3,320,640]{2,1,0:T(8,128)(2,1)} %copy-done.8, bf16[3,320,640]{2,1,0:T(8,128)(2,1)} %copy-done.9, bf16[8,128,640]{2,1,0:T(8,128)(2,1)} %copy-done.10, ...), custom_call_target="tpu_custom_call" | custom-call | flops 2516582400 | bytes 8388608 | tf_op jit(solution)/shard_map/grads/pallas_call | solution.py:297
  75.4 2.8 %collective-permute-start.3 = (bf16[240,640]{1,0:T(8,128)(2,1)}, bf16[240,640]{1,0:T(8,128)(2,1)}, u32[]{:S(2)}, u32[]{:S(2)}) collective-permute-start(bf16[240,640]{1,0:T(8,128)(2,1)} %get-tuple-element.54), channel_id=1, source_target_pairs={{0,64},{32,96},{64,0},{96,32},{1,65},{33,97},{65,1},{97,33},{2,66}... | collective-permute-start | bytes 921608 | tf_op jit(solution)/shard_map/ppermute | solution.py:45
  79.7 2.5 constant_dynamic-slice_fusion
  82.7 3.5 %collective-permute-done.3 = bf16[240,640]{1,0:T(8,128)(2,1)} collective-permute-done((bf16[240,640]{1,0:T(8,128)(2,1)}, bf16[240,640]{1,0:T(8,128)(2,1)}, u32[]{:S(2)}, u32[]{:S(2)}) %collective-permute-start.3) | collective-permute-done | bytes 307232 | tf_op jit(solution)/shard_map/ppermute | solution.py:45
  86.2 6.7 %collective-permute-done.2 = bf16[240,640]{1,0:T(8,128)(2,1)} collective-permute-done((bf16[240,640]{1,0:T(8,128)(2,1)}, bf16[240,640]{1,0:T(8,128)(2,1)}, u32[]{:S(2)}, u32[]{:S(2)}) %collective-permute-start.2) | collective-permute-done | bytes 307232 | tf_op jit(solution)/shard_map/ppermute | solution.py:45
  93.1 1.5 convert_add_fusion.1
  94.6 2.7 %collective-permute-start.4 = (bf16[240,640]{1,0:T(8,128)(2,1)S(1)}, bf16[240,640]{1,0:T(8,128)(2,1)S(1)}, u32[]{:S(2)}, u32[]{:S(2)}) collective-permute-start(bf16[240,640]{1,0:T(8,128)(2,1)S(1)} %convert_element_type.39), channel_id=1, source_target_pairs={{0,16},{16,0},{1,17},{17,1},{2,18},{18,2},{3,19},{19,3},{4,20},{20... | collective-permute-start | bytes 921608 | tf_op jit(solution)/shard_map/ppermute | solution.py:45
  97.4 1.7 constant_dynamic-slice_fusion.1
  99.1 2.7 %collective-permute-start.29 = (bf16[640,1536]{1,0:T(8,128)(2,1)S(1)}, bf16[640,1536]{1,0:T(8,128)(2,1)S(1)}, u32[]{:S(2)}, u32[]{:S(2)}) collective-permute-start(bf16[640,1536]{1,0:T(8,128)(2,1)S(1)} %constant_dynamic-slice_fusion.1), channel_id=1, source_target_pairs={{0,6},{2,0},{4,2},{6,4},{1,7},{3,1},{5,3},{7,5},{8,14},{10,8},{12,... | collective-permute-start | bytes 5898248 | tf_op jit(solution)/shard_map/ppermute | solution.py:45
  101.8 18.4 %collective-permute-done.4 = bf16[240,640]{1,0:T(8,128)(2,1)S(1)} collective-permute-done((bf16[240,640]{1,0:T(8,128)(2,1)S(1)}, bf16[240,640]{1,0:T(8,128)(2,1)S(1)}, u32[]{:S(2)}, u32[]{:S(2)}) %collective-permute-start.4) | collective-permute-done | bytes 307232 | tf_op jit(solution)/shard_map/ppermute | solution.py:45
  120.6 2.9 %collective-permute-start.6 = (bf16[240,640]{1,0:T(8,128)(2,1)S(1)}, bf16[240,640]{1,0:T(8,128)(2,1)S(1)}, u32[]{:S(2)}, u32[]{:S(2)}) collective-permute-start(bf16[240,640]{1,0:T(8,128)(2,1)S(1)} %add_convert_fusion.1.refs_4_), channel_id=1, source_target_pairs={{0,64},{32,96},{64,0},{96,32},{1,65},{33,97},{65,1},{97,33},{2,66}... | collective-permute-start | bytes 921608 | tf_op jit(solution)/shard_map/ppermute | solution.py:45
  123.6 5.1 %collective-permute-done.5.refs_5_ = bf16[240,640]{1,0:T(8,128)(2,1)S(1)} collective-permute-done((bf16[240,640]{1,0:T(8,128)(2,1)S(1)}, bf16[240,640]{1,0:T(8,128)(2,1)S(1)}, u32[]{:S(2)}, u32[]{:S(2)}) %collective-permute-start.5) | collective-permute-done | bytes 307232 | tf_op jit(solution)/shard_map/ppermute | solution.py:45
  129.5 6.3 %collective-permute-done.6.refs_6_ = bf16[240,640]{1,0:T(8,128)(2,1)S(1)} collective-permute-done((bf16[240,640]{1,0:T(8,128)(2,1)S(1)}, bf16[240,640]{1,0:T(8,128)(2,1)S(1)}, u32[]{:S(2)}, u32[]{:S(2)}) %collective-permute-start.6) | collective-permute-done | bytes 307232 | tf_op jit(solution)/shard_map/ppermute | solution.py:45
  135.8 2.6 collective-permute-start.8
  138.4 1.2 collective-permute-start.9
  141.7 1.3 start_full.1
  143.0 2.5 renorm.2
  145.5 8.0 %grads.3 = (f32[240,640]{1,0:T(8,128)S(1)}, bf16[240,640]{1,0:T(8,128)(2,1)S(1)}, bf16[240,640]{1,0:T(8,128)(2,1)S(1)}, bf16[240,640]{1,0:T(8,128)(2,1)S(1)}) custom-call(s32[4]{0:T(128)S(1)} %copy-done.7, bf16[3,640,640]{2,1,0:T(8,128)(2,1)S(1)} %get-tuple-element.55.high_ref.refs_1_, bf16[3,640,640]{2,1,0:T(8,128)(2,1)S(1)} %get-tuple-element.56.low_ref.refs_2_, ...), custom_call_target="tpu_custom_call" | custom-call | flops 2516582400 | bytes 8388608 | tf_op jit(solution)/shard_map/grads/pallas_call | solution.py:297
  154.9 1.8 collective-permute-start.14
  157.4 6.5 %collective-permute-done.15 = bf16[240,640]{1,0:T(8,128)(2,1)S(1)} collective-permute-done((bf16[240,640]{1,0:T(8,128)(2,1)S(1)}, bf16[240,640]{1,0:T(8,128)(2,1)S(1)}, u32[]{:S(2)}, u32[]{:S(2)}) %collective-permute-start.15) | collective-permute-done | bytes 307232 | tf_op jit(solution)/shard_map/ppermute | solution.py:45
  164.7 6.0 %collective-permute-done.14 = bf16[240,640]{1,0:T(8,128)(2,1)S(1)} collective-permute-done((bf16[240,640]{1,0:T(8,128)(2,1)S(1)}, bf16[240,640]{1,0:T(8,128)(2,1)S(1)}, u32[]{:S(2)}, u32[]{:S(2)}) %collective-permute-start.14) | collective-permute-done | bytes 307232 | tf_op jit(solution)/shard_map/ppermute | solution.py:45
  171.5 1.2 collective-permute-start.32
  172.7 3.7 %apply_weights.3 = (bf16[128,640]{1,0:T(8,128)(2,1)S(1)}, bf16[128,640]{1,0:T(8,128)(2,1)S(1)}, bf16[128,640]{1,0:T(8,128)(2,1)S(1)}, bf16[128,640]{1,0:T(8,128)(2,1)S(1)}, bf16[256,640]{1,0:T(8,128)(2,1)S(1)}) custom-call(s32[4]{0:T(128)S(1)} %copy-done.7, bf16[3,640,640]{2,1,0:T(8,128)(2,1)S(1)} %get-tuple-element.55.high_ref.refs_1_, ...), custom_call_target="tpu_custom_call" | custom-call | flops 1258291200 | bytes 5242880 | tf_op jit(solution)/shard_map/apply_weights/pallas_call | solution.py:352
  176.4 2.3 collective-permute-done.28.refs_7_
  178.7 1.9 collective-permute-done.16
  181.2 4.4 %collective-permute-done.30.refs_8_ = bf16[320,1536]{1,0:T(8,128)(2,1)S(1)} collective-permute-done((bf16[320,1536]{1,0:T(8,128)(2,1)S(1)}, bf16[320,1536]{1,0:T(8,128)(2,1)S(1)}, u32[]{:S(2)}, u32[]{:S(2)}) %collective-permute-start.30) | collective-permute-done | bytes 983072 | tf_op jit(solution)/shard_map/ppermute | solution.py:45
  185.5 1.1 collective-permute-start.17
  186.7 3.5 %collective-permute-start.18 = (bf16[240,640]{1,0:T(8,128)(2,1)S(1)}, bf16[240,640]{1,0:T(8,128)(2,1)S(1)}, u32[]{:S(2)}, u32[]{:S(2)}) collective-permute-start(bf16[240,640]{1,0:T(8,128)(2,1)S(1)} %add_convert_fusion.refs_5_), channel_id=1, source_target_pairs={{0,64},{32,96},{64,0},{96,32},{1,65},{33,97},{65,1},{97,33},{2,66}... | collective-permute-start | bytes 921608 | tf_op jit(solution)/shard_map/ppermute | solution.py:45
  190.2 1.3 collective-permute-start.45
  191.5 3.2 %collective-permute-done.45.refs_4_ = bf16[128,640]{1,0:T(8,128)(2,1)S(1)} collective-permute-done((bf16[128,640]{1,0:T(8,128)(2,1)S(1)}, bf16[128,640]{1,0:T(8,128)(2,1)S(1)}, u32[]{:S(2)}, u32[]{:S(2)}) %collective-permute-start.45) | collective-permute-done | bytes 163872 | tf_op jit(solution)/shard_map/ppermute | solution.py:45
  194.7 3.1 %collective-permute-start.19 = (bf16[240,640]{1,0:T(8,128)(2,1)S(1)}, bf16[240,640]{1,0:T(8,128)(2,1)S(1)}, u32[]{:S(2)}, u32[]{:S(2)}) collective-permute-start(bf16[240,640]{1,0:T(8,128)(2,1)S(1)} %add_convert_fusion.refs_5_), channel_id=1, source_target_pairs={{0,96},{32,0},{64,32},{96,64},{1,97},{33,1},{65,33},{97,65},{2,98}... | collective-permute-start | bytes 921608 | tf_op jit(solution)/shard_map/ppermute | solution.py:45
  197.8 3.1 %collective-permute-start.20 = (bf16[240,640]{1,0:T(8,128)(2,1)S(1)}, bf16[240,640]{1,0:T(8,128)(2,1)S(1)}, u32[]{:S(2)}, u32[]{:S(2)}) collective-permute-start(bf16[240,640]{1,0:T(8,128)(2,1)S(1)} %add_convert_fusion.refs_5_), channel_id=1, source_target_pairs={{0,8},{8,0},{1,9},{9,1},{2,10},{10,2},{3,11},{11,3},{4,12},{12,4},... | collective-permute-start | bytes 921608 | tf_op jit(solution)/shard_map/ppermute | solution.py:45
  200.9 3.3 %collective-permute-start.21 = (bf16[240,640]{1,0:T(8,128)(2,1)S(1)}, bf16[240,640]{1,0:T(8,128)(2,1)S(1)}, u32[]{:S(2)}, u32[]{:S(2)}) collective-permute-start(bf16[240,640]{1,0:T(8,128)(2,1)S(1)} %collective-permute-done.17.refs_6_), channel_id=1, source_target_pairs={{0,8},{8,0},{1,9},{9,1},{2,10},{10,2},{3,11},{11,3},{4,12},{12,4},... | collective-permute-start | bytes 921608 | tf_op jit(solution)/shard_map/ppermute | solution.py:45
  204.2 2.4 collective-permute-start.33
  207.2 3.5 %collective-permute-done.22.refs_11_ = bf16[240,640]{1,0:T(8,128)(2,1)S(1)} collective-permute-done((bf16[240,640]{1,0:T(8,128)(2,1)S(1)}, bf16[240,640]{1,0:T(8,128)(2,1)S(1)}, u32[]{:S(2)}, u32[]{:S(2)}) %collective-permute-start.22) | collective-permute-done | bytes 307232 | tf_op jit(solution)/shard_map/ppermute | solution.py:45
  211.1 1.2 collective-permute-done.23.refs_12_
  212.5 3.1 %project.6 = (bf16[64,1536]{1,0:T(8,128)(2,1)S(1)}, bf16[64,1536]{1,0:T(8,128)(2,1)S(1)}) custom-call(s32[4]{0:T(128)S(1)} %copy-done.7, bf16[128,640]{1,0:T(8,128)(2,1)S(1)} %get-tuple-element.74.refs_1_.refs_0_, bf16[128,640]{1,0:T(8,128)(2,1)S(1)} %collective-permute-done.43.refs_2_, bf16[128,640]{1,0:T(8,128)(2,1)S(1)} %collective-permute-done.44.refs_3_, ...), custom_call_target="tpu_custom_call" | custom-call | flops 2013265920 | bytes 7864320 | tf_op jit(solution)/shard_map/project/pallas_call | solution.py:414
  215.6 2.3 renorm.3.high_ref
  217.9 3.7 %apply_weights.2 = (bf16[128,640]{1,0:T(8,128)(2,1)S(1)}, bf16[128,640]{1,0:T(8,128)(2,1)S(1)}, bf16[128,640]{1,0:T(8,128)(2,1)S(1)}, bf16[128,640]{1,0:T(8,128)(2,1)S(1)}, bf16[256,640]{1,0:T(8,128)(2,1)S(1)}) custom-call(s32[4]{0:T(128)S(1)} %copy-done.7, bf16[3,640,640]{2,1,0:T(8,128)(2,1)S(1)} %renorm.3.high_ref, f32[1,640]{1,0:T(1,128)S(1)} %reshape.3.gain_ref, ...), custom_call_target="tpu_custom_call" | custom-call | flops 1258291200 | bytes 5242880 | tf_op jit(solution)/shard_map/apply_weights/pallas_call | solution.py:352
  221.6 1.6 collective-permute-start.24
  223.1 3.1 %collective-permute-start.25 = (bf16[128,640]{1,0:T(8,128)(2,1)S(1)}, bf16[128,640]{1,0:T(8,128)(2,1)S(1)}, u32[]{:S(2)}, u32[]{:S(2)}) collective-permute-start(bf16[128,640]{1,0:T(8,128)(2,1)S(1)} %get-tuple-element.63.refs_2_), channel_id=1, source_target_pairs={{0,4},{2,6},{4,0},{6,2},{1,5},{3,7},{5,1},{7,3},{8,12},{10,14},{12... | collective-permute-start | bytes 491528 | tf_op jit(solution)/shard_map/ppermute | solution.py:45
  227.1 3.1 %project.7 = (bf16[64,1536]{1,0:T(8,128)(2,1)S(1)}, bf16[64,1536]{1,0:T(8,128)(2,1)S(1)}) custom-call(s32[4]{0:T(128)S(1)} %copy-done.7, bf16[128,640]{1,0:T(8,128)(2,1)S(1)} %get-tuple-element.74.refs_1_.refs_0_, bf16[128,640]{1,0:T(8,128)(2,1)S(1)} %collective-permute-done.43.refs_2_, bf16[128,640]{1,0:T(8,128)(2,1)S(1)} %collective-permute-done.44.refs_3_, ...), custom_call_target="tpu_custom_call" | custom-call | flops 2013265920 | bytes 7864320 | tf_op jit(solution)/shard_map/project/pallas_call | solution.py:414
  230.9 3.2 %pair_project.3 = (bf16[64,2048]{1,0:T(8,128)(2,1)S(1)}, bf16[64,2048]{1,0:T(8,128)(2,1)S(1)}, bf16[64,2048]{1,0:T(8,128)(2,1)S(1)}, bf16[64,2048]{1,0:T(8,128)(2,1)S(1)}) custom-call(s32[4]{0:T(128)S(1)} %copy-done.7, bf16[128,640]{1,0:T(8,128)(2,1)S(1)} %get-tuple-element.74.refs_1_.refs_0_, bf16[128,640]{1,0:T(8,128)(2,1)S(1)} %get-tuple-element.77.refs_1_, ...), custom_call_target="tpu_custom_call" | custom-call | flops 1342177280 | bytes 5242880 | tf_op jit(solution)/shard_map/pair_project/pallas_call | solution.py:467
  235.8 2.4 collective-permute-start.50
  238.2 3.1 %project.4 = (bf16[64,1536]{1,0:T(8,128)(2,1)S(1)}, bf16[64,1536]{1,0:T(8,128)(2,1)S(1)}) custom-call(s32[4]{0:T(128)S(1)} %copy-done.7, bf16[128,640]{1,0:T(8,128)(2,1)S(1)} %get-tuple-element.61.refs_1_.refs_0_, bf16[128,640]{1,0:T(8,128)(2,1)S(1)} %collective-permute-done.24.refs_2_, bf16[128,640]{1,0:T(8,128)(2,1)S(1)} %collective-permute-done.25.refs_3_, ...), custom_call_target="tpu_custom_call" | custom-call | flops 2013265920 | bytes 7864320 | tf_op jit(solution)/shard_map/project/pallas_call | solution.py:414
  241.4 3.2 %pair_project.2 = (bf16[64,2048]{1,0:T(8,128)(2,1)S(1)}, bf16[64,2048]{1,0:T(8,128)(2,1)S(1)}, bf16[64,2048]{1,0:T(8,128)(2,1)S(1)}, bf16[64,2048]{1,0:T(8,128)(2,1)S(1)}) custom-call(s32[4]{0:T(128)S(1)} %copy-done.7, bf16[128,640]{1,0:T(8,128)(2,1)S(1)} %get-tuple-element.61.refs_1_.refs_0_, bf16[128,640]{1,0:T(8,128)(2,1)S(1)} %get-tuple-element.64.refs_1_, ...), custom_call_target="tpu_custom_call" | custom-call | flops 1342177280 | bytes 5242880 | tf_op jit(solution)/shard_map/pair_project/pallas_call | solution.py:467
  244.7 2.7 %collective-permute-start.40 = (bf16[64,2048]{1,0:T(8,128)(2,1)S(1)}, bf16[64,2048]{1,0:T(8,128)(2,1)S(1)}, u32[]{:S(2)}, u32[]{:S(2)}) collective-permute-start(bf16[64,2048]{1,0:T(8,128)(2,1)S(1)} %get-tuple-element.71), channel_id=1, source_target_pairs={{0,6},{2,0},{4,2},{6,4},{1,7},{3,1},{5,3},{7,5},{8,14},{10,8},{12,... | collective-permute-start | bytes 786440 | tf_op jit(solution)/shard_map/ppermute | solution.py:45
  248.1 3.1 %project.5 = (bf16[64,1536]{1,0:T(8,128)(2,1)S(1)}, bf16[64,1536]{1,0:T(8,128)(2,1)S(1)}) custom-call(s32[4]{0:T(128)S(1)} %copy-done.7, bf16[128,640]{1,0:T(8,128)(2,1)S(1)} %get-tuple-element.61.refs_1_.refs_0_, bf16[128,640]{1,0:T(8,128)(2,1)S(1)} %collective-permute-done.24.refs_2_, bf16[128,640]{1,0:T(8,128)(2,1)S(1)} %collective-permute-done.25.refs_3_, ...), custom_call_target="tpu_custom_call" | custom-call | flops 2013265920 | bytes 7864320 | tf_op jit(solution)/shard_map/project/pallas_call | solution.py:414
  252.7 1.6 finish.2.refs_8_
  254.3 1.7 collective-permute-done.31.refs_1_
  256.1 2.1 collective-permute-done.36.refs_3_
  258.2 4.4 %collective-permute-done.42.refs_7_ = bf16[64,2048]{1,0:T(8,128)(2,1)S(1)} collective-permute-done((bf16[64,2048]{1,0:T(8,128)(2,1)S(1)}, bf16[64,2048]{1,0:T(8,128)(2,1)S(1)}, u32[]{:S(2)}, u32[]{:S(2)}) %collective-permute-start.42) | collective-permute-done | bytes 262176 | tf_op jit(solution)/shard_map/ppermute | solution.py:45
  262.6 1.6 finish.3
  (103 shorter events, 19.0 us)
Async XLA Ops:
  2.5 24.6 %all-to-all-start = ((bf16[8,128,640]{2,1,0:T(8,128)(2,1)}), bf16[8,128,640]{2,1,0:T(8,128)(2,1)S(1)}, u32[]{:S(2)}, u32[]{:S(2)}) async-start(bf16[8,128,640]{2,1,0:T(8,128)(2,1)} %pack_first.1), calls=%async_computation | async-start | bytes 2621440 | tf_op jit(solution)/shard_map/all_to_all | solution.py:49
  12.9 20.6 %copy-start = (f32[1,640,640]{2,1,0:T(8,128)S(1)}, f32[1,640,640]{2,1,0:T(8,128)}, u32[]{:S(2)}) copy-start(f32[1,640,640]{2,1,0:T(8,128)} %gate_ref.3) | copy-start | bytes 4915204
  27.1 4.4 %copy-start.10 = (bf16[8,128,640]{2,1,0:T(8,128)(2,1)}, bf16[8,128,640]{2,1,0:T(8,128)(2,1)S(1)}, u32[]{:S(2)}) copy-start(bf16[8,128,640]{2,1,0:T(8,128)(2,1)S(1)} %all-to-all-done.near_ref) | copy-start | bytes 3932164
  27.1 35.3 %all-to-all-start.1 = ((bf16[8,256,640]{2,1,0:T(8,128)(2,1)}), bf16[8,256,640]{2,1,0:T(8,128)(2,1)}, u32[]{:S(2)}, u32[]{:S(2)}) async-start(bf16[8,256,640]{2,1,0:T(8,128)(2,1)} %pack_second.1), calls=%async_computation.1 | async-start | bytes 5242880 | tf_op jit(solution)/shard_map/all_to_all | solution.py:49
  31.5 33.6 %collective-permute-start = (bf16[8,128,640]{2,1,0:T(8,128)(2,1)S(1)}, bf16[8,128,640]{2,1,0:T(8,128)(2,1)}, u32[]{:S(2)}, u32[]{:S(2)}) collective-permute-start(bf16[8,128,640]{2,1,0:T(8,128)(2,1)S(1)} %all-to-all-done.near_ref), channel_id=1, source_target_pairs={{0,8},{8,0},{1,9},{9,1},{2,10},{10,2},{3,11},{11,3},{4,12},{12,4},... | collective-permute-start | bytes 3932168 | tf_op jit(solution)/shard_map/ppermute | solution.py:45
  36.4 2.0 copy-start.6
  62.4 83.1 %collective-permute-start.12 = (bf16[8,256,640]{2,1,0:T(8,128)(2,1)}, bf16[8,256,640]{2,1,0:T(8,128)(2,1)}, u32[]{:S(2)}, u32[]{:S(2)}) collective-permute-start(bf16[8,256,640]{2,1,0:T(8,128)(2,1)} %all-to-all-done.1.near_ref.query_ref), channel_id=1, source_target_pairs={{0,8},{8,0},{1,9},{9,1},{2,10},{10,2},{3,11},{11,3},{4,12},{12,4},... | collective-permute-start | bytes 7864328 | tf_op jit(solution)/shard_map/ppermute | solution.py:45
  75.4 4.3 %copy-start.5 = (f32[240,640]{1,0:T(8,128)}, f32[240,640]{1,0:T(8,128)S(1)}, u32[]{:S(2)}) copy-start(f32[240,640]{1,0:T(8,128)S(1)} %get-tuple-element.51) | copy-start | bytes 1843204
  75.4 10.8 %collective-permute-start.3 = (bf16[240,640]{1,0:T(8,128)(2,1)}, bf16[240,640]{1,0:T(8,128)(2,1)}, u32[]{:S(2)}, u32[]{:S(2)}) collective-permute-start(bf16[240,640]{1,0:T(8,128)(2,1)} %get-tuple-element.54), channel_id=1, source_target_pairs={{0,64},{32,96},{64,0},{96,32},{1,65},{33,97},{65,1},{97,33},{2,66}... | collective-permute-start | bytes 921608 | tf_op jit(solution)/shard_map/ppermute | solution.py:45
  78.3 14.6 %collective-permute-start.2 = (bf16[240,640]{1,0:T(8,128)(2,1)}, bf16[240,640]{1,0:T(8,128)(2,1)}, u32[]{:S(2)}, u32[]{:S(2)}) collective-permute-start(bf16[240,640]{1,0:T(8,128)(2,1)} %get-tuple-element.53), channel_id=1, source_target_pairs={{0,96},{32,0},{64,32},{96,64},{1,97},{33,1},{65,33},{97,65},{2,98}... | collective-permute-start | bytes 921608 | tf_op jit(solution)/shard_map/ppermute | solution.py:45
  79.1 14.0 %collective-permute-start.1 = (bf16[240,640]{1,0:T(8,128)(2,1)S(1)}, bf16[240,640]{1,0:T(8,128)(2,1)}, u32[]{:S(2)}, u32[]{:S(2)}) collective-permute-start(bf16[240,640]{1,0:T(8,128)(2,1)S(1)} %get-tuple-element.52), channel_id=1, source_target_pairs={{0,32},{32,64},{64,96},{96,0},{1,33},{33,65},{65,97},{97,1},{2,34}... | collective-permute-start | bytes 921608 | tf_op jit(solution)/shard_map/ppermute | solution.py:45
  82.2 38.4 %collective-permute-start.38 = (bf16[640,1024]{1,0:T(8,128)(2,1)}, bf16[640,1024]{1,0:T(8,128)(2,1)S(1)}, u32[]{:S(2)}, u32[]{:S(2)}) collective-permute-start(bf16[640,1024]{1,0:T(8,128)(2,1)} %constant_dynamic-slice_fusion), channel_id=1, source_target_pairs={{0,1},{1,0},{2,3},{3,2},{4,5},{5,4},{6,7},{7,6},{8,9},{9,8},{10,11... | collective-permute-start | bytes 3932168 | tf_op jit(solution)/shard_map/ppermute | solution.py:45
  94.6 47.0 %copy-start.2 = (f32[1,640,640]{2,1,0:T(8,128)S(1)}, f32[1,640,640]{2,1,0:T(8,128)}, u32[]{:S(2)}) copy-start(f32[1,640,640]{2,1,0:T(8,128)} %up_ref.3) | copy-start | bytes 4915204
  94.6 47.0 %copy-start.4 = (f32[1,640,640]{2,1,0:T(8,128)S(1)}, f32[1,640,640]{2,1,0:T(8,128)}, u32[]{:S(2)}) copy-start(f32[1,640,640]{2,1,0:T(8,128)} %down_ref.3) | copy-start | bytes 4915204
  94.6 25.5 %collective-permute-start.4 = (bf16[240,640]{1,0:T(8,128)(2,1)S(1)}, bf16[240,640]{1,0:T(8,128)(2,1)S(1)}, u32[]{:S(2)}, u32[]{:S(2)}) collective-permute-start(bf16[240,640]{1,0:T(8,128)(2,1)S(1)} %convert_element_type.39), channel_id=1, source_target_pairs={{0,16},{16,0},{1,17},{17,1},{2,18},{18,2},{3,19},{19,3},{4,20},{20... | collective-permute-start | bytes 921608 | tf_op jit(solution)/shard_map/ppermute | solution.py:45
  99.0 55.5 %collective-permute-start.27 = (bf16[640,1536]{1,0:T(8,128)(2,1)S(1)}, bf16[640,1536]{1,0:T(8,128)(2,1)S(1)}, u32[]{:S(2)}, u32[]{:S(2)}) collective-permute-start(bf16[640,1536]{1,0:T(8,128)(2,1)S(1)} %constant_dynamic-slice_fusion.1), channel_id=1, source_target_pairs={{0,2},{2,4},{4,6},{6,0},{1,3},{3,5},{5,7},{7,1},{8,10},{10,12},{12... | collective-permute-start | bytes 5898248 | tf_op jit(solution)/shard_map/ppermute | solution.py:45
  99.1 57.6 %collective-permute-start.29 = (bf16[640,1536]{1,0:T(8,128)(2,1)S(1)}, bf16[640,1536]{1,0:T(8,128)(2,1)S(1)}, u32[]{:S(2)}, u32[]{:S(2)}) collective-permute-start(bf16[640,1536]{1,0:T(8,128)(2,1)S(1)} %constant_dynamic-slice_fusion.1), channel_id=1, source_target_pairs={{0,6},{2,0},{4,2},{6,4},{1,7},{3,1},{5,3},{7,5},{8,14},{10,8},{12,... | collective-permute-start | bytes 5898248 | tf_op jit(solution)/shard_map/ppermute | solution.py:45
  120.2 22.8 %copy-start.7 = (s32[4]{0:T(128)S(1)}, s32[4]{0:T(128)}, u32[]{:S(2)}) copy-start(s32[4]{0:T(128)} %copy-done.6) | copy-start | bytes 52
  120.2 8.4 %collective-permute-start.5 = (bf16[240,640]{1,0:T(8,128)(2,1)S(1)}, bf16[240,640]{1,0:T(8,128)(2,1)S(1)}, u32[]{:S(2)}, u32[]{:S(2)}) collective-permute-start(bf16[240,640]{1,0:T(8,128)(2,1)S(1)} %add_convert_fusion.1.refs_4_), channel_id=1, source_target_pairs={{0,32},{32,64},{64,96},{96,0},{1,33},{33,65},{65,97},{97,1},{2,34}... | collective-permute-start | bytes 921608 | tf_op jit(solution)/shard_map/ppermute | solution.py:45
  120.6 15.2 %collective-permute-start.6 = (bf16[240,640]{1,0:T(8,128)(2,1)S(1)}, bf16[240,640]{1,0:T(8,128)(2,1)S(1)}, u32[]{:S(2)}, u32[]{:S(2)}) collective-permute-start(bf16[240,640]{1,0:T(8,128)(2,1)S(1)} %add_convert_fusion.1.refs_4_), channel_id=1, source_target_pairs={{0,64},{32,96},{64,0},{96,32},{1,65},{33,97},{65,1},{97,33},{2,66}... | collective-permute-start | bytes 921608 | tf_op jit(solution)/shard_map/ppermute | solution.py:45
  128.6 9.7 %collective-permute-start.7 = (bf16[240,640]{1,0:T(8,128)(2,1)S(1)}, bf16[240,640]{1,0:T(8,128)(2,1)S(1)}, u32[]{:S(2)}, u32[]{:S(2)}) collective-permute-start(bf16[240,640]{1,0:T(8,128)(2,1)S(1)} %add_convert_fusion.1.refs_4_), channel_id=1, source_target_pairs={{0,96},{32,0},{64,32},{96,64},{1,97},{33,1},{65,33},{97,65},{2,98}... | collective-permute-start | bytes 921608 | tf_op jit(solution)/shard_map/ppermute | solution.py:45
  135.8 3.8 %collective-permute-start.8 = (bf16[240,640]{1,0:T(8,128)(2,1)S(1)}, bf16[240,640]{1,0:T(8,128)(2,1)S(1)}, u32[]{:S(2)}, u32[]{:S(2)}) collective-permute-start(bf16[240,640]{1,0:T(8,128)(2,1)S(1)} %add_convert_fusion.1.refs_4_), channel_id=1, source_target_pairs={{0,8},{8,0},{1,9},{9,1},{2,10},{10,2},{3,11},{11,3},{4,12},{12,4},... | collective-permute-start | bytes 921608 | tf_op jit(solution)/shard_map/ppermute | solution.py:45
  138.4 2.5 collective-permute-start.9
  139.6 1.7 collective-permute-start.10
  140.8 2.2 collective-permute-start.11
  141.3 31.4 %collective-permute-start.39 = (bf16[640,1024]{1,0:T(8,128)(2,1)S(1)}, bf16[640,1024]{1,0:T(8,128)(2,1)S(1)}, u32[]{:S(2)}, u32[]{:S(2)}) collective-permute-start(bf16[640,1024]{1,0:T(8,128)(2,1)S(1)} %collective-permute-done.38.refs_6_), channel_id=1, source_target_pairs={{0,8},{8,0},{1,9},{9,1},{2,10},{10,2},{3,11},{11,3},{4,12},{12,4},... | collective-permute-start | bytes 3932168 | tf_op jit(solution)/shard_map/ppermute | solution.py:45
  145.5 67.1 %slice-start = ((s8[6553600]{0:T(1024)(128)(4,1)}), s8[2359296]{0:T(1024)(128)(4,1)S(1)}, s32[]{:S(2)}) async-start(s8[6553600]{0:T(1024)(128)(4,1)} %bitcast.5), calls=%async_computation.2 | async-start | bytes 4718592
  153.5 59.1 %slice-start.1 = ((s8[6553600]{0:T(1024)(128)(4,1)}), s8[4194304]{0:T(1024)(128)(4,1)S(1)}, s32[]{:S(2)}) async-start(s8[6553600]{0:T(1024)(128)(4,1)} %bitcast.5), calls=%async_computation.3 | async-start | bytes 8388608
  153.5 10.3 %collective-permute-start.15 = (bf16[240,640]{1,0:T(8,128)(2,1)S(1)}, bf16[240,640]{1,0:T(8,128)(2,1)S(1)}, u32[]{:S(2)}, u32[]{:S(2)}) collective-permute-start(bf16[240,640]{1,0:T(8,128)(2,1)S(1)} %get-tuple-element.60), channel_id=1, source_target_pairs={{0,64},{32,96},{64,0},{96,32},{1,65},{33,97},{65,1},{97,33},{2,66}... | collective-permute-start | bytes 921608 | tf_op jit(solution)/shard_map/ppermute | solution.py:45
  154.6 24.2 %collective-permute-start.28 = (bf16[320,1536]{1,0:T(8,128)(2,1)S(1)}, bf16[320,1536]{1,0:T(8,128)(2,1)S(1)}, u32[]{:S(2)}, u32[]{:S(2)}) collective-permute-start(bf16[320,1536]{1,0:T(8,128)(2,1)S(1)} %slice.8), channel_id=1, source_target_pairs={{0,2},{2,4},{4,6},{6,0},{1,3},{3,5},{5,7},{7,1},{8,10},{10,12},{12... | collective-permute-start | bytes 2949128 | tf_op jit(solution)/shard_map/ppermute | solution.py:45
  154.9 15.8 %collective-permute-start.14 = (bf16[240,640]{1,0:T(8,128)(2,1)S(1)}, bf16[240,640]{1,0:T(8,128)(2,1)S(1)}, u32[]{:S(2)}, u32[]{:S(2)}) collective-permute-start(bf16[240,640]{1,0:T(8,128)(2,1)S(1)} %get-tuple-element.59), channel_id=1, source_target_pairs={{0,96},{32,0},{64,32},{96,64},{1,97},{33,1},{65,33},{97,65},{2,98}... | collective-permute-start | bytes 921608 | tf_op jit(solution)/shard_map/ppermute | solution.py:45
  156.7 14.1 %collective-permute-start.13 = (bf16[240,640]{1,0:T(8,128)(2,1)S(1)}, bf16[240,640]{1,0:T(8,128)(2,1)S(1)}, u32[]{:S(2)}, u32[]{:S(2)}) collective-permute-start(bf16[240,640]{1,0:T(8,128)(2,1)S(1)} %get-tuple-element.58), channel_id=1, source_target_pairs={{0,32},{32,64},{64,96},{96,0},{1,33},{33,65},{65,97},{97,1},{2,34}... | collective-permute-start | bytes 921608 | tf_op jit(solution)/shard_map/ppermute | solution.py:45
  157.3 14.1 %copy-start.11 = (f32[640]{0:T(1024)S(1)}, f32[640]{0:T(1024)}, u32[]{:S(2)}) copy-start(f32[640]{0:T(1024)} %param.16) | copy-start | bytes 7684
  163.8 21.7 %collective-permute-start.30 = (bf16[320,1536]{1,0:T(8,128)(2,1)S(1)}, bf16[320,1536]{1,0:T(8,128)(2,1)S(1)}, u32[]{:S(2)}, u32[]{:S(2)}) collective-permute-start(bf16[320,1536]{1,0:T(8,128)(2,1)S(1)} %slice.9), channel_id=1, source_target_pairs={{0,6},{2,0},{4,2},{6,4},{1,7},{3,1},{5,3},{7,5},{8,14},{10,8},{12,... | collective-permute-start | bytes 2949128 | tf_op jit(solution)/shard_map/ppermute | solution.py:45
  171.1 9.6 %collective-permute-start.16 = (bf16[240,640]{1,0:T(8,128)(2,1)S(1)}, bf16[240,640]{1,0:T(8,128)(2,1)S(1)}, u32[]{:S(2)}, u32[]{:S(2)}) collective-permute-start(bf16[240,640]{1,0:T(8,128)(2,1)S(1)} %convert_element_type.45), channel_id=1, source_target_pairs={{0,16},{16,0},{1,17},{17,1},{2,18},{18,2},{3,19},{19,3},{4,20},{20... | collective-permute-start | bytes 921608 | tf_op jit(solution)/shard_map/ppermute | solution.py:45
  171.5 50.1 %collective-permute-start.32 = (bf16[640,1536]{1,0:T(8,128)(2,1)S(1)}, bf16[640,1536]{1,0:T(8,128)(2,1)S(1)}, u32[]{:S(2)}, u32[]{:S(2)}) collective-permute-start(bf16[640,1536]{1,0:T(8,128)(2,1)S(1)} %collective-permute-done.27.refs_6_), channel_id=1, source_target_pairs={{0,8},{8,0},{1,9},{9,1},{2,10},{10,2},{3,11},{11,3},{4,12},{12,4},... | collective-permute-start | bytes 5898248 | tf_op jit(solution)/shard_map/ppermute | solution.py:45
  172.6 53.6 %collective-permute-start.35 = (bf16[640,1536]{1,0:T(8,128)(2,1)S(1)}, bf16[640,1536]{1,0:T(8,128)(2,1)S(1)}, u32[]{:S(2)}, u32[]{:S(2)}) collective-permute-start(bf16[640,1536]{1,0:T(8,128)(2,1)S(1)} %collective-permute-done.29.refs_9_), channel_id=1, source_target_pairs={{0,8},{8,0},{1,9},{9,1},{2,10},{10,2},{3,11},{11,3},{4,12},{12,4},... | collective-permute-start | bytes 5898248 | tf_op jit(solution)/shard_map/ppermute | solution.py:45
  178.7 8.0 %collective-permute-start.43 = (bf16[128,640]{1,0:T(8,128)(2,1)S(1)}, bf16[128,640]{1,0:T(8,128)(2,1)S(1)}, u32[]{:S(2)}, u32[]{:S(2)}) collective-permute-start(bf16[128,640]{1,0:T(8,128)(2,1)S(1)} %get-tuple-element.75.refs_3_), channel_id=1, source_target_pairs={{0,2},{2,4},{4,6},{6,0},{1,3},{3,5},{5,7},{7,1},{8,10},{10,12},{12... | collective-permute-start | bytes 491528 | tf_op jit(solution)/shard_map/ppermute | solution.py:45
  180.6 9.6 %collective-permute-start.44 = (bf16[128,640]{1,0:T(8,128)(2,1)S(1)}, bf16[128,640]{1,0:T(8,128)(2,1)S(1)}, u32[]{:S(2)}, u32[]{:S(2)}) collective-permute-start(bf16[128,640]{1,0:T(8,128)(2,1)S(1)} %get-tuple-element.76.refs_2_), channel_id=1, source_target_pairs={{0,4},{2,6},{4,0},{6,2},{1,5},{3,7},{5,1},{7,3},{8,12},{10,14},{12... | collective-permute-start | bytes 491528 | tf_op jit(solution)/shard_map/ppermute | solution.py:45
  185.5 12.3 %collective-permute-start.17 = (bf16[240,640]{1,0:T(8,128)(2,1)S(1)}, bf16[240,640]{1,0:T(8,128)(2,1)S(1)}, u32[]{:S(2)}, u32[]{:S(2)}) collective-permute-start(bf16[240,640]{1,0:T(8,128)(2,1)S(1)} %add_convert_fusion.refs_5_), channel_id=1, source_target_pairs={{0,32},{32,64},{64,96},{96,0},{1,33},{33,65},{65,97},{97,1},{2,34}... | collective-permute-start | bytes 921608 | tf_op jit(solution)/shard_map/ppermute | solution.py:45
  186.7 14.2 %collective-permute-start.18 = (bf16[240,640]{1,0:T(8,128)(2,1)S(1)}, bf16[240,640]{1,0:T(8,128)(2,1)S(1)}, u32[]{:S(2)}, u32[]{:S(2)}) collective-permute-start(bf16[240,640]{1,0:T(8,128)(2,1)S(1)} %add_convert_fusion.refs_5_), channel_id=1, source_target_pairs={{0,64},{32,96},{64,0},{96,32},{1,65},{33,97},{65,1},{97,33},{2,66}... | collective-permute-start | bytes 921608 | tf_op jit(solution)/shard_map/ppermute | solution.py:45
  190.2 4.5 %collective-permute-start.45 = (bf16[128,640]{1,0:T(8,128)(2,1)S(1)}, bf16[128,640]{1,0:T(8,128)(2,1)S(1)}, u32[]{:S(2)}, u32[]{:S(2)}) collective-permute-start(bf16[128,640]{1,0:T(8,128)(2,1)S(1)} %get-tuple-element.77.refs_1_), channel_id=1, source_target_pairs={{0,6},{2,0},{4,2},{6,4},{1,7},{3,1},{5,3},{7,5},{8,14},{10,8},{12,... | collective-permute-start | bytes 491528 | tf_op jit(solution)/shard_map/ppermute | solution.py:45
  194.7 9.6 %collective-permute-start.19 = (bf16[240,640]{1,0:T(8,128)(2,1)S(1)}, bf16[240,640]{1,0:T(8,128)(2,1)S(1)}, u32[]{:S(2)}, u32[]{:S(2)}) collective-permute-start(bf16[240,640]{1,0:T(8,128)(2,1)S(1)} %add_convert_fusion.refs_5_), channel_id=1, source_target_pairs={{0,96},{32,0},{64,32},{96,64},{1,97},{33,1},{65,33},{97,65},{2,98}... | collective-permute-start | bytes 921608 | tf_op jit(solution)/shard_map/ppermute | solution.py:45
  197.8 8.9 %collective-permute-start.20 = (bf16[240,640]{1,0:T(8,128)(2,1)S(1)}, bf16[240,640]{1,0:T(8,128)(2,1)S(1)}, u32[]{:S(2)}, u32[]{:S(2)}) collective-permute-start(bf16[240,640]{1,0:T(8,128)(2,1)S(1)} %add_convert_fusion.refs_5_), channel_id=1, source_target_pairs={{0,8},{8,0},{1,9},{9,1},{2,10},{10,2},{3,11},{11,3},{4,12},{12,4},... | collective-permute-start | bytes 921608 | tf_op jit(solution)/shard_map/ppermute | solution.py:45
  200.9 5.7 %collective-permute-start.21 = (bf16[240,640]{1,0:T(8,128)(2,1)S(1)}, bf16[240,640]{1,0:T(8,128)(2,1)S(1)}, u32[]{:S(2)}, u32[]{:S(2)}) collective-permute-start(bf16[240,640]{1,0:T(8,128)(2,1)S(1)} %collective-permute-done.17.refs_6_), channel_id=1, source_target_pairs={{0,8},{8,0},{1,9},{9,1},{2,10},{10,2},{3,11},{11,3},{4,12},{12,4},... | collective-permute-start | bytes 921608 | tf_op jit(solution)/shard_map/ppermute | solution.py:45
  204.2 18.9 %collective-permute-start.33 = (bf16[320,1536]{1,0:T(8,128)(2,1)S(1)}, bf16[320,1536]{1,0:T(8,128)(2,1)S(1)}, u32[]{:S(2)}, u32[]{:S(2)}) collective-permute-start(bf16[320,1536]{1,0:T(8,128)(2,1)S(1)} %collective-permute-done.28.refs_7_), channel_id=1, source_target_pairs={{0,8},{8,0},{1,9},{9,1},{2,10},{10,2},{3,11},{11,3},{4,12},{12,4},... | collective-permute-start | bytes 2949128 | tf_op jit(solution)/shard_map/ppermute | solution.py:45
  206.7 19.6 %collective-permute-start.34 = (bf16[320,1536]{1,0:T(8,128)(2,1)S(1)}, bf16[320,1536]{1,0:T(8,128)(2,1)S(1)}, u32[]{:S(2)}, u32[]{:S(2)}) collective-permute-start(bf16[320,1536]{1,0:T(8,128)(2,1)S(1)} %collective-permute-done.30.refs_8_), channel_id=1, source_target_pairs={{0,8},{8,0},{1,9},{9,1},{2,10},{10,2},{3,11},{11,3},{4,12},{12,4},... | collective-permute-start | bytes 2949128 | tf_op jit(solution)/shard_map/ppermute | solution.py:45
  206.7 4.0 %collective-permute-start.22 = (bf16[240,640]{1,0:T(8,128)(2,1)S(1)}, bf16[240,640]{1,0:T(8,128)(2,1)S(1)}, u32[]{:S(2)}, u32[]{:S(2)}) collective-permute-start(bf16[240,640]{1,0:T(8,128)(2,1)S(1)} %collective-permute-done.18.refs_7_), channel_id=1, source_target_pairs={{0,8},{8,0},{1,9},{9,1},{2,10},{10,2},{3,11},{11,3},{4,12},{12,4},... | collective-permute-start | bytes 921608 | tf_op jit(solution)/shard_map/ppermute | solution.py:45
  210.7 1.6 collective-permute-start.23
  212.3 17.9 %collective-permute-start.48 = (bf16[256,640]{1,0:T(8,128)(2,1)S(1)}, bf16[256,640]{1,0:T(8,128)(2,1)S(1)}, u32[]{:S(2)}, u32[]{:S(2)}) collective-permute-start(bf16[256,640]{1,0:T(8,128)(2,1)S(1)} %get-tuple-element.82), channel_id=1, source_target_pairs={{0,1},{1,0},{2,3},{3,2},{4,5},{5,4},{6,7},{7,6},{8,9},{9,8},{10,11... | collective-permute-start | bytes 983048 | tf_op jit(solution)/shard_map/ppermute | solution.py:45
  221.6 12.6 %collective-permute-start.24 = (bf16[128,640]{1,0:T(8,128)(2,1)S(1)}, bf16[128,640]{1,0:T(8,128)(2,1)S(1)}, u32[]{:S(2)}, u32[]{:S(2)}) collective-permute-start(bf16[128,640]{1,0:T(8,128)(2,1)S(1)} %get-tuple-element.62.refs_3_), channel_id=1, source_target_pairs={{0,2},{2,4},{4,6},{6,0},{1,3},{3,5},{5,7},{7,1},{8,10},{10,12},{12... | collective-permute-start | bytes 491528 | tf_op jit(solution)/shard_map/ppermute | solution.py:45
  223.1 11.9 %collective-permute-start.25 = (bf16[128,640]{1,0:T(8,128)(2,1)S(1)}, bf16[128,640]{1,0:T(8,128)(2,1)S(1)}, u32[]{:S(2)}, u32[]{:S(2)}) collective-permute-start(bf16[128,640]{1,0:T(8,128)(2,1)S(1)} %get-tuple-element.63.refs_2_), channel_id=1, source_target_pairs={{0,4},{2,6},{4,0},{6,2},{1,5},{3,7},{5,1},{7,3},{8,12},{10,14},{12... | collective-permute-start | bytes 491528 | tf_op jit(solution)/shard_map/ppermute | solution.py:45
  226.2 9.6 %collective-permute-start.26 = (bf16[128,640]{1,0:T(8,128)(2,1)S(1)}, bf16[128,640]{1,0:T(8,128)(2,1)S(1)}, u32[]{:S(2)}, u32[]{:S(2)}) collective-permute-start(bf16[128,640]{1,0:T(8,128)(2,1)S(1)} %get-tuple-element.64.refs_1_), channel_id=1, source_target_pairs={{0,6},{2,0},{4,2},{6,4},{1,7},{3,1},{5,3},{7,5},{8,14},{10,8},{12,... | collective-permute-start | bytes 491528 | tf_op jit(solution)/shard_map/ppermute | solution.py:45
  226.2 15.1 %collective-permute-start.37 = (bf16[256,640]{1,0:T(8,128)(2,1)S(1)}, bf16[256,640]{1,0:T(8,128)(2,1)S(1)}, u32[]{:S(2)}, u32[]{:S(2)}) collective-permute-start(bf16[256,640]{1,0:T(8,128)(2,1)S(1)} %get-tuple-element.69), channel_id=1, source_target_pairs={{0,1},{1,0},{2,3},{3,2},{4,5},{5,4},{6,7},{7,6},{8,9},{9,8},{10,11... | collective-permute-start | bytes 983048 | tf_op jit(solution)/shard_map/ppermute | solution.py:45
  230.2 14.5 %collective-permute-start.46 = (bf16[64,1536]{1,0:T(8,128)(2,1)S(1)}, bf16[64,1536]{1,0:T(8,128)(2,1)S(1)}, u32[]{:S(2)}, u32[]{:S(2)}) collective-permute-start(bf16[64,1536]{1,0:T(8,128)(2,1)S(1)} %get-tuple-element.79), channel_id=1, source_target_pairs={{0,1},{1,0},{2,3},{3,2},{4,5},{5,4},{6,7},{7,6},{8,9},{9,8},{10,11... | collective-permute-start | bytes 589832 | tf_op jit(solution)/shard_map/ppermute | solution.py:45
  234.2 13.2 %collective-permute-start.47 = (bf16[64,1536]{1,0:T(8,128)(2,1)S(1)}, bf16[64,1536]{1,0:T(8,128)(2,1)S(1)}, u32[]{:S(2)}, u32[]{:S(2)}) collective-permute-start(bf16[64,1536]{1,0:T(8,128)(2,1)S(1)} %get-tuple-element.81), channel_id=1, source_target_pairs={{0,1},{1,0},{2,3},{3,2},{4,5},{5,4},{6,7},{7,6},{8,9},{9,8},{10,11... | collective-permute-start | bytes 589832 | tf_op jit(solution)/shard_map/ppermute | solution.py:45
  235.1 12.3 %collective-permute-start.49 = (bf16[64,2048]{1,0:T(8,128)(2,1)S(1)}, bf16[64,2048]{1,0:T(8,128)(2,1)S(1)}, u32[]{:S(2)}, u32[]{:S(2)}) collective-permute-start(bf16[64,2048]{1,0:T(8,128)(2,1)S(1)} %get-tuple-element.84), channel_id=1, source_target_pairs={{0,6},{2,0},{4,2},{6,4},{1,7},{3,1},{5,3},{7,5},{8,14},{10,8},{12,... | collective-permute-start | bytes 786440 | tf_op jit(solution)/shard_map/ppermute | solution.py:45
  235.8 15.3 %collective-permute-start.50 = (bf16[64,2048]{1,0:T(8,128)(2,1)S(1)}, bf16[64,2048]{1,0:T(8,128)(2,1)S(1)}, u32[]{:S(2)}, u32[]{:S(2)}) collective-permute-start(bf16[64,2048]{1,0:T(8,128)(2,1)S(1)} %get-tuple-element.85), channel_id=1, source_target_pairs={{0,4},{2,6},{4,0},{6,2},{1,5},{3,7},{5,1},{7,3},{8,12},{10,14},{12... | collective-permute-start | bytes 786440 | tf_op jit(solution)/shard_map/ppermute | solution.py:45
  241.3 10.6 %collective-permute-start.51 = (bf16[64,2048]{1,0:T(8,128)(2,1)S(1)}, bf16[64,2048]{1,0:T(8,128)(2,1)S(1)}, u32[]{:S(2)}, u32[]{:S(2)}) collective-permute-start(bf16[64,2048]{1,0:T(8,128)(2,1)S(1)} %get-tuple-element.86), channel_id=1, source_target_pairs={{0,2},{2,4},{4,6},{6,0},{1,3},{3,5},{5,7},{7,1},{8,10},{10,12},{12... | collective-permute-start | bytes 786440 | tf_op jit(solution)/shard_map/ppermute | solution.py:45
  244.7 13.5 %collective-permute-start.40 = (bf16[64,2048]{1,0:T(8,128)(2,1)S(1)}, bf16[64,2048]{1,0:T(8,128)(2,1)S(1)}, u32[]{:S(2)}, u32[]{:S(2)}) collective-permute-start(bf16[64,2048]{1,0:T(8,128)(2,1)S(1)} %get-tuple-element.71), channel_id=1, source_target_pairs={{0,6},{2,0},{4,2},{6,4},{1,7},{3,1},{5,3},{7,5},{8,14},{10,8},{12,... | collective-permute-start | bytes 786440 | tf_op jit(solution)/shard_map/ppermute | solution.py:45
  247.4 10.8 %collective-permute-start.41 = (bf16[64,2048]{1,0:T(8,128)(2,1)S(1)}, bf16[64,2048]{1,0:T(8,128)(2,1)S(1)}, u32[]{:S(2)}, u32[]{:S(2)}) collective-permute-start(bf16[64,2048]{1,0:T(8,128)(2,1)S(1)} %get-tuple-element.72), channel_id=1, source_target_pairs={{0,4},{2,6},{4,0},{6,2},{1,5},{3,7},{5,1},{7,3},{8,12},{10,14},{12... | collective-permute-start | bytes 786440 | tf_op jit(solution)/shard_map/ppermute | solution.py:45
  247.4 15.2 %collective-permute-start.42 = (bf16[64,2048]{1,0:T(8,128)(2,1)S(1)}, bf16[64,2048]{1,0:T(8,128)(2,1)S(1)}, u32[]{:S(2)}, u32[]{:S(2)}) collective-permute-start(bf16[64,2048]{1,0:T(8,128)(2,1)S(1)} %get-tuple-element.73), channel_id=1, source_target_pairs={{0,2},{2,4},{4,6},{6,0},{1,3},{3,5},{5,7},{7,1},{8,10},{10,12},{12... | collective-permute-start | bytes 786440 | tf_op jit(solution)/shard_map/ppermute | solution.py:45
  251.2 4.9 %collective-permute-start.31 = (bf16[64,1536]{1,0:T(8,128)(2,1)S(1)}, bf16[64,1536]{1,0:T(8,128)(2,1)S(1)}, u32[]{:S(2)}, u32[]{:S(2)}) collective-permute-start(bf16[64,1536]{1,0:T(8,128)(2,1)S(1)} %get-tuple-element.66), channel_id=1, source_target_pairs={{0,1},{1,0},{2,3},{3,2},{4,5},{5,4},{6,7},{7,6},{8,9},{9,8},{10,11... | collective-permute-start | bytes 589832 | tf_op jit(solution)/shard_map/ppermute | solution.py:45
  251.9 6.3 %collective-permute-start.36 = (bf16[64,1536]{1,0:T(8,128)(2,1)S(1)}, bf16[64,1536]{1,0:T(8,128)(2,1)S(1)}, u32[]{:S(2)}, u32[]{:S(2)}) collective-permute-start(bf16[64,1536]{1,0:T(8,128)(2,1)S(1)} %get-tuple-element.68), channel_id=1, source_target_pairs={{0,1},{1,0},{2,3},{3,2},{4,5},{5,4},{6,7},{7,6},{8,9},{9,8},{10,11... | collective-permute-start | bytes 589832 | tf_op jit(solution)/shard_map/ppermute | solution.py:45
  (4 other events, 5.0 us)

commit v4 on v3

--- a/solution.py
+++ b/solution.py
@@ -480,16 +480,18 @@
     )(place, *rows, got, own, cross, cross_other)
 
 
-def finish_kernel(place_ref, *refs):
-    parts, out_ref = refs[:8], refs[-1]
+def finish_kernel(sides, place_ref, *refs):
+    out_ref = refs[-1]
+    parts = refs[: 2 * sides + 4]
     for side in range(2):
         half = place_ref[0] if side == 0 else 1 - place_ref[0]
         start = half * COLS
-        total = parts[2 * side][...].astype(F32) + parts[2 * side + 1][...].astype(F32)
-        out_ref[0, :, pl.ds(pl.multiple_of(start, 512), LONG)] = total.astype(BF16)
+        if side < sides:
+            total = parts[2 * side][...].astype(F32) + parts[2 * side + 1][...].astype(F32)
+            out_ref[0, :, pl.ds(pl.multiple_of(start, 512), LONG)] = total.astype(BF16)
         cols = slice(side * WIDTH, (side + 1) * WIDTH)
-        total = parts[4][:, cols].astype(F32)
-        for part in parts[5:8]:
+        total = parts[2 * sides][:, cols].astype(F32)
+        for part in parts[2 * sides + 1 :]:
             total = total + part[:, cols].astype(F32)
         out_ref[0, :, pl.ds(pl.multiple_of(start + LONG, 512), WIDTH)] = total.astype(BF16)
 
@@ -497,17 +499,41 @@
 def finish(block, place, parts, held=None):
     held = [] if held is None else [held]
     whole = [pl.BlockSpec(part.shape, lambda i: (0, 0)) for part in parts]
-    return pl.pallas_call(
-        finish_kernel,
+    sides = (len(parts) - 4) // 2
+    return pl.pallas_call(
+        lambda *refs: finish_kernel(sides, *refs),
         grid=(1,),
         in_specs=[SMEM] + whole + [pl.BlockSpec(memory_space=pl.ANY)] * len(held),
         out_specs=pl.BlockSpec((1, TOK, WIDE), lambda i: (block, 0, 0)),
         out_shape=jax.ShapeDtypeStruct((2, TOK, WIDE), BF16),
-        input_output_aliases={9: 0} if held else {},
+        input_output_aliases={1 + len(parts): 0} if held else {},
         compiler_params=room(16),
         cost_estimate=cost(1 << 20, 3 << 20),
         name="finish",
     )(place, *parts, *held)
+
+
+def finish_last_kernel(place_ref, keep_ref, got_ref, held_ref, out_ref, total, sem):
+    start = (1 - place_ref[0]) * COLS
+    total[...] = (keep_ref[...].astype(F32) + got_ref[...].astype(F32)).astype(BF16)
+    cols = pl.ds(pl.multiple_of(start, 512), LONG)
+    copy = pltpu.make_async_copy(total, out_ref.at[1, :, cols], sem)
+    copy.start()
+    copy.wait()
+
+
+def finish_last(place, keep, got, held):
+    return pl.pallas_call(
+        finish_last_kernel,
+        in_specs=[SMEM, VMEM, VMEM, pl.BlockSpec(memory_space=pl.ANY)],
+        out_specs=pl.BlockSpec(memory_space=pl.ANY),
+        out_shape=jax.ShapeDtypeStruct((2, TOK, WIDE), BF16),
+        scratch_shapes=[pltpu.VMEM((TOK, LONG), BF16), pltpu.SemaphoreType.DMA(())],
+        input_output_aliases={3: 0},
+        compiler_params=room(16),
+        cost_estimate=cost(1 << 18, 1 << 19),
+        name="finish_last",
+    )(place, keep, got, held)
 
 
 def per_device(queries, keys, values, rates, gate_fast, up_fast, down_fast, out_gain, out_proj):
@@ -558,7 +584,9 @@
     parts = spread(0, weights)
     out = finish(0, place, parts)
     weights = renorm(place, weights, row_norm, col_norm, total, True)
-    return finish(1, place, spread(1, weights), out)
+    parts = spread(1, weights)
+    out = finish(1, place, parts[:2] + parts[4:], out)
+    return finish_last(place, parts[2], parts[3], out)
 
 
 def solution(mesh):

time: 265 us -> 266 us (level)
  transfers between devices with their start and end apart: 54 -> 54, of which waited for: 22 -> 21; matrix products, arithmetic and copies ran while one was open for 2% -> 2% of each run, Pallas kernels for 22% -> 22%
where the time goes in v4:
time: 266 us; the launch traced here: 265 us
  waiting for transfers between devices  114 us (43%)
  starting transfers between devices  76.3 us (29%)
  Pallas kernels  62.9 us (24%)
  local copies, waits for them, and re-layouts  9.34 us (4%)
    ppermute x52, waiting for transfers between devices, shift(): lax.ppermute(array, axis, [(i, (i + by) % size) for i in range(size)])  78 us
    ppermute x52, starting transfers between devices, shift(): lax.ppermute(array, axis, [(i, (i + by) % size) for i in range(size)])  65 us
    all_to_all x2, waiting for transfers between devices, to_heads(): return lax.all_to_all(array, ('z', 'yl'), 0, 0, tiled=True)  36.1 us
    pallas_call x2, Pallas kernels, grads(): pl.pallas_call(grads_kernel, grid=(1,), in_specs=[SMEM] + [held] * 2 + [p...  18.3 us
    pallas_call x4, Pallas kernels, project(): pl.pallas_call(lambda *refs: project_body(side, *refs), grid_spec=pltpu.P...  12.2 us
    all_to_all x2, starting transfers between devices, to_heads(): return lax.all_to_all(array, ('z', 'yl'), 0, 0, tiled=True)  11.3 us
    pallas_call x2, Pallas kernels, apply_weights(): pl.pallas_call(apply_kernel, grid=(1,), in_specs=[SMEM, pl.BlockSpec((3,...  7.35 us
    pallas_call x2, Pallas kernels, pair_project(): pl.pallas_call(pair_kernel, in_specs=[SMEM] + [VMEM] * 5 + [pl.BlockSpec(...  6.48 us
  transfers between devices with their start and end apart: 54, of which 21 were waited for; matrix products, arithmetic and copies ran while one was open for 2% of the time, Pallas kernels for 22%

profile of v4, /device:TPU:1, one launch (start us, length us, event | category | flops | bytes accessed | tf_op | source)
XLA Modules:
  0.0 265.0 jit_solution(13518851735761202641)
XLA Ops:
  0.0 2.5 pack_first.1
  2.5 6.9 %all-to-all-start = ((bf16[8,128,640]{2,1,0:T(8,128)(2,1)}), bf16[8,128,640]{2,1,0:T(8,128)(2,1)S(1)}, u32[]{:S(2)}, u32[]{:S(2)}) async-start(bf16[8,128,640]{2,1,0:T(8,128)(2,1)} %pack_first.1), calls=%async_computation | async-start | bytes 2621440 | tf_op jit(solution)/shard_map/all_to_all | solution.py:49
  9.4 3.5 %pack_second.1 = bf16[8,256,640]{2,1,0:T(8,128)(2,1)} custom-call(bf16[2,64,5120]{2,1,0:T(8,128)(2,1)} %key_ref.3, bf16[2,64,5120]{2,1,0:T(8,128)(2,1)} %value_ref.3, bf16[2,8,64]{2,1,0:T(8,128)(2,1)} %bitcast.8, bf16[2,64,5120]{2,1,0:T(8,128)(2,1)} %query_ref.1), custom_call_target="tpu_custom_call" | custom-call | flops 1048576 | bytes 5242880 | tf_op jit(solution)/shard_map/pack_second/pallas_call | solution.py:111
  12.9 14.2 %all-to-all-done.near_ref = bf16[8,128,640]{2,1,0:T(8,128)(2,1)S(1)} async-done(((bf16[8,128,640]{2,1,0:T(8,128)(2,1)}), bf16[8,128,640]{2,1,0:T(8,128)(2,1)S(1)}, u32[]{:S(2)}, u32[]{:S(2)}) %all-to-all-start) | async-done | bytes 1310752 | tf_op jit(solution)/shard_map/all_to_all | solution.py:49
  27.1 4.4 %all-to-all-start.1 = ((bf16[8,256,640]{2,1,0:T(8,128)(2,1)}), bf16[8,256,640]{2,1,0:T(8,128)(2,1)}, u32[]{:S(2)}, u32[]{:S(2)}) async-start(bf16[8,256,640]{2,1,0:T(8,128)(2,1)} %pack_second.1), calls=%async_computation.1 | async-start | bytes 5242880 | tf_op jit(solution)/shard_map/all_to_all | solution.py:49
  31.5 1.9 collective-permute-start
  33.5 1.4 copy-done.1
  34.9 1.4 copy-done.3
  36.4 2.0 start_half.1
  38.4 1.1 copy-done.8
  40.5 21.9 %all-to-all-done.1.near_ref.query_ref = bf16[8,256,640]{2,1,0:T(8,128)(2,1)} async-done(((bf16[8,256,640]{2,1,0:T(8,128)(2,1)}), bf16[8,256,640]{2,1,0:T(8,128)(2,1)}, u32[]{:S(2)}, u32[]{:S(2)}) %all-to-all-start.1) | async-done | bytes 2621472 | tf_op jit(solution)/shard_map/all_to_all | solution.py:49
  62.4 2.7 %collective-permute-start.12 = (bf16[8,256,640]{2,1,0:T(8,128)(2,1)}, bf16[8,256,640]{2,1,0:T(8,128)(2,1)}, u32[]{:S(2)}, u32[]{:S(2)}) collective-permute-start(bf16[8,256,640]{2,1,0:T(8,128)(2,1)} %all-to-all-done.1.near_ref.query_ref), channel_id=1, source_target_pairs={{0,8},{8,0},{1,9},{9,1},{2,10},{10,2},{3,11},{11,3},{4,12},{12,4},... | collective-permute-start | bytes 7864328 | tf_op jit(solution)/shard_map/ppermute | solution.py:45
  65.1 10.3 %grads.2 = (f32[240,640]{1,0:T(8,128)S(1)}, bf16[240,640]{1,0:T(8,128)(2,1)S(1)}, bf16[240,640]{1,0:T(8,128)(2,1)}, bf16[240,640]{1,0:T(8,128)(2,1)}) custom-call(s32[4]{0:T(128)} %copy-done.6, bf16[3,320,640]{2,1,0:T(8,128)(2,1)} %copy-done.8, bf16[3,320,640]{2,1,0:T(8,128)(2,1)} %copy-done.9, bf16[8,128,640]{2,1,0:T(8,128)(2,1)} %copy-done.10, ...), custom_call_target="tpu_custom_call" | custom-call | flops 2516582400 | bytes 8388608 | tf_op jit(solution)/shard_map/grads/pallas_call | solution.py:297
  75.4 2.8 %collective-permute-start.3 = (bf16[240,640]{1,0:T(8,128)(2,1)}, bf16[240,640]{1,0:T(8,128)(2,1)}, u32[]{:S(2)}, u32[]{:S(2)}) collective-permute-start(bf16[240,640]{1,0:T(8,128)(2,1)} %get-tuple-element.54), channel_id=1, source_target_pairs={{0,64},{32,96},{64,0},{96,32},{1,65},{33,97},{65,1},{97,33},{2,66}... | collective-permute-start | bytes 921608 | tf_op jit(solution)/shard_map/ppermute | solution.py:45
  79.7 2.5 constant_dynamic-slice_fusion
  82.7 3.5 %collective-permute-done.3 = bf16[240,640]{1,0:T(8,128)(2,1)} collective-permute-done((bf16[240,640]{1,0:T(8,128)(2,1)}, bf16[240,640]{1,0:T(8,128)(2,1)}, u32[]{:S(2)}, u32[]{:S(2)}) %collective-permute-start.3) | collective-permute-done | bytes 307232 | tf_op jit(solution)/shard_map/ppermute | solution.py:45
  86.2 6.7 %collective-permute-done.2 = bf16[240,640]{1,0:T(8,128)(2,1)} collective-permute-done((bf16[240,640]{1,0:T(8,128)(2,1)}, bf16[240,640]{1,0:T(8,128)(2,1)}, u32[]{:S(2)}, u32[]{:S(2)}) %collective-permute-start.2) | collective-permute-done | bytes 307232 | tf_op jit(solution)/shard_map/ppermute | solution.py:45
  93.1 1.5 convert_add_fusion.1
  94.6 2.7 %collective-permute-start.4 = (bf16[240,640]{1,0:T(8,128)(2,1)S(1)}, bf16[240,640]{1,0:T(8,128)(2,1)S(1)}, u32[]{:S(2)}, u32[]{:S(2)}) collective-permute-start(bf16[240,640]{1,0:T(8,128)(2,1)S(1)} %convert_element_type.39), channel_id=1, source_target_pairs={{0,16},{16,0},{1,17},{17,1},{2,18},{18,2},{3,19},{19,3},{4,20},{20... | collective-permute-start | bytes 921608 | tf_op jit(solution)/shard_map/ppermute | solution.py:45
  97.4 1.7 constant_dynamic-slice_fusion.1
  99.1 2.7 %collective-permute-start.31 = (bf16[640,1536]{1,0:T(8,128)(2,1)S(1)}, bf16[640,1536]{1,0:T(8,128)(2,1)S(1)}, u32[]{:S(2)}, u32[]{:S(2)}) collective-permute-start(bf16[640,1536]{1,0:T(8,128)(2,1)S(1)} %constant_dynamic-slice_fusion.1), channel_id=1, source_target_pairs={{0,6},{2,0},{4,2},{6,4},{1,7},{3,1},{5,3},{7,5},{8,14},{10,8},{12,... | collective-permute-start | bytes 5898248 | tf_op jit(solution)/shard_map/ppermute | solution.py:45
  101.8 18.4 %collective-permute-done.4 = bf16[240,640]{1,0:T(8,128)(2,1)S(1)} collective-permute-done((bf16[240,640]{1,0:T(8,128)(2,1)S(1)}, bf16[240,640]{1,0:T(8,128)(2,1)S(1)}, u32[]{:S(2)}, u32[]{:S(2)}) %collective-permute-start.4) | collective-permute-done | bytes 307232 | tf_op jit(solution)/shard_map/ppermute | solution.py:45
  120.6 2.9 %collective-permute-start.6 = (bf16[240,640]{1,0:T(8,128)(2,1)S(1)}, bf16[240,640]{1,0:T(8,128)(2,1)S(1)}, u32[]{:S(2)}, u32[]{:S(2)}) collective-permute-start(bf16[240,640]{1,0:T(8,128)(2,1)S(1)} %add_convert_fusion.1.refs_4_), channel_id=1, source_target_pairs={{0,64},{32,96},{64,0},{96,32},{1,65},{33,97},{65,1},{97,33},{2,66}... | collective-permute-start | bytes 921608 | tf_op jit(solution)/shard_map/ppermute | solution.py:45
  123.6 5.1 %collective-permute-done.5.refs_5_ = bf16[240,640]{1,0:T(8,128)(2,1)S(1)} collective-permute-done((bf16[240,640]{1,0:T(8,128)(2,1)S(1)}, bf16[240,640]{1,0:T(8,128)(2,1)S(1)}, u32[]{:S(2)}, u32[]{:S(2)}) %collective-permute-start.5) | collective-permute-done | bytes 307232 | tf_op jit(solution)/shard_map/ppermute | solution.py:45
  129.5 6.3 %collective-permute-done.6.refs_6_ = bf16[240,640]{1,0:T(8,128)(2,1)S(1)} collective-permute-done((bf16[240,640]{1,0:T(8,128)(2,1)S(1)}, bf16[240,640]{1,0:T(8,128)(2,1)S(1)}, u32[]{:S(2)}, u32[]{:S(2)}) %collective-permute-start.6) | collective-permute-done | bytes 307232 | tf_op jit(solution)/shard_map/ppermute | solution.py:45
  135.8 2.6 collective-permute-start.8
  138.4 1.2 collective-permute-start.9
  141.7 1.3 start_full.1
  143.0 2.5 renorm.2
  145.5 8.0 %grads.3 = (f32[240,640]{1,0:T(8,128)S(1)}, bf16[240,640]{1,0:T(8,128)(2,1)S(1)}, bf16[240,640]{1,0:T(8,128)(2,1)S(1)}, bf16[240,640]{1,0:T(8,128)(2,1)S(1)}) custom-call(s32[4]{0:T(128)S(1)} %copy-done.7, bf16[3,640,640]{2,1,0:T(8,128)(2,1)S(1)} %get-tuple-element.55.high_ref.refs_1_, bf16[3,640,640]{2,1,0:T(8,128)(2,1)S(1)} %get-tuple-element.56.low_ref.refs_2_, ...), custom_call_target="tpu_custom_call" | custom-call | flops 2516582400 | bytes 8388608 | tf_op jit(solution)/shard_map/grads/pallas_call | solution.py:297
  154.9 1.8 collective-permute-start.14
  157.4 6.5 %collective-permute-done.15 = bf16[240,640]{1,0:T(8,128)(2,1)S(1)} collective-permute-done((bf16[240,640]{1,0:T(8,128)(2,1)S(1)}, bf16[240,640]{1,0:T(8,128)(2,1)S(1)}, u32[]{:S(2)}, u32[]{:S(2)}) %collective-permute-start.15) | collective-permute-done | bytes 307232 | tf_op jit(solution)/shard_map/ppermute | solution.py:45
  164.7 6.0 %collective-permute-done.14 = bf16[240,640]{1,0:T(8,128)(2,1)S(1)} collective-permute-done((bf16[240,640]{1,0:T(8,128)(2,1)S(1)}, bf16[240,640]{1,0:T(8,128)(2,1)S(1)}, u32[]{:S(2)}, u32[]{:S(2)}) %collective-permute-start.14) | collective-permute-done | bytes 307232 | tf_op jit(solution)/shard_map/ppermute | solution.py:45
  171.5 1.2 collective-permute-start.28
  172.7 3.7 %apply_weights.3 = (bf16[128,640]{1,0:T(8,128)(2,1)S(1)}, bf16[128,640]{1,0:T(8,128)(2,1)S(1)}, bf16[128,640]{1,0:T(8,128)(2,1)S(1)}, bf16[128,640]{1,0:T(8,128)(2,1)S(1)}, bf16[256,640]{1,0:T(8,128)(2,1)S(1)}) custom-call(s32[4]{0:T(128)S(1)} %copy-done.7, bf16[3,640,640]{2,1,0:T(8,128)(2,1)S(1)} %get-tuple-element.55.high_ref.refs_1_, ...), custom_call_target="tpu_custom_call" | custom-call | flops 1258291200 | bytes 5242880 | tf_op jit(solution)/shard_map/apply_weights/pallas_call | solution.py:352
  176.4 2.3 collective-permute-done.29.refs_7_
  178.7 1.9 collective-permute-done.16
  181.2 4.4 %collective-permute-done.32.refs_8_ = bf16[320,1536]{1,0:T(8,128)(2,1)S(1)} collective-permute-done((bf16[320,1536]{1,0:T(8,128)(2,1)S(1)}, bf16[320,1536]{1,0:T(8,128)(2,1)S(1)}, u32[]{:S(2)}, u32[]{:S(2)}) %collective-permute-start.32) | collective-permute-done | bytes 983072 | tf_op jit(solution)/shard_map/ppermute | solution.py:45
  185.5 1.1 collective-permute-start.17
  186.7 3.5 %collective-permute-start.18 = (bf16[240,640]{1,0:T(8,128)(2,1)S(1)}, bf16[240,640]{1,0:T(8,128)(2,1)S(1)}, u32[]{:S(2)}, u32[]{:S(2)}) collective-permute-start(bf16[240,640]{1,0:T(8,128)(2,1)S(1)} %add_convert_fusion.refs_5_), channel_id=1, source_target_pairs={{0,64},{32,96},{64,0},{96,32},{1,65},{33,97},{65,1},{97,33},{2,66}... | collective-permute-start | bytes 921608 | tf_op jit(solution)/shard_map/ppermute | solution.py:45
  190.2 1.3 collective-permute-start.45
  191.5 3.2 %collective-permute-done.45.refs_4_ = bf16[128,640]{1,0:T(8,128)(2,1)S(1)} collective-permute-done((bf16[128,640]{1,0:T(8,128)(2,1)S(1)}, bf16[128,640]{1,0:T(8,128)(2,1)S(1)}, u32[]{:S(2)}, u32[]{:S(2)}) %collective-permute-start.45) | collective-permute-done | bytes 163872 | tf_op jit(solution)/shard_map/ppermute | solution.py:45
  194.7 3.1 %collective-permute-start.19 = (bf16[240,640]{1,0:T(8,128)(2,1)S(1)}, bf16[240,640]{1,0:T(8,128)(2,1)S(1)}, u32[]{:S(2)}, u32[]{:S(2)}) collective-permute-start(bf16[240,640]{1,0:T(8,128)(2,1)S(1)} %add_convert_fusion.refs_5_), channel_id=1, source_target_pairs={{0,96},{32,0},{64,32},{96,64},{1,97},{33,1},{65,33},{97,65},{2,98}... | collective-permute-start | bytes 921608 | tf_op jit(solution)/shard_map/ppermute | solution.py:45
  197.8 3.1 %collective-permute-start.20 = (bf16[240,640]{1,0:T(8,128)(2,1)S(1)}, bf16[240,640]{1,0:T(8,128)(2,1)S(1)}, u32[]{:S(2)}, u32[]{:S(2)}) collective-permute-start(bf16[240,640]{1,0:T(8,128)(2,1)S(1)} %add_convert_fusion.refs_5_), channel_id=1, source_target_pairs={{0,8},{8,0},{1,9},{9,1},{2,10},{10,2},{3,11},{11,3},{4,12},{12,4},... | collective-permute-start | bytes 921608 | tf_op jit(solution)/shard_map/ppermute | solution.py:45
  200.9 3.3 %collective-permute-start.21 = (bf16[240,640]{1,0:T(8,128)(2,1)S(1)}, bf16[240,640]{1,0:T(8,128)(2,1)S(1)}, u32[]{:S(2)}, u32[]{:S(2)}) collective-permute-start(bf16[240,640]{1,0:T(8,128)(2,1)S(1)} %collective-permute-done.17.refs_6_), channel_id=1, source_target_pairs={{0,8},{8,0},{1,9},{9,1},{2,10},{10,2},{3,11},{11,3},{4,12},{12,4},... | collective-permute-start | bytes 921608 | tf_op jit(solution)/shard_map/ppermute | solution.py:45
  204.2 2.4 collective-permute-start.30
  207.2 3.5 %collective-permute-done.22.refs_11_ = bf16[240,640]{1,0:T(8,128)(2,1)S(1)} collective-permute-done((bf16[240,640]{1,0:T(8,128)(2,1)S(1)}, bf16[240,640]{1,0:T(8,128)(2,1)S(1)}, u32[]{:S(2)}, u32[]{:S(2)}) %collective-permute-start.22) | collective-permute-done | bytes 307232 | tf_op jit(solution)/shard_map/ppermute | solution.py:45
  211.1 1.2 collective-permute-done.23.refs_12_
  212.5 3.1 %project.6 = (bf16[64,1536]{1,0:T(8,128)(2,1)S(1)}, bf16[64,1536]{1,0:T(8,128)(2,1)S(1)}) custom-call(s32[4]{0:T(128)S(1)} %copy-done.7, bf16[128,640]{1,0:T(8,128)(2,1)S(1)} %get-tuple-element.74.refs_1_.refs_0_, bf16[128,640]{1,0:T(8,128)(2,1)S(1)} %collective-permute-done.43.refs_2_, bf16[128,640]{1,0:T(8,128)(2,1)S(1)} %collective-permute-done.44.refs_3_, ...), custom_call_target="tpu_custom_call" | custom-call | flops 2013265920 | bytes 7864320 | tf_op jit(solution)/shard_map/project/pallas_call | solution.py:414
  215.6 2.3 renorm.3.high_ref
  217.9 3.7 %apply_weights.2 = (bf16[128,640]{1,0:T(8,128)(2,1)S(1)}, bf16[128,640]{1,0:T(8,128)(2,1)S(1)}, bf16[128,640]{1,0:T(8,128)(2,1)S(1)}, bf16[128,640]{1,0:T(8,128)(2,1)S(1)}, bf16[256,640]{1,0:T(8,128)(2,1)S(1)}) custom-call(s32[4]{0:T(128)S(1)} %copy-done.7, bf16[3,640,640]{2,1,0:T(8,128)(2,1)S(1)} %renorm.3.high_ref, f32[1,640]{1,0:T(1,128)S(1)} %reshape.3.gain_ref, ...), custom_call_target="tpu_custom_call" | custom-call | flops 1258291200 | bytes 5242880 | tf_op jit(solution)/shard_map/apply_weights/pallas_call | solution.py:352
  221.6 1.6 collective-permute-start.24
  223.1 3.1 %collective-permute-start.25 = (bf16[128,640]{1,0:T(8,128)(2,1)S(1)}, bf16[128,640]{1,0:T(8,128)(2,1)S(1)}, u32[]{:S(2)}, u32[]{:S(2)}) collective-permute-start(bf16[128,640]{1,0:T(8,128)(2,1)S(1)} %get-tuple-element.63.refs_2_), channel_id=1, source_target_pairs={{0,4},{2,6},{4,0},{6,2},{1,5},{3,7},{5,1},{7,3},{8,12},{10,14},{12... | collective-permute-start | bytes 491528 | tf_op jit(solution)/shard_map/ppermute | solution.py:45
  227.1 3.1 %project.7 = (bf16[64,1536]{1,0:T(8,128)(2,1)S(1)}, bf16[64,1536]{1,0:T(8,128)(2,1)S(1)}) custom-call(s32[4]{0:T(128)S(1)} %copy-done.7, bf16[128,640]{1,0:T(8,128)(2,1)S(1)} %get-tuple-element.74.refs_1_.refs_0_, bf16[128,640]{1,0:T(8,128)(2,1)S(1)} %collective-permute-done.43.refs_2_, bf16[128,640]{1,0:T(8,128)(2,1)S(1)} %collective-permute-done.44.refs_3_, ...), custom_call_target="tpu_custom_call" | custom-call | flops 2013265920 | bytes 7864320 | tf_op jit(solution)/shard_map/project/pallas_call | solution.py:414
  230.9 3.2 %pair_project.3 = (bf16[64,2048]{1,0:T(8,128)(2,1)S(1)}, bf16[64,2048]{1,0:T(8,128)(2,1)S(1)}, bf16[64,2048]{1,0:T(8,128)(2,1)S(1)}, bf16[64,2048]{1,0:T(8,128)(2,1)S(1)}) custom-call(s32[4]{0:T(128)S(1)} %copy-done.7, bf16[128,640]{1,0:T(8,128)(2,1)S(1)} %get-tuple-element.74.refs_1_.refs_0_, bf16[128,640]{1,0:T(8,128)(2,1)S(1)} %get-tuple-element.77.refs_1_, ...), custom_call_target="tpu_custom_call" | custom-call | flops 1342177280 | bytes 5242880 | tf_op jit(solution)/shard_map/pair_project/pallas_call | solution.py:467
  235.8 2.4 collective-permute-start.50
  238.2 3.1 %project.5 = (bf16[64,1536]{1,0:T(8,128)(2,1)S(1)}, bf16[64,1536]{1,0:T(8,128)(2,1)S(1)}) custom-call(s32[4]{0:T(128)S(1)} %copy-done.7, bf16[128,640]{1,0:T(8,128)(2,1)S(1)} %get-tuple-element.61.refs_1_.refs_0_, bf16[128,640]{1,0:T(8,128)(2,1)S(1)} %collective-permute-done.24.refs_2_, bf16[128,640]{1,0:T(8,128)(2,1)S(1)} %collective-permute-done.25.refs_3_, ...), custom_call_target="tpu_custom_call" | custom-call | flops 2013265920 | bytes 7864320 | tf_op jit(solution)/shard_map/project/pallas_call | solution.py:414
  241.4 3.2 %pair_project.2 = (bf16[64,2048]{1,0:T(8,128)(2,1)S(1)}, bf16[64,2048]{1,0:T(8,128)(2,1)S(1)}, bf16[64,2048]{1,0:T(8,128)(2,1)S(1)}, bf16[64,2048]{1,0:T(8,128)(2,1)S(1)}) custom-call(s32[4]{0:T(128)S(1)} %copy-done.7, bf16[128,640]{1,0:T(8,128)(2,1)S(1)} %get-tuple-element.61.refs_1_.refs_0_, bf16[128,640]{1,0:T(8,128)(2,1)S(1)} %get-tuple-element.64.refs_1_, ...), custom_call_target="tpu_custom_call" | custom-call | flops 1342177280 | bytes 5242880 | tf_op jit(solution)/shard_map/pair_project/pallas_call | solution.py:467
  245.4 2.7 %collective-permute-start.40 = (bf16[64,2048]{1,0:T(8,128)(2,1)S(1)}, bf16[64,2048]{1,0:T(8,128)(2,1)S(1)}, u32[]{:S(2)}, u32[]{:S(2)}) collective-permute-start(bf16[64,2048]{1,0:T(8,128)(2,1)S(1)} %get-tuple-element.71), channel_id=1, source_target_pairs={{0,6},{2,0},{4,2},{6,4},{1,7},{3,1},{5,3},{7,5},{8,14},{10,8},{12,... | collective-permute-start | bytes 786440 | tf_op jit(solution)/shard_map/ppermute | solution.py:45
  248.8 3.1 %project.4 = (bf16[64,1536]{1,0:T(8,128)(2,1)S(1)}, bf16[64,1536]{1,0:T(8,128)(2,1)S(1)}) custom-call(s32[4]{0:T(128)S(1)} %copy-done.7, bf16[128,640]{1,0:T(8,128)(2,1)S(1)} %get-tuple-element.61.refs_1_.refs_0_, bf16[128,640]{1,0:T(8,128)(2,1)S(1)} %collective-permute-done.24.refs_2_, bf16[128,640]{1,0:T(8,128)(2,1)S(1)} %collective-permute-done.25.refs_3_, ...), custom_call_target="tpu_custom_call" | custom-call | flops 2013265920 | bytes 7864320 | tf_op jit(solution)/shard_map/project/pallas_call | solution.py:414
  252.7 1.6 finish.2.refs_7_
  254.9 7.0 %collective-permute-done.42.refs_6_ = bf16[64,2048]{1,0:T(8,128)(2,1)S(1)} collective-permute-done((bf16[64,2048]{1,0:T(8,128)(2,1)S(1)}, bf16[64,2048]{1,0:T(8,128)(2,1)S(1)}, u32[]{:S(2)}, u32[]{:S(2)}) %collective-permute-start.42) | collective-permute-done | bytes 262176 | tf_op jit(solution)/shard_map/ppermute | solution.py:45
  262.0 1.6 finish.3.held_ref
  263.5 1.3 finish_last.1
  (104 shorter events, 18.6 us)
Async XLA Ops:
  2.5 24.6 %all-to-all-start = ((bf16[8,128,640]{2,1,0:T(8,128)(2,1)}), bf16[8,128,640]{2,1,0:T(8,128)(2,1)S(1)}, u32[]{:S(2)}, u32[]{:S(2)}) async-start(bf16[8,128,640]{2,1,0:T(8,128)(2,1)} %pack_first.1), calls=%async_computation | async-start | bytes 2621440 | tf_op jit(solution)/shard_map/all_to_all | solution.py:49
  12.9 20.6 %copy-start = (f32[1,640,640]{2,1,0:T(8,128)S(1)}, f32[1,640,640]{2,1,0:T(8,128)}, u32[]{:S(2)}) copy-start(f32[1,640,640]{2,1,0:T(8,128)} %gate_ref.3) | copy-start | bytes 4915204
  27.1 4.4 %copy-start.10 = (bf16[8,128,640]{2,1,0:T(8,128)(2,1)}, bf16[8,128,640]{2,1,0:T(8,128)(2,1)S(1)}, u32[]{:S(2)}) copy-start(bf16[8,128,640]{2,1,0:T(8,128)(2,1)S(1)} %all-to-all-done.near_ref) | copy-start | bytes 3932164
  27.1 35.3 %all-to-all-start.1 = ((bf16[8,256,640]{2,1,0:T(8,128)(2,1)}), bf16[8,256,640]{2,1,0:T(8,128)(2,1)}, u32[]{:S(2)}, u32[]{:S(2)}) async-start(bf16[8,256,640]{2,1,0:T(8,128)(2,1)} %pack_second.1), calls=%async_computation.1 | async-start | bytes 5242880 | tf_op jit(solution)/shard_map/all_to_all | solution.py:49
  31.5 33.6 %collective-permute-start = (bf16[8,128,640]{2,1,0:T(8,128)(2,1)S(1)}, bf16[8,128,640]{2,1,0:T(8,128)(2,1)}, u32[]{:S(2)}, u32[]{:S(2)}) collective-permute-start(bf16[8,128,640]{2,1,0:T(8,128)(2,1)S(1)} %all-to-all-done.near_ref), channel_id=1, source_target_pairs={{0,8},{8,0},{1,9},{9,1},{2,10},{10,2},{3,11},{11,3},{4,12},{12,4},... | collective-permute-start | bytes 3932168 | tf_op jit(solution)/shard_map/ppermute | solution.py:45
  36.4 2.0 copy-start.6
  62.4 83.1 %collective-permute-start.12 = (bf16[8,256,640]{2,1,0:T(8,128)(2,1)}, bf16[8,256,640]{2,1,0:T(8,128)(2,1)}, u32[]{:S(2)}, u32[]{:S(2)}) collective-permute-start(bf16[8,256,640]{2,1,0:T(8,128)(2,1)} %all-to-all-done.1.near_ref.query_ref), channel_id=1, source_target_pairs={{0,8},{8,0},{1,9},{9,1},{2,10},{10,2},{3,11},{11,3},{4,12},{12,4},... | collective-permute-start | bytes 7864328 | tf_op jit(solution)/shard_map/ppermute | solution.py:45
  75.4 4.3 %copy-start.5 = (f32[240,640]{1,0:T(8,128)}, f32[240,640]{1,0:T(8,128)S(1)}, u32[]{:S(2)}) copy-start(f32[240,640]{1,0:T(8,128)S(1)} %get-tuple-element.51) | copy-start | bytes 1843204
  75.4 10.8 %collective-permute-start.3 = (bf16[240,640]{1,0:T(8,128)(2,1)}, bf16[240,640]{1,0:T(8,128)(2,1)}, u32[]{:S(2)}, u32[]{:S(2)}) collective-permute-start(bf16[240,640]{1,0:T(8,128)(2,1)} %get-tuple-element.54), channel_id=1, source_target_pairs={{0,64},{32,96},{64,0},{96,32},{1,65},{33,97},{65,1},{97,33},{2,66}... | collective-permute-start | bytes 921608 | tf_op jit(solution)/shard_map/ppermute | solution.py:45
  78.3 14.6 %collective-permute-start.2 = (bf16[240,640]{1,0:T(8,128)(2,1)}, bf16[240,640]{1,0:T(8,128)(2,1)}, u32[]{:S(2)}, u32[]{:S(2)}) collective-permute-start(bf16[240,640]{1,0:T(8,128)(2,1)} %get-tuple-element.53), channel_id=1, source_target_pairs={{0,96},{32,0},{64,32},{96,64},{1,97},{33,1},{65,33},{97,65},{2,98}... | collective-permute-start | bytes 921608 | tf_op jit(solution)/shard_map/ppermute | solution.py:45
  79.1 14.0 %collective-permute-start.1 = (bf16[240,640]{1,0:T(8,128)(2,1)S(1)}, bf16[240,640]{1,0:T(8,128)(2,1)}, u32[]{:S(2)}, u32[]{:S(2)}) collective-permute-start(bf16[240,640]{1,0:T(8,128)(2,1)S(1)} %get-tuple-element.52), channel_id=1, source_target_pairs={{0,32},{32,64},{64,96},{96,0},{1,33},{33,65},{65,97},{97,1},{2,34}... | collective-permute-start | bytes 921608 | tf_op jit(solution)/shard_map/ppermute | solution.py:45
  82.2 38.4 %collective-permute-start.38 = (bf16[640,1024]{1,0:T(8,128)(2,1)}, bf16[640,1024]{1,0:T(8,128)(2,1)S(1)}, u32[]{:S(2)}, u32[]{:S(2)}) collective-permute-start(bf16[640,1024]{1,0:T(8,128)(2,1)} %constant_dynamic-slice_fusion), channel_id=1, source_target_pairs={{0,1},{1,0},{2,3},{3,2},{4,5},{5,4},{6,7},{7,6},{8,9},{9,8},{10,11... | collective-permute-start | bytes 3932168 | tf_op jit(solution)/shard_map/ppermute | solution.py:45
  94.6 47.0 %copy-start.2 = (f32[1,640,640]{2,1,0:T(8,128)S(1)}, f32[1,640,640]{2,1,0:T(8,128)}, u32[]{:S(2)}) copy-start(f32[1,640,640]{2,1,0:T(8,128)} %up_ref.3) | copy-start | bytes 4915204
  94.6 47.0 %copy-start.4 = (f32[1,640,640]{2,1,0:T(8,128)S(1)}, f32[1,640,640]{2,1,0:T(8,128)}, u32[]{:S(2)}) copy-start(f32[1,640,640]{2,1,0:T(8,128)} %down_ref.3) | copy-start | bytes 4915204
  94.6 25.5 %collective-permute-start.4 = (bf16[240,640]{1,0:T(8,128)(2,1)S(1)}, bf16[240,640]{1,0:T(8,128)(2,1)S(1)}, u32[]{:S(2)}, u32[]{:S(2)}) collective-permute-start(bf16[240,640]{1,0:T(8,128)(2,1)S(1)} %convert_element_type.39), channel_id=1, source_target_pairs={{0,16},{16,0},{1,17},{17,1},{2,18},{18,2},{3,19},{19,3},{4,20},{20... | collective-permute-start | bytes 921608 | tf_op jit(solution)/shard_map/ppermute | solution.py:45
  99.0 55.5 %collective-permute-start.27 = (bf16[640,1536]{1,0:T(8,128)(2,1)S(1)}, bf16[640,1536]{1,0:T(8,128)(2,1)S(1)}, u32[]{:S(2)}, u32[]{:S(2)}) collective-permute-start(bf16[640,1536]{1,0:T(8,128)(2,1)S(1)} %constant_dynamic-slice_fusion.1), channel_id=1, source_target_pairs={{0,2},{2,4},{4,6},{6,0},{1,3},{3,5},{5,7},{7,1},{8,10},{10,12},{12... | collective-permute-start | bytes 5898248 | tf_op jit(solution)/shard_map/ppermute | solution.py:45
  99.1 57.6 %collective-permute-start.31 = (bf16[640,1536]{1,0:T(8,128)(2,1)S(1)}, bf16[640,1536]{1,0:T(8,128)(2,1)S(1)}, u32[]{:S(2)}, u32[]{:S(2)}) collective-permute-start(bf16[640,1536]{1,0:T(8,128)(2,1)S(1)} %constant_dynamic-slice_fusion.1), channel_id=1, source_target_pairs={{0,6},{2,0},{4,2},{6,4},{1,7},{3,1},{5,3},{7,5},{8,14},{10,8},{12,... | collective-permute-start | bytes 5898248 | tf_op jit(solution)/shard_map/ppermute | solution.py:45
  120.2 22.8 %copy-start.7 = (s32[4]{0:T(128)S(1)}, s32[4]{0:T(128)}, u32[]{:S(2)}) copy-start(s32[4]{0:T(128)} %copy-done.6) | copy-start | bytes 52
  120.2 8.4 %collective-permute-start.5 = (bf16[240,640]{1,0:T(8,128)(2,1)S(1)}, bf16[240,640]{1,0:T(8,128)(2,1)S(1)}, u32[]{:S(2)}, u32[]{:S(2)}) collective-permute-start(bf16[240,640]{1,0:T(8,128)(2,1)S(1)} %add_convert_fusion.1.refs_4_), channel_id=1, source_target_pairs={{0,32},{32,64},{64,96},{96,0},{1,33},{33,65},{65,97},{97,1},{2,34}... | collective-permute-start | bytes 921608 | tf_op jit(solution)/shard_map/ppermute | solution.py:45
  120.6 15.2 %collective-permute-start.6 = (bf16[240,640]{1,0:T(8,128)(2,1)S(1)}, bf16[240,640]{1,0:T(8,128)(2,1)S(1)}, u32[]{:S(2)}, u32[]{:S(2)}) collective-permute-start(bf16[240,640]{1,0:T(8,128)(2,1)S(1)} %add_convert_fusion.1.refs_4_), channel_id=1, source_target_pairs={{0,64},{32,96},{64,0},{96,32},{1,65},{33,97},{65,1},{97,33},{2,66}... | collective-permute-start | bytes 921608 | tf_op jit(solution)/shard_map/ppermute | solution.py:45
  128.6 9.7 %collective-permute-start.7 = (bf16[240,640]{1,0:T(8,128)(2,1)S(1)}, bf16[240,640]{1,0:T(8,128)(2,1)S(1)}, u32[]{:S(2)}, u32[]{:S(2)}) collective-permute-start(bf16[240,640]{1,0:T(8,128)(2,1)S(1)} %add_convert_fusion.1.refs_4_), channel_id=1, source_target_pairs={{0,96},{32,0},{64,32},{96,64},{1,97},{33,1},{65,33},{97,65},{2,98}... | collective-permute-start | bytes 921608 | tf_op jit(solution)/shard_map/ppermute | solution.py:45
  135.8 3.8 %collective-permute-start.8 = (bf16[240,640]{1,0:T(8,128)(2,1)S(1)}, bf16[240,640]{1,0:T(8,128)(2,1)S(1)}, u32[]{:S(2)}, u32[]{:S(2)}) collective-permute-start(bf16[240,640]{1,0:T(8,128)(2,1)S(1)} %add_convert_fusion.1.refs_4_), channel_id=1, source_target_pairs={{0,8},{8,0},{1,9},{9,1},{2,10},{10,2},{3,11},{11,3},{4,12},{12,4},... | collective-permute-start | bytes 921608 | tf_op jit(solution)/shard_map/ppermute | solution.py:45
  138.4 2.5 collective-permute-start.9
  139.6 1.7 collective-permute-start.10
  140.8 2.2 collective-permute-start.11
  141.3 31.4 %collective-permute-start.39 = (bf16[640,1024]{1,0:T(8,128)(2,1)S(1)}, bf16[640,1024]{1,0:T(8,128)(2,1)S(1)}, u32[]{:S(2)}, u32[]{:S(2)}) collective-permute-start(bf16[640,1024]{1,0:T(8,128)(2,1)S(1)} %collective-permute-done.38.refs_6_), channel_id=1, source_target_pairs={{0,8},{8,0},{1,9},{9,1},{2,10},{10,2},{3,11},{11,3},{4,12},{12,4},... | collective-permute-start | bytes 3932168 | tf_op jit(solution)/shard_map/ppermute | solution.py:45
  145.5 67.1 %slice-start = ((s8[6553600]{0:T(1024)(128)(4,1)}), s8[2359296]{0:T(1024)(128)(4,1)S(1)}, s32[]{:S(2)}) async-start(s8[6553600]{0:T(1024)(128)(4,1)} %bitcast.5), calls=%async_computation.2 | async-start | bytes 4718592
  153.5 59.1 %slice-start.1 = ((s8[6553600]{0:T(1024)(128)(4,1)}), s8[4194304]{0:T(1024)(128)(4,1)S(1)}, s32[]{:S(2)}) async-start(s8[6553600]{0:T(1024)(128)(4,1)} %bitcast.5), calls=%async_computation.3 | async-start | bytes 8388608
  153.5 10.3 %collective-permute-start.15 = (bf16[240,640]{1,0:T(8,128)(2,1)S(1)}, bf16[240,640]{1,0:T(8,128)(2,1)S(1)}, u32[]{:S(2)}, u32[]{:S(2)}) collective-permute-start(bf16[240,640]{1,0:T(8,128)(2,1)S(1)} %get-tuple-element.60), channel_id=1, source_target_pairs={{0,64},{32,96},{64,0},{96,32},{1,65},{33,97},{65,1},{97,33},{2,66}... | collective-permute-start | bytes 921608 | tf_op jit(solution)/shard_map/ppermute | solution.py:45
  154.6 24.2 %collective-permute-start.29 = (bf16[320,1536]{1,0:T(8,128)(2,1)S(1)}, bf16[320,1536]{1,0:T(8,128)(2,1)S(1)}, u32[]{:S(2)}, u32[]{:S(2)}) collective-permute-start(bf16[320,1536]{1,0:T(8,128)(2,1)S(1)} %slice.8), channel_id=1, source_target_pairs={{0,2},{2,4},{4,6},{6,0},{1,3},{3,5},{5,7},{7,1},{8,10},{10,12},{12... | collective-permute-start | bytes 2949128 | tf_op jit(solution)/shard_map/ppermute | solution.py:45
  154.9 15.8 %collective-permute-start.14 = (bf16[240,640]{1,0:T(8,128)(2,1)S(1)}, bf16[240,640]{1,0:T(8,128)(2,1)S(1)}, u32[]{:S(2)}, u32[]{:S(2)}) collective-permute-start(bf16[240,640]{1,0:T(8,128)(2,1)S(1)} %get-tuple-element.59), channel_id=1, source_target_pairs={{0,96},{32,0},{64,32},{96,64},{1,97},{33,1},{65,33},{97,65},{2,98}... | collective-permute-start | bytes 921608 | tf_op jit(solution)/shard_map/ppermute | solution.py:45
  156.7 14.1 %collective-permute-start.13 = (bf16[240,640]{1,0:T(8,128)(2,1)S(1)}, bf16[240,640]{1,0:T(8,128)(2,1)S(1)}, u32[]{:S(2)}, u32[]{:S(2)}) collective-permute-start(bf16[240,640]{1,0:T(8,128)(2,1)S(1)} %get-tuple-element.58), channel_id=1, source_target_pairs={{0,32},{32,64},{64,96},{96,0},{1,33},{33,65},{65,97},{97,1},{2,34}... | collective-permute-start | bytes 921608 | tf_op jit(solution)/shard_map/ppermute | solution.py:45
  157.3 14.1 %copy-start.11 = (f32[640]{0:T(1024)S(1)}, f32[640]{0:T(1024)}, u32[]{:S(2)}) copy-start(f32[640]{0:T(1024)} %param.16) | copy-start | bytes 7684
  163.8 21.7 %collective-permute-start.32 = (bf16[320,1536]{1,0:T(8,128)(2,1)S(1)}, bf16[320,1536]{1,0:T(8,128)(2,1)S(1)}, u32[]{:S(2)}, u32[]{:S(2)}) collective-permute-start(bf16[320,1536]{1,0:T(8,128)(2,1)S(1)} %slice.9), channel_id=1, source_target_pairs={{0,6},{2,0},{4,2},{6,4},{1,7},{3,1},{5,3},{7,5},{8,14},{10,8},{12,... | collective-permute-start | bytes 2949128 | tf_op jit(solution)/shard_map/ppermute | solution.py:45
  171.1 9.6 %collective-permute-start.16 = (bf16[240,640]{1,0:T(8,128)(2,1)S(1)}, bf16[240,640]{1,0:T(8,128)(2,1)S(1)}, u32[]{:S(2)}, u32[]{:S(2)}) collective-permute-start(bf16[240,640]{1,0:T(8,128)(2,1)S(1)} %convert_element_type.45), channel_id=1, source_target_pairs={{0,16},{16,0},{1,17},{17,1},{2,18},{18,2},{3,19},{19,3},{4,20},{20... | collective-permute-start | bytes 921608 | tf_op jit(solution)/shard_map/ppermute | solution.py:45
  171.5 50.1 %collective-permute-start.28 = (bf16[640,1536]{1,0:T(8,128)(2,1)S(1)}, bf16[640,1536]{1,0:T(8,128)(2,1)S(1)}, u32[]{:S(2)}, u32[]{:S(2)}) collective-permute-start(bf16[640,1536]{1,0:T(8,128)(2,1)S(1)} %collective-permute-done.27.refs_6_), channel_id=1, source_target_pairs={{0,8},{8,0},{1,9},{9,1},{2,10},{10,2},{3,11},{11,3},{4,12},{12,4},... | collective-permute-start | bytes 5898248 | tf_op jit(solution)/shard_map/ppermute | solution.py:45
  172.6 53.6 %collective-permute-start.34 = (bf16[640,1536]{1,0:T(8,128)(2,1)S(1)}, bf16[640,1536]{1,0:T(8,128)(2,1)S(1)}, u32[]{:S(2)}, u32[]{:S(2)}) collective-permute-start(bf16[640,1536]{1,0:T(8,128)(2,1)S(1)} %collective-permute-done.31.refs_9_), channel_id=1, source_target_pairs={{0,8},{8,0},{1,9},{9,1},{2,10},{10,2},{3,11},{11,3},{4,12},{12,4},... | collective-permute-start | bytes 5898248 | tf_op jit(solution)/shard_map/ppermute | solution.py:45
  178.7 8.0 %collective-permute-start.43 = (bf16[128,640]{1,0:T(8,128)(2,1)S(1)}, bf16[128,640]{1,0:T(8,128)(2,1)S(1)}, u32[]{:S(2)}, u32[]{:S(2)}) collective-permute-start(bf16[128,640]{1,0:T(8,128)(2,1)S(1)} %get-tuple-element.75.refs_3_), channel_id=1, source_target_pairs={{0,2},{2,4},{4,6},{6,0},{1,3},{3,5},{5,7},{7,1},{8,10},{10,12},{12... | collective-permute-start | bytes 491528 | tf_op jit(solution)/shard_map/ppermute | solution.py:45
  180.6 9.6 %collective-permute-start.44 = (bf16[128,640]{1,0:T(8,128)(2,1)S(1)}, bf16[128,640]{1,0:T(8,128)(2,1)S(1)}, u32[]{:S(2)}, u32[]{:S(2)}) collective-permute-start(bf16[128,640]{1,0:T(8,128)(2,1)S(1)} %get-tuple-element.76.refs_2_), channel_id=1, source_target_pairs={{0,4},{2,6},{4,0},{6,2},{1,5},{3,7},{5,1},{7,3},{8,12},{10,14},{12... | collective-permute-start | bytes 491528 | tf_op jit(solution)/shard_map/ppermute | solution.py:45
  185.5 12.3 %collective-permute-start.17 = (bf16[240,640]{1,0:T(8,128)(2,1)S(1)}, bf16[240,640]{1,0:T(8,128)(2,1)S(1)}, u32[]{:S(2)}, u32[]{:S(2)}) collective-permute-start(bf16[240,640]{1,0:T(8,128)(2,1)S(1)} %add_convert_fusion.refs_5_), channel_id=1, source_target_pairs={{0,32},{32,64},{64,96},{96,0},{1,33},{33,65},{65,97},{97,1},{2,34}... | collective-permute-start | bytes 921608 | tf_op jit(solution)/shard_map/ppermute | solution.py:45
  186.7 14.2 %collective-permute-start.18 = (bf16[240,640]{1,0:T(8,128)(2,1)S(1)}, bf16[240,640]{1,0:T(8,128)(2,1)S(1)}, u32[]{:S(2)}, u32[]{:S(2)}) collective-permute-start(bf16[240,640]{1,0:T(8,128)(2,1)S(1)} %add_convert_fusion.refs_5_), channel_id=1, source_target_pairs={{0,64},{32,96},{64,0},{96,32},{1,65},{33,97},{65,1},{97,33},{2,66}... | collective-permute-start | bytes 921608 | tf_op jit(solution)/shard_map/ppermute | solution.py:45
  190.2 4.5 %collective-permute-start.45 = (bf16[128,640]{1,0:T(8,128)(2,1)S(1)}, bf16[128,640]{1,0:T(8,128)(2,1)S(1)}, u32[]{:S(2)}, u32[]{:S(2)}) collective-permute-start(bf16[128,640]{1,0:T(8,128)(2,1)S(1)} %get-tuple-element.77.refs_1_), channel_id=1, source_target_pairs={{0,6},{2,0},{4,2},{6,4},{1,7},{3,1},{5,3},{7,5},{8,14},{10,8},{12,... | collective-permute-start | bytes 491528 | tf_op jit(solution)/shard_map/ppermute | solution.py:45
  194.7 9.6 %collective-permute-start.19 = (bf16[240,640]{1,0:T(8,128)(2,1)S(1)}, bf16[240,640]{1,0:T(8,128)(2,1)S(1)}, u32[]{:S(2)}, u32[]{:S(2)}) collective-permute-start(bf16[240,640]{1,0:T(8,128)(2,1)S(1)} %add_convert_fusion.refs_5_), channel_id=1, source_target_pairs={{0,96},{32,0},{64,32},{96,64},{1,97},{33,1},{65,33},{97,65},{2,98}... | collective-permute-start | bytes 921608 | tf_op jit(solution)/shard_map/ppermute | solution.py:45
  197.8 8.9 %collective-permute-start.20 = (bf16[240,640]{1,0:T(8,128)(2,1)S(1)}, bf16[240,640]{1,0:T(8,128)(2,1)S(1)}, u32[]{:S(2)}, u32[]{:S(2)}) collective-permute-start(bf16[240,640]{1,0:T(8,128)(2,1)S(1)} %add_convert_fusion.refs_5_), channel_id=1, source_target_pairs={{0,8},{8,0},{1,9},{9,1},{2,10},{10,2},{3,11},{11,3},{4,12},{12,4},... | collective-permute-start | bytes 921608 | tf_op jit(solution)/shard_map/ppermute | solution.py:45
  200.9 5.7 %collective-permute-start.21 = (bf16[240,640]{1,0:T(8,128)(2,1)S(1)}, bf16[240,640]{1,0:T(8,128)(2,1)S(1)}, u32[]{:S(2)}, u32[]{:S(2)}) collective-permute-start(bf16[240,640]{1,0:T(8,128)(2,1)S(1)} %collective-permute-done.17.refs_6_), channel_id=1, source_target_pairs={{0,8},{8,0},{1,9},{9,1},{2,10},{10,2},{3,11},{11,3},{4,12},{12,4},... | collective-permute-start | bytes 921608 | tf_op jit(solution)/shard_map/ppermute | solution.py:45
  204.2 18.9 %collective-permute-start.30 = (bf16[320,1536]{1,0:T(8,128)(2,1)S(1)}, bf16[320,1536]{1,0:T(8,128)(2,1)S(1)}, u32[]{:S(2)}, u32[]{:S(2)}) collective-permute-start(bf16[320,1536]{1,0:T(8,128)(2,1)S(1)} %collective-permute-done.29.refs_7_), channel_id=1, source_target_pairs={{0,8},{8,0},{1,9},{9,1},{2,10},{10,2},{3,11},{11,3},{4,12},{12,4},... | collective-permute-start | bytes 2949128 | tf_op jit(solution)/shard_map/ppermute | solution.py:45
  206.7 19.6 %collective-permute-start.33 = (bf16[320,1536]{1,0:T(8,128)(2,1)S(1)}, bf16[320,1536]{1,0:T(8,128)(2,1)S(1)}, u32[]{:S(2)}, u32[]{:S(2)}) collective-permute-start(bf16[320,1536]{1,0:T(8,128)(2,1)S(1)} %collective-permute-done.32.refs_8_), channel_id=1, source_target_pairs={{0,8},{8,0},{1,9},{9,1},{2,10},{10,2},{3,11},{11,3},{4,12},{12,4},... | collective-permute-start | bytes 2949128 | tf_op jit(solution)/shard_map/ppermute | solution.py:45
  206.7 4.0 %collective-permute-start.22 = (bf16[240,640]{1,0:T(8,128)(2,1)S(1)}, bf16[240,640]{1,0:T(8,128)(2,1)S(1)}, u32[]{:S(2)}, u32[]{:S(2)}) collective-permute-start(bf16[240,640]{1,0:T(8,128)(2,1)S(1)} %collective-permute-done.18.refs_7_), channel_id=1, source_target_pairs={{0,8},{8,0},{1,9},{9,1},{2,10},{10,2},{3,11},{11,3},{4,12},{12,4},... | collective-permute-start | bytes 921608 | tf_op jit(solution)/shard_map/ppermute | solution.py:45
  210.7 1.6 collective-permute-start.23
  212.3 17.9 %collective-permute-start.48 = (bf16[256,640]{1,0:T(8,128)(2,1)S(1)}, bf16[256,640]{1,0:T(8,128)(2,1)S(1)}, u32[]{:S(2)}, u32[]{:S(2)}) collective-permute-start(bf16[256,640]{1,0:T(8,128)(2,1)S(1)} %get-tuple-element.82), channel_id=1, source_target_pairs={{0,1},{1,0},{2,3},{3,2},{4,5},{5,4},{6,7},{7,6},{8,9},{9,8},{10,11... | collective-permute-start | bytes 983048 | tf_op jit(solution)/shard_map/ppermute | solution.py:45
  221.6 12.6 %collective-permute-start.24 = (bf16[128,640]{1,0:T(8,128)(2,1)S(1)}, bf16[128,640]{1,0:T(8,128)(2,1)S(1)}, u32[]{:S(2)}, u32[]{:S(2)}) collective-permute-start(bf16[128,640]{1,0:T(8,128)(2,1)S(1)} %get-tuple-element.62.refs_3_), channel_id=1, source_target_pairs={{0,2},{2,4},{4,6},{6,0},{1,3},{3,5},{5,7},{7,1},{8,10},{10,12},{12... | collective-permute-start | bytes 491528 | tf_op jit(solution)/shard_map/ppermute | solution.py:45
  223.1 11.9 %collective-permute-start.25 = (bf16[128,640]{1,0:T(8,128)(2,1)S(1)}, bf16[128,640]{1,0:T(8,128)(2,1)S(1)}, u32[]{:S(2)}, u32[]{:S(2)}) collective-permute-start(bf16[128,640]{1,0:T(8,128)(2,1)S(1)} %get-tuple-element.63.refs_2_), channel_id=1, source_target_pairs={{0,4},{2,6},{4,0},{6,2},{1,5},{3,7},{5,1},{7,3},{8,12},{10,14},{12... | collective-permute-start | bytes 491528 | tf_op jit(solution)/shard_map/ppermute | solution.py:45
  226.2 9.6 %collective-permute-start.26 = (bf16[128,640]{1,0:T(8,128)(2,1)S(1)}, bf16[128,640]{1,0:T(8,128)(2,1)S(1)}, u32[]{:S(2)}, u32[]{:S(2)}) collective-permute-start(bf16[128,640]{1,0:T(8,128)(2,1)S(1)} %get-tuple-element.64.refs_1_), channel_id=1, source_target_pairs={{0,6},{2,0},{4,2},{6,4},{1,7},{3,1},{5,3},{7,5},{8,14},{10,8},{12,... | collective-permute-start | bytes 491528 | tf_op jit(solution)/shard_map/ppermute | solution.py:45
  226.2 15.1 %collective-permute-start.37 = (bf16[256,640]{1,0:T(8,128)(2,1)S(1)}, bf16[256,640]{1,0:T(8,128)(2,1)S(1)}, u32[]{:S(2)}, u32[]{:S(2)}) collective-permute-start(bf16[256,640]{1,0:T(8,128)(2,1)S(1)} %get-tuple-element.69), channel_id=1, source_target_pairs={{0,1},{1,0},{2,3},{3,2},{4,5},{5,4},{6,7},{7,6},{8,9},{9,8},{10,11... | collective-permute-start | bytes 983048 | tf_op jit(solution)/shard_map/ppermute | solution.py:45
  230.2 14.5 %collective-permute-start.46 = (bf16[64,1536]{1,0:T(8,128)(2,1)S(1)}, bf16[64,1536]{1,0:T(8,128)(2,1)S(1)}, u32[]{:S(2)}, u32[]{:S(2)}) collective-permute-start(bf16[64,1536]{1,0:T(8,128)(2,1)S(1)} %get-tuple-element.79), channel_id=1, source_target_pairs={{0,1},{1,0},{2,3},{3,2},{4,5},{5,4},{6,7},{7,6},{8,9},{9,8},{10,11... | collective-permute-start | bytes 589832 | tf_op jit(solution)/shard_map/ppermute | solution.py:45
  234.2 11.2 %collective-permute-start.47 = (bf16[64,1536]{1,0:T(8,128)(2,1)S(1)}, bf16[64,1536]{1,0:T(8,128)(2,1)S(1)}, u32[]{:S(2)}, u32[]{:S(2)}) collective-permute-start(bf16[64,1536]{1,0:T(8,128)(2,1)S(1)} %get-tuple-element.81), channel_id=1, source_target_pairs={{0,1},{1,0},{2,3},{3,2},{4,5},{5,4},{6,7},{7,6},{8,9},{9,8},{10,11... | collective-permute-start | bytes 589832 | tf_op jit(solution)/shard_map/ppermute | solution.py:45
  235.1 13.0 %collective-permute-start.49 = (bf16[64,2048]{1,0:T(8,128)(2,1)S(1)}, bf16[64,2048]{1,0:T(8,128)(2,1)S(1)}, u32[]{:S(2)}, u32[]{:S(2)}) collective-permute-start(bf16[64,2048]{1,0:T(8,128)(2,1)S(1)} %get-tuple-element.84), channel_id=1, source_target_pairs={{0,6},{2,0},{4,2},{6,4},{1,7},{3,1},{5,3},{7,5},{8,14},{10,8},{12,... | collective-permute-start | bytes 786440 | tf_op jit(solution)/shard_map/ppermute | solution.py:45
  235.8 12.3 %collective-permute-start.50 = (bf16[64,2048]{1,0:T(8,128)(2,1)S(1)}, bf16[64,2048]{1,0:T(8,128)(2,1)S(1)}, u32[]{:S(2)}, u32[]{:S(2)}) collective-permute-start(bf16[64,2048]{1,0:T(8,128)(2,1)S(1)} %get-tuple-element.85), channel_id=1, source_target_pairs={{0,4},{2,6},{4,0},{6,2},{1,5},{3,7},{5,1},{7,3},{8,12},{10,14},{12... | collective-permute-start | bytes 786440 | tf_op jit(solution)/shard_map/ppermute | solution.py:45
  241.3 10.5 %collective-permute-start.51 = (bf16[64,2048]{1,0:T(8,128)(2,1)S(1)}, bf16[64,2048]{1,0:T(8,128)(2,1)S(1)}, u32[]{:S(2)}, u32[]{:S(2)}) collective-permute-start(bf16[64,2048]{1,0:T(8,128)(2,1)S(1)} %get-tuple-element.86), channel_id=1, source_target_pairs={{0,2},{2,4},{4,6},{6,0},{1,3},{3,5},{5,7},{7,1},{8,10},{10,12},{12... | collective-permute-start | bytes 786440 | tf_op jit(solution)/shard_map/ppermute | solution.py:45
  244.7 9.6 %collective-permute-start.36 = (bf16[64,1536]{1,0:T(8,128)(2,1)S(1)}, bf16[64,1536]{1,0:T(8,128)(2,1)S(1)}, u32[]{:S(2)}, u32[]{:S(2)}) collective-permute-start(bf16[64,1536]{1,0:T(8,128)(2,1)S(1)} %get-tuple-element.68), channel_id=1, source_target_pairs={{0,1},{1,0},{2,3},{3,2},{4,5},{5,4},{6,7},{7,6},{8,9},{9,8},{10,11... | collective-permute-start | bytes 589832 | tf_op jit(solution)/shard_map/ppermute | solution.py:45
  245.4 8.9 %collective-permute-start.40 = (bf16[64,2048]{1,0:T(8,128)(2,1)S(1)}, bf16[64,2048]{1,0:T(8,128)(2,1)S(1)}, u32[]{:S(2)}, u32[]{:S(2)}) collective-permute-start(bf16[64,2048]{1,0:T(8,128)(2,1)S(1)} %get-tuple-element.71), channel_id=1, source_target_pairs={{0,6},{2,0},{4,2},{6,4},{1,7},{3,1},{5,3},{7,5},{8,14},{10,8},{12,... | collective-permute-start | bytes 786440 | tf_op jit(solution)/shard_map/ppermute | solution.py:45
  248.1 6.8 %collective-permute-start.41 = (bf16[64,2048]{1,0:T(8,128)(2,1)S(1)}, bf16[64,2048]{1,0:T(8,128)(2,1)S(1)}, u32[]{:S(2)}, u32[]{:S(2)}) collective-permute-start(bf16[64,2048]{1,0:T(8,128)(2,1)S(1)} %get-tuple-element.72), channel_id=1, source_target_pairs={{0,4},{2,6},{4,0},{6,2},{1,5},{3,7},{5,1},{7,3},{8,12},{10,14},{12... | collective-permute-start | bytes 786440 | tf_op jit(solution)/shard_map/ppermute | solution.py:45
  248.1 13.9 %collective-permute-start.42 = (bf16[64,2048]{1,0:T(8,128)(2,1)S(1)}, bf16[64,2048]{1,0:T(8,128)(2,1)S(1)}, u32[]{:S(2)}, u32[]{:S(2)}) collective-permute-start(bf16[64,2048]{1,0:T(8,128)(2,1)S(1)} %get-tuple-element.73), channel_id=1, source_target_pairs={{0,2},{2,4},{4,6},{6,0},{1,3},{3,5},{5,7},{7,1},{8,10},{10,12},{12... | collective-permute-start | bytes 786440 | tf_op jit(solution)/shard_map/ppermute | solution.py:45
  251.8 11.7 %collective-permute-start.35 = (bf16[64,1536]{1,0:T(8,128)(2,1)S(1)}, bf16[64,1536]{1,0:T(8,128)(2,1)S(1)}, u32[]{:S(2)}, u32[]{:S(2)}) collective-permute-start(bf16[64,1536]{1,0:T(8,128)(2,1)S(1)} %get-tuple-element.66), channel_id=1, source_target_pairs={{0,1},{1,0},{2,3},{3,2},{4,5},{5,4},{6,7},{7,6},{8,9},{9,8},{10,11... | collective-permute-start | bytes 589832 | tf_op jit(solution)/shard_map/ppermute | solution.py:45
  (4 other events, 5.0 us)
